TPU v7x, 32 devices: a whole 2x2x4 slice. The times are simulated.
32 devices in a mesh: gz: 4 (over z), gx: 2 (over x), gy: 4 (over y, core).
Axes of the slice: x: 2, y: 2, z: 4, core: 2. Of those that a mesh axis runs over, the one named last changes fastest.
Arguments:
- density: float32 [128, 256, 512], P('gx', 'gy', 'gz'), may hold values from 0.01 to 1
- design_mask: int32 [128, 256, 512], P('gx', 'gy', 'gz'), may hold values from 0 to 2
- energy: bfloat16 [4, 128, 256, 512], P(None, 'gx', 'gy', 'gz'), may hold values from 0.099609375 to 3
- decay: float32 [4, 512], P(None, 'gz'), may hold values from 0.3 to 1
- case_index: int32 [4], replicated, may hold values from 0 to 15
- case_weight: float32 [16], replicated, may hold values from 0.2 to 1
Outputs:
- sensitivity: float32 [128, 256, 512], P('gx', 'gy', 'gz')
- compliance: float32 [4], replicated
All inputs are finite; a program needn't handle non-finite values.
Results may differ from a plain program's by a relative error of at most 0.0006.
Values may be sent and summed in bfloat16 or wider, within the bound.
No kernel may reach another device: no remote copies, remote signals or barrier semaphores. Data moves between devices by JAX's collectives and lax.ppermute only.
A program may use at most 128 MiB of HBM per device.

v0:
```python
import jax
import jax.numpy as jnp
from jax import lax
from jax.sharding import PartitionSpec as P

LOADS = 16
RADIUS = 3


def entering_2(value, axis, join, neutral, backward):
    count, mine = (lax.axis_size(axis), lax.axis_index(axis))
    pieces = jax.tree.map(lambda part: lax.all_gather(part, axis), value)
    if backward:
        pieces = jax.tree.map(lambda part: part[::-1], pieces)
        mine = count - 1 - mine
    total = jax.tree.map(
        lambda part, zero: jnp.full_like(part, 0) + jnp.asarray(zero, part.dtype), value, neutral
    )

    def step(position, total):
        longer = join(total, jax.tree.map(lambda part: part[position], pieces))
        return jax.tree.map(lambda new, old: jnp.where(position < mine, new, old), longer, total)

    return lax.fori_loop(0, count - 1, step, total)


def with_halo(shard, sides, width):
    for axis, dim in sides:
        devices, length = (lax.axis_size(axis), shard.shape[dim])
        up = [(i, (i + 1) % devices) for i in range(devices - 1)]
        down = [(j, i) for i, j in up]
        last = lax.slice_in_dim(shard, length - width, length, axis=dim)
        initial = lax.slice_in_dim(shard, 0, width, axis=dim)
        before = lax.ppermute(last, axis, up)
        after = lax.ppermute(initial, axis, down)
        shard = jnp.concatenate([before, shard, after], axis=dim)
    return shard


def kernel_taps():
    offsets = jnp.arange(-RADIUS, RADIUS + 1).astype(jnp.float32)
    raw_taps = jnp.exp(-2.0 * offsets * offsets / (RADIUS * RADIUS))
    return raw_taps / jnp.sum(raw_taps)


def planar_filter(padded):
    width_x = padded.shape[1] - 2 * RADIUS
    width_y = padded.shape[2] - 2 * RADIUS
    taps = kernel_taps()
    along_x = taps[0] * padded[:, 0:width_x]
    for offset in range(1, 2 * RADIUS + 1):
        along_x = along_x + taps[offset] * padded[:, offset : offset + width_x]
    along_y = taps[0] * along_x[:, :, 0:width_y]
    for offset in range(1, 2 * RADIUS + 1):
        along_y = along_y + taps[offset] * along_x[:, :, offset : offset + width_y]
    return along_y


def solid_density(density, design_mask):
    return jnp.where(design_mask == 1, 0.001, jnp.where(design_mask == 2, 1.0, density))


def chain_maps(earlier, later):
    return (earlier[0] * later[0], later[0] * earlier[1] + later[1])


def slab_smooth(field, decay):
    depth = decay.shape[1]
    logs = jnp.log(decay)
    row_index = jnp.arange(depth)[:, None]
    col_index = jnp.arange(depth)[None, :]
    below_mask = (row_index >= col_index)[None]
    above_mask = (row_index <= col_index)[None]
    keep_in = (1.0 - decay)[:, None, :]
    upward = jnp.cumsum(logs, axis=1)
    spread = upward[:, :, None] - upward[:, None, :]
    forward_map = jnp.where(below_mask, jnp.exp(jnp.where(below_mask, spread, 0.0)), 0.0) * keep_in
    local_forward = jnp.einsum(
        "cxyj,cij->cxyi", field, forward_map, precision=lax.Precision.HIGHEST
    )
    leading = jnp.exp(upward)
    ones_part = jnp.ones((field.shape[0], 1, 1), jnp.float32)
    zero_part = jnp.zeros(field.shape[:3], jnp.float32)
    _, entering = entering_2(
        (leading[:, -1][:, None, None], local_forward[..., -1]),
        "gz",
        chain_maps,
        (ones_part, zero_part),
        False,
    )
    forward = local_forward + leading[:, None, None, :] * entering[..., None]
    remain = jnp.cumsum(logs[:, ::-1], axis=1)[:, ::-1]
    spread_back = remain[:, :, None] - remain[:, None, :]
    backward_map = (
        jnp.where(above_mask, jnp.exp(jnp.where(above_mask, spread_back, 0.0)), 0.0) * keep_in
    )
    local_backward = jnp.einsum(
        "cxyj,cij->cxyi", forward, backward_map, precision=lax.Precision.HIGHEST
    )
    trailing = jnp.exp(remain)
    _, from_above = entering_2(
        (trailing[:, 0][:, None, None], local_backward[..., 0]),
        "gz",
        chain_maps,
        (ones_part, zero_part),
        True,
    )
    return local_backward + trailing[:, None, None, :] * from_above[..., None]


def shards(density, design_mask, energy, decay, case_index, case_weight):
    dense = solid_density(density, design_mask)
    energy_wide = energy.astype(jnp.float32)
    source = -3.0 * (dense**3)[None] * energy_wide
    along_z = slab_smooth(source, decay)
    padded = with_halo(along_z.astype(jnp.bfloat16), (("gx", 1), ("gy", 2)), RADIUS).astype(
        along_z.dtype
    )
    smooth = planar_filter(padded)
    filtered = smooth / jnp.maximum(dense, 0.1)[None]
    selector = (case_index[:, None] == jnp.arange(LOADS)[None, :]).astype(jnp.float32)
    weights = jnp.sum(selector * case_weight[None, :], axis=1)
    combined = jnp.sum(weights[:, None, None, None] * filtered, axis=0)
    sensitivity = jnp.where(design_mask == 0, combined, 0.0).astype(jnp.float32)
    partial_sums = jnp.sum((dense**3)[None] * energy_wide, axis=(1, 2, 3))
    totals = lax.psum(partial_sums, ("gz", "gx", "gy"))
    all_cells = (
        density.shape[0]
        * density.shape[1]
        * density.shape[2]
        * lax.axis_size("gz")
        * lax.axis_size("gx")
        * lax.axis_size("gy")
    )
    return (sensitivity, totals / all_cells)


def solution(mesh):
    placed = (
        P("gx", "gy", "gz"),
        P("gx", "gy", "gz"),
        P(None, "gx", "gy", "gz"),
        P(None, "gz"),
        P(),
        P(),
    )
    return jax.shard_map(
        shards, mesh=mesh, in_specs=placed, out_specs=(P("gx", "gy", "gz"), P()), check_vma=False
    )
```

profile of v0, /device:TPU:1, one launch (start us, length us, event | category | flops | bytes accessed | tf_op | source)
XLA Modules:
  0.0 231.6 jit_solution(8170152929128144087)
XLA Ops:
  0.7 0.7 fusion.53
  1.4 0.1 rev.12
  1.5 0.3 reduce_window_sum.17
  1.8 0.3 reduce_window_sum.18
  2.1 0.1 rev.13
  2.2 0.1 slice_reduce_fusion
  2.3 0.2 slice_reduce_fusion.1
  2.5 1.2 dynamic-slice
  4.4 0.2 dynamic-update-slice.1
  4.7 0.2 dynamic-update-slice
  4.9 10.7 %all-reduce.2 = (f32[16]{0:T(128)S(1)}, f32[16]{0:T(128)S(1)}) all-reduce(f32[16]{0:T(128)S(1)} %dynamic-update-slice, f32[16]{0:T(128)S(1)} %dynamic-update-slice.1), channel_id=2, replica_groups=mesh['gz'=4,'gx'=2,'gy'=4] {'gz'}, use_global_device_ids=true, to_apply=%add | all-reduce | flops 32 | bytes 256
  15.6 0.1 reshape.48
  15.7 0.1 reshape.50
  15.8 4.5 %broadcast_multiply_fusion = (f32[64,64,128]{2,1,0:T(8,128)S(1)}, f32[64,64,128]{2,1,0:T(8,128)}, f32[64,64,128]{2,1,0:T(8,128)S(1)}) fusion(f32[64,64,128]{2,1,0:T(8,128)} %param.10, s32[64,64,128]{2,1,0:T(8,128)} %param.11), kind=kLoop, calls=%fused_computation.51 | loop fusion | flops 4194304 | bytes 10485760 | tf_op jit(solution)/shard_map/mul | solution.py:114
  20.3 0.0 copy-done.2
  20.3 8.6 %fusion.8 = f32[4,64,64,128]{3,2,1,0:T(8,128)S(1)} fusion(bf16[4,64,64,128]{3,2,1,0:T(8,128)(2,1)S(1)} %copy-done.2, f32[64,64,128]{2,1,0:T(8,128)S(1)} %get-tuple-element.290, f32[4,128]{1,0:T(4,128)S(1)} %get-tuple-element.298, f32[4,128]{1,0:T(4,128)S(1)} %reduce_window_sum.17, pred[128,128]{1,0:T(8,128)(4,1)S(1)} %iota_compare_fusion.1), kind=kOutput, calls=%fused_computation.21 | convolution fusion | flops 3225681920 | bytes 14700544 | tf_op jit(solution)/shard_map/cxyj,cij->cxyi/dot_general | solution.py:78
  28.9 0.0 copy-start
  28.9 3.2 %copy-done = f32[4,64,64,128]{3,2,1,0:T(8,128)} copy-done((f32[4,64,64,128]{3,2,1,0:T(8,128)}, f32[4,64,64,128]{3,2,1,0:T(8,128)S(1)}, u32[]{:S(2)}) %copy-start) | copy-done | bytes 8388632
  32.1 5.4 %slice.123 = f32[4,64,64,1]{3,2,1,0:T(8,128)} slice(f32[4,64,64,128]{3,2,1,0:T(8,128)S(1)} %fusion.8), slice={[0:4], [0:64], [0:64], [127:128]} | slice | bytes 131072 | tf_op jit(solution)/shard_map/slice | solution.py:85
  37.6 5.4 %copy.16 = f32[4,64,64,1]{2,1,3,0:T(8,128)S(1)} copy(f32[4,64,64,1]{3,2,1,0:T(8,128)} %slice.123) | data formatting | bytes 131072 | tf_op jit(solution)/shard_map/slice | solution.py:85
  43.0 12.8 %all-gather.1 = f32[16,64,64,1]{2,1,3,0:T(8,128)S(1)} all-gather(f32[4,64,64,1]{2,1,3,0:T(8,128)S(1)} %copy.16), channel_id=3, replica_groups=mesh['gz'=4,'gx'=2,'gy'=4] {'gz'}, dimensions={0}, use_global_device_ids=true | all-gather | bytes 327680 | tf_op jit(solution)/shard_map/all_gather | solution.py:12
  55.8 0.4 while.28
  55.8 0.1 fusion.57
  55.9 0.1 fusion.57
  56.0 0.1 fusion.57
  56.1 11.1 %fusion.18 = f32[4,64,64,128]{3,2,1,0:T(8,128)} fusion(f32[4,64,64,128]{3,2,1,0:T(8,128)} %copy-done, f32[4,64,64]{2,1,0:T(8,128)S(1)} %get-tuple-element.190, f32[4,128]{1,0:T(4,128)S(1)} %exp.23, f32[4,128]{1,0:T(4,128)S(1)} %rev.13, f32[4,128]{1,0:T(4,128)S(1)} %get-tuple-element.298, pred[128,128]{1,0:T(8,128)(4,1)S(1)} %iota_compare_fusion), kind=kOutput, calls=%fused_computation.39 | convolution fusion | flops 3225681920 | bytes 16865280 | tf_op jit(solution)/shard_map/cxyj,cij->cxyi/dot_general | solution.py:97
  67.2 5.4 %copy.18 = f32[4,64,64,1]{2,1,3,0:T(8,128)S(1)} copy(f32[4,64,64,1]{3,2,1,0:T(8,128)} %bitcast.43) | data formatting | bytes 131072 | tf_op jit(solution)/shard_map/slice | solution.py:102
  72.6 13.0 %all-gather.3 = f32[16,64,64,1]{2,1,3,0:T(8,128)S(1)} all-gather(f32[4,64,64,1]{2,1,3,0:T(8,128)S(1)} %copy.18), channel_id=5, replica_groups=mesh['gz'=4,'gx'=2,'gy'=4] {'gz'}, dimensions={0}, use_global_device_ids=true | all-gather | bytes 327680 | tf_op jit(solution)/shard_map/all_gather | solution.py:12
  85.6 0.4 while.29
  85.7 0.1 fusion.58
  85.8 0.1 fusion.58
  85.9 0.1 fusion.58
  86.0 0.0 copy-start.3
  86.0 0.0 copy-start.5
  86.1 0.0 copy-start.6
  86.1 0.0 copy-start.7
  86.1 6.0 %add_convert_fusion = bf16[4,64,64,128]{3,2,1,0:T(8,128)(2,1)S(1)} fusion(f32[4,64,64,128]{3,2,1,0:T(8,128)} %fusion.18, f32[4,64,64]{2,1,0:T(8,128)S(1)} %get-tuple-element.191, f32[4,128]{1,0:T(4,128)S(1)} %exp.25), kind=kLoop, calls=%fused_computation.38 | loop fusion | flops 6291456 | bytes 12650496 | tf_op jit(solution)/shard_map/convert_element_type | solution.py:116
  92.0 0.0 copy-start.1
  92.1 2.1 copy-done.1
  94.2 3.1 %collective-permute-start = (bf16[4,3,64,128]{3,2,1,0:T(8,128)(2,1)S(1)}, bf16[4,3,64,128]{3,2,1,0:T(8,128)(2,1)S(1)}, u32[]{:S(2)}, u32[]{:S(2)}) collective-permute-start(bf16[4,3,64,128]{3,2,1,0:T(8,128)(2,1)S(1)} %get-tuple-element.295), channel_id=1, source_target_pairs={{0,4},{1,5},{2,6},{3,7},{8,12},{9,13},{10,14},{11,15},{16,20},{17,... | collective-permute-start | bytes 589832 | tf_op jit(solution)/shard_map/ppermute | solution.py:34
  97.3 1.3 collective-permute-start.1
  98.6 0.6 fusion.49
  99.2 0.0 copy-done.3
  99.2 0.0 copy-done.5
  99.2 1.5 fusion.9
  100.7 0.7 broadcast_divide_fusion
  101.4 45.9 %psum.7 = f32[4]{0:T(128)S(1)} all-reduce(f32[4]{0:T(128)S(1)} %fusion.9), channel_id=1, replica_groups=mesh['gz'=4,'gx'=2,'gy'=4] {'gz','gx','gy'}, use_global_device_ids=true, to_apply=%region_10.11 | all-reduce | flops 4 | bytes 32 | tf_op jit(solution)/shard_map/psum | solution.py:126
  147.3 0.7 fusion.54
  148.0 0.0 copy-done.6
  148.0 0.0 copy-done.7
  148.0 0.2 select_reduce_fusion
  148.2 0.0 collective-permute-done
  148.2 0.0 collective-permute-done.1
  148.2 1.5 pad_maximum_fusion.2
  149.7 5.3 %collective-permute-start.2 = (bf16[4,70,3,128]{3,2,1,0:T(4,128)(2,1)S(1)}, bf16[4,70,3,128]{3,2,1,0:T(4,128)(2,1)S(1)}, u32[]{:S(2)}, u32[]{:S(2)}) collective-permute-start(bf16[4,70,3,128]{3,2,1,0:T(4,128)(2,1)S(1)} %get-tuple-element.292), channel_id=1, source_target_pairs={{0,1},{1,2},{2,3},{4,5},{5,6},{6,7},{8,9},{9,10},{10,11},{12,13},{... | collective-permute-start | bytes 645128 | tf_op jit(solution)/shard_map/ppermute | solution.py:34
  155.0 2.1 collective-permute-start.3
  157.1 0.5 broadcast_multiply_fusion.1
  157.6 0.9 collective-permute-done.2
  158.5 4.4 %collective-permute-done.3 = bf16[4,70,3,128]{3,2,1,0:T(4,128)(2,1)S(1)} collective-permute-done((bf16[4,70,3,128]{3,2,1,0:T(4,128)(2,1)S(1)}, bf16[4,70,3,128]{3,2,1,0:T(4,128)(2,1)S(1)}, u32[]{:S(2)}, u32[]{:S(2)}) %collective-permute-start.3) | collective-permute-done | bytes 215072 | tf_op jit(solution)/shard_map/ppermute | solution.py:35
  162.9 8.4 %maximum_convert_fusion = f32[4,70,70,128]{3,2,1,0:T(8,128)} fusion(bf16[4,70,3,128]{3,2,1,0:T(4,128)(2,1)S(1)} %collective-permute-done.3, bf16[4,3,64,128]{3,2,1,0:T(8,128)(2,1)S(1)} %collective-permute-done.1, bf16[4,64,64,128]{3,2,1,0:T(8,128)(2,1)} %copy-done.1, bf16[4,3,64,128]{3,2,1,0:T(8,128)(2,1)S(1)} %collective-permute-done, ...), kind=kLoop, calls=%fused_computation.43 | loop fusion | flops 25088000 | bytes 15052800 | tf_op jit(solution)/shard_map/convert_element_type | solution.py:116
  171.3 30.3 %fusion.2 = f32[4,64,70,128]{3,2,1,0:T(8,128)} fusion(f32[4,70,70,128]{3,2,1,0:T(8,128)} %maximum_convert_fusion, f32[]{:T(128)} %bitcast.15, f32[]{:T(128)} %bitcast.14, f32[]{:T(128)} %bitcast.13, f32[]{:T(128)} %bitcast.12, f32[]{:T(128)} %bitcast.11, f32[]{:T(128)} %bitcast.10, f32[]{:T(128)} %bitcast), kind=kLoop, calls=%fused_computation.9 | loop fusion | flops 29818880 | bytes 73400352 | tf_op jit(solution)/shard_map/add | solution.py:52
  201.6 28.3 %fusion.21 = f32[64,64,128]{2,1,0:T(8,128)S(1)} fusion(f32[4,64,70,128]{3,2,1,0:T(8,128)} %fusion.2, f32[64,64,128]{2,1,0:T(8,128)S(1)} %get-tuple-element.294, f32[]{:T(128)} %bitcast.15, f32[]{:T(128)} %bitcast.14, f32[]{:T(128)} %bitcast.13, f32[]{:T(128)} %bitcast.12, f32[]{:T(128)} %bitcast.11, f32[]{:T(128)} %bitcast.10, f32[]{:T(128)} %bitcast, ...), kind=kLoop, calls=%fused_computation.42 | loop fusion | flops 33030144 | bytes 62914604 | tf_op jit(solution)/shard_map/reduce_sum | solution.py:123
  229.9 0.0 copy-done.4
  229.9 1.7 compare_select_fusion
  (19 shorter events, 0.2 us)
Async XLA Ops:
  15.8 4.5 %copy-start.2 = (bf16[4,64,64,128]{3,2,1,0:T(8,128)(2,1)S(1)}, bf16[4,64,64,128]{3,2,1,0:T(8,128)(2,1)}, u32[]{:S(2)}) copy-start(bf16[4,64,64,128]{3,2,1,0:T(8,128)(2,1)} %param.12) | copy-start | bytes 12582916
  28.9 3.2 %copy-start = (f32[4,64,64,128]{3,2,1,0:T(8,128)}, f32[4,64,64,128]{3,2,1,0:T(8,128)S(1)}, u32[]{:S(2)}) copy-start(f32[4,64,64,128]{3,2,1,0:T(8,128)S(1)} %fusion.8) | copy-start | bytes 25165828
  86.0 13.2 %copy-start.3 = (bf16[4,64,64,128]{3,2,1,0:T(8,128)(2,1)S(1)}, bf16[4,64,64,128]{3,2,1,0:T(8,128)(2,1)}, u32[]{:S(2)}) copy-start(bf16[4,64,64,128]{3,2,1,0:T(8,128)(2,1)} %param.12) | copy-start | bytes 12582916
  86.0 13.2 %copy-start.5 = (f32[64,64,128]{2,1,0:T(8,128)S(1)}, f32[64,64,128]{2,1,0:T(8,128)}, u32[]{:S(2)}) copy-start(f32[64,64,128]{2,1,0:T(8,128)} %get-tuple-element.291) | copy-start | bytes 6291460
  86.1 62.0 %copy-start.6 = (f32[16]{0:T(128)S(1)}, f32[16]{0:T(128)}, u32[]{:S(2)}) copy-start(f32[16]{0:T(128)} %param.15) | copy-start | bytes 196
  86.1 61.9 %copy-start.7 = (s32[4]{0:T(128)S(1)}, s32[4]{0:T(128)}, u32[]{:S(2)}) copy-start(s32[4]{0:T(128)} %param.14) | copy-start | bytes 52
  92.0 2.1 copy-start.1
  94.2 54.0 %collective-permute-start = (bf16[4,3,64,128]{3,2,1,0:T(8,128)(2,1)S(1)}, bf16[4,3,64,128]{3,2,1,0:T(8,128)(2,1)S(1)}, u32[]{:S(2)}, u32[]{:S(2)}) collective-permute-start(bf16[4,3,64,128]{3,2,1,0:T(8,128)(2,1)S(1)} %get-tuple-element.295), channel_id=1, source_target_pairs={{0,4},{1,5},{2,6},{3,7},{8,12},{9,13},{10,14},{11,15},{16,20},{17,... | collective-permute-start | bytes 589832 | tf_op jit(solution)/shard_map/ppermute | solution.py:34
  97.3 50.9 %collective-permute-start.1 = (bf16[4,3,64,128]{3,2,1,0:T(8,128)(2,1)S(1)}, bf16[4,3,64,128]{3,2,1,0:T(8,128)(2,1)S(1)}, u32[]{:S(2)}, u32[]{:S(2)}) collective-permute-start(bf16[4,3,64,128]{3,2,1,0:T(8,128)(2,1)S(1)} %get-tuple-element.296), channel_id=1, source_target_pairs={{4,0},{5,1},{6,2},{7,3},{12,8},{13,9},{14,10},{15,11},{20,16},{21,... | collective-permute-start | bytes 589832 | tf_op jit(solution)/shard_map/ppermute | solution.py:35
  149.7 8.8 %collective-permute-start.2 = (bf16[4,70,3,128]{3,2,1,0:T(4,128)(2,1)S(1)}, bf16[4,70,3,128]{3,2,1,0:T(4,128)(2,1)S(1)}, u32[]{:S(2)}, u32[]{:S(2)}) collective-permute-start(bf16[4,70,3,128]{3,2,1,0:T(4,128)(2,1)S(1)} %get-tuple-element.292), channel_id=1, source_target_pairs={{0,1},{1,2},{2,3},{4,5},{5,6},{6,7},{8,9},{9,10},{10,11},{12,13},{... | collective-permute-start | bytes 645128 | tf_op jit(solution)/shard_map/ppermute | solution.py:34
  155.0 8.0 %collective-permute-start.3 = (bf16[4,70,3,128]{3,2,1,0:T(4,128)(2,1)S(1)}, bf16[4,70,3,128]{3,2,1,0:T(4,128)(2,1)S(1)}, u32[]{:S(2)}, u32[]{:S(2)}) collective-permute-start(bf16[4,70,3,128]{3,2,1,0:T(4,128)(2,1)S(1)} %get-tuple-element.293), channel_id=1, source_target_pairs={{1,0},{2,1},{3,2},{5,4},{6,5},{7,6},{9,8},{10,9},{11,10},{13,12},{... | collective-permute-start | bytes 645128 | tf_op jit(solution)/shard_map/ppermute | solution.py:35
  201.6 28.3 %copy-start.4 = (s32[64,64,128]{2,1,0:T(8,128)S(1)}, s32[64,64,128]{2,1,0:T(8,128)}, u32[]{:S(2)}) copy-start(s32[64,64,128]{2,1,0:T(8,128)} %param.11) | copy-start | bytes 6291460
where the time goes:
time: 232 us
  other arithmetic  86 us (37%)
  blocking collectives  82.4 us (36%)
  local copies, waits for them, and re-layouts  24.7 us (11%)
  matrix products  19.7 us (8%)
  starting transfers between devices  11.8 us (5%)
  waiting for transfers between devices  5.3 us (2%)
    psum x1, blocking collectives, shards(): totals = lax.psum(partial_sums, ('gz', 'gx', 'gy'))  45.9 us
    add x1, other arithmetic, planar_filter(): along_x = along_x + taps[offset] * padded[:, offset:offset + width_x]  30.3 us
    reduce_sum x1, other arithmetic, shards(): combined = jnp.sum(weights[:, None, None, None] * filtered, axis=0)  28.3 us
    all_gather x2, blocking collectives, entering_2(): pieces = jax.tree.map(lambda part: lax.all_gather(part, axis), value)  25.8 us
    dot_general x1, matrix products, slab_smooth(): jnp.einsum('cxyj,cij->cxyi', forward, backward_map, precision=lax.Precisi...  11.1 us
    slice x2, local copies, waits for them, and re-layouts, slab_smooth(): local_forward[..., -1]  10.8 us
    unnamed x1, blocking collectives  10.7 us
    dot_general x1, matrix products, slab_smooth(): jnp.einsum('cxyj,cij->cxyi', field, forward_map, precision=lax.Precision....  8.58 us
  transfers between devices with their start and end apart: 4, of which 2 were waited for; matrix products, arithmetic and copies ran while one was open for 2% of the time, Pallas kernels for 0%

commit v1 on v0

v1 whole, which is shorter than its diff:
```python
import functools
import jax
import jax.numpy as jnp
from jax import lax
from jax.experimental import pallas as pl
from jax.experimental.pallas import tpu as pltpu
from jax.sharding import PartitionSpec as P
import math

RADIUS = 3
LANES = 128
F32 = jnp.float32
BF16 = jnp.bfloat16
HIGH = lax.Precision.HIGHEST


def taps_1d():
    raw = [math.exp(-2.0 * k * k / (RADIUS * RADIUS)) for k in range(-RADIUS, RADIUS + 1)]
    total = sum(raw)
    return [r / total for r in raw]


def dot_hi(a, b, dims=((1,), (0,))):
    return lax.dot_general(a, b, (dims, ((), ())), precision=HIGH, preferred_element_type=F32)


def split2(v):
    hi = v.astype(BF16)
    lo = (v - hi.astype(F32)).astype(BF16)
    return hi, lo


def slab_kernel(cases, depth, bx, ny, nsteps, *refs):
    (index_ref, weight_ref, decay_ref, density_ref, mask_ref, energy_ref,
     t_ref, states_ref, umap_ref, rmat, wmat, acc) = refs
    step = pl.program_id(0)
    cols = bx * ny

    @pl.when(step == 0)
    def _():
        acc[...] = jnp.zeros_like(acc)
        states_ref[...] = jnp.zeros_like(states_ref)
        decay = decay_ref[...]
        logs = jnp.log(decay)
        row = lax.broadcasted_iota(jnp.int32, (depth, depth), 0)
        col = lax.broadcasted_iota(jnp.int32, (depth, depth), 1)
        upto = (row <= col).astype(F32)
        up = dot_hi(logs, upto)
        up_ex = up - logs
        up_t = jnp.transpose(up)
        logs_t = jnp.transpose(logs)
        keep_t = 1.0 - jnp.transpose(decay)
        up_ex_t = up_t - logs_t
        total = up[:, depth - 1:depth]
        zero_row = jnp.zeros((1, depth), F32)
        e_rows, h_rows, a_rows, c_rows = [], [], [], []
        d_col, k_col = [], []
        for c in range(cases):
            scale = -3.0 * weight_ref[index_ref[c]]
            keep = keep_t[:, c:c + 1]
            gap_f = up[c:c + 1, :] - up_t[:, c:c + 1]
            f_t = jnp.where(col >= row, jnp.exp(jnp.minimum(gap_f, 0.0)), 0.0) * keep
            gap_b = up_ex_t[:, c:c + 1] - up_ex[c:c + 1, :]
            b_t = jnp.where(col <= row, jnp.exp(jnp.minimum(gap_b, 0.0)), 0.0) * keep
            full = dot_hi(f_t, b_t) * scale
            hi, lo = split2(full)
            rmat[c * depth:(c + 1) * depth, 0:depth] = hi
            rmat[c * depth:(c + 1) * depth, depth:2 * depth] = lo
            e_row = jnp.exp(total[c:c + 1] - up[c:c + 1, :]) * (1.0 - decay[c:c + 1, :]) * scale
            b_row = jnp.exp(up_ex[c:c + 1, :]) * (1.0 - decay[c:c + 1, :])
            h_row = dot_hi(b_row, f_t, ((1,), (1,))) * scale
            pads = lambda r: jnp.concatenate([zero_row] * c + [r] + [zero_row] * (cases - 1 - c), axis=1)
            e_rows.append(pads(e_row))
            h_rows.append(pads(h_row))
            lead = jnp.exp(up[c:c + 1, :])
            a_row = dot_hi(lead, b_t)
            c_row = jnp.exp(total[c:c + 1] - up_ex[c:c + 1, :])
            a_rows.append(a_row)
            c_rows.append(c_row)
        w_hi, w_lo = split2(jnp.concatenate(e_rows + h_rows, axis=0))
        wmat[...] = jnp.concatenate([w_hi, w_lo], axis=0)
        a_all = jnp.concatenate(a_rows, axis=0)
        u_all = jnp.concatenate([a_all] + c_rows, axis=0)
        u_hi = u_all.astype(BF16).astype(F32)
        u_lo = u_all - u_hi
        umap_ref[...] = jnp.concatenate([u_hi, u_hi, u_lo, jnp.zeros_like(u_lo)], axis=0)
        aux = nsteps * cols
        lane = lax.broadcasted_iota(jnp.int32, (cases, LANES), 1)
        states_ref[0:cases, aux:aux + LANES] = jnp.where(
            lane == 0, jnp.exp(total), jnp.where(lane == 1, a_all[:, 0:1], 0.0))

    mask = mask_ref[...]
    dense = jnp.where(mask == 1, 0.001, jnp.where(mask == 2, 1.0, density_ref[...]))
    cube = dense * dense * dense
    parts = []
    for c in range(cases):
        work = cube * energy_ref[c].astype(F32)
        acc[c] += jnp.sum(work.reshape(cols // 8, 8, depth), axis=0)
        parts.append(work.astype(BF16).reshape(cols, depth))
    source = jnp.concatenate(parts, axis=1)
    both = lax.dot_general(source, rmat[...], (((1,), (0,)), ((), ())), preferred_element_type=F32)
    t_ref[...] = (both[:, 0:depth] + both[:, depth:2 * depth]).reshape(bx, ny, depth)
    faces = lax.dot_general(wmat[...], source, (((1,), (1,)), ((), ())), preferred_element_type=F32)
    start = pl.multiple_of(step * cols, LANES)
    states_ref[:, pl.ds(start, cols)] = faces[0:2 * cases] + faces[2 * cases:4 * cases]

    @pl.when(step == nsteps - 1)
    def _():
        aux = nsteps * cols
        lane = lax.broadcasted_iota(jnp.int32, (cases, LANES), 1)
        sums = jnp.sum(jnp.sum(acc[...], axis=1), axis=1, keepdims=True)
        now = states_ref[0:cases, aux:aux + LANES]
        states_ref[0:cases, aux:aux + LANES] = jnp.where(lane == 2, sums, now)


def slab_call(density, design_mask, energy, decay, case_index, case_weight):
    cases, nx, ny, depth = energy.shape
    bx = 8
    nsteps = nx // bx
    body = functools.partial(slab_kernel, cases, depth, bx, ny, nsteps)
    smem = pl.BlockSpec(memory_space=pltpu.SMEM)
    whole = lambda shape: pl.BlockSpec(shape, lambda i: (0,) * len(shape))
    return pl.pallas_call(
        body,
        grid=(nsteps,),
        in_specs=[
            smem, smem, whole((cases, depth)),
            pl.BlockSpec((bx, ny, depth), lambda i: (i, 0, 0)),
            pl.BlockSpec((bx, ny, depth), lambda i: (i, 0, 0)),
            pl.BlockSpec((cases, bx, ny, depth), lambda i: (0, i, 0, 0)),
        ],
        out_specs=[
            pl.BlockSpec((bx, ny, depth), lambda i: (i, 0, 0)),
            whole((2 * cases, nx * ny + LANES)),
            whole((8 * cases, depth)),
        ],
        out_shape=[
            jax.ShapeDtypeStruct((nx, ny, depth), F32),
            jax.ShapeDtypeStruct((2 * cases, nx * ny + LANES), F32),
            jax.ShapeDtypeStruct((8 * cases, depth), F32),
        ],
        scratch_shapes=[
            pltpu.VMEM((cases * depth, 2 * depth), BF16),
            pltpu.VMEM((4 * cases, cases * depth), BF16),
            pltpu.VMEM((cases, 8, depth), F32),
        ],
        compiler_params=pltpu.CompilerParams(
            dimension_semantics=("arbitrary",), vmem_limit_bytes=24 * 2**20),
        name="slab",
    )(case_index, case_weight, decay, density, design_mask, energy)


def couple_kernel(cases, nslabs, nx, ny, depth, *refs):
    slot_ref, msgs, t_ref, umap_ref = refs[0], refs[1:1 + nslabs], refs[1 + nslabs], refs[2 + nslabs]
    out_ref, xedge_ref, sums_ref, gains = refs[3 + nslabs:]
    cols = nx * ny
    mine = slot_ref[0]
    up_x = slot_ref[1]

    def pick(j):
        return None

    stack = gains
    for m in range(nslabs):
        stack[m] = msgs[m][...]
    comp = jnp.zeros((2 * cases, LANES), F32)
    for m in range(nslabs):
        comp = comp + stack[m, :, cols:cols + LANES]
    sums_ref[...] = comp
    state = jnp.zeros((cases, cols), F32)
    entering = jnp.zeros((cases, cols), F32)
    tops = []
    scalars = []
    for j in range(nslabs):
        at = slot_ref[2 + j]
        aux = stack[at, 0:cases, cols:cols + LANES]
        gain, turn = aux[:, 0:1], aux[:, 1:2]
        scalars.append((at, gain))
        entering = jnp.where(mine == j, state, entering)
        tops.append(stack[at, cases:2 * cases, 0:cols] + turn * state)
        state = gain * state + stack[at, 0:cases, 0:cols]
    state = jnp.zeros((cases, cols), F32)
    above = jnp.zeros((cases, cols), F32)
    for j in reversed(range(nslabs)):
        gain = scalars[j][1]
        above = jnp.where(mine == j, state, above)
        state = tops[j] + gain * state
    faces = jnp.concatenate([entering, above], axis=0)
    hi = faces.astype(BF16).astype(F32)
    lo = faces - hi
    lhs = jnp.concatenate([hi, lo, hi, jnp.zeros_like(hi)], axis=0).astype(BF16)
    add = lax.dot_general(lhs, umap_ref[...].astype(BF16), (((0,), (0,)), ((), ())), preferred_element_type=F32)
    out_ref[...] = t_ref[...] + add.reshape(nx, ny, depth)
    xedge_ref[...] = out_ref[pl.ds(up_x, RADIUS)].astype(BF16)


def couple_call(slots, msgs, t_local, umap, cases):
    nx, ny, depth = t_local.shape
    nslabs = len(msgs)
    body = functools.partial(couple_kernel, cases, nslabs, nx, ny, depth)
    vm = pl.BlockSpec(memory_space=pltpu.VMEM)
    return pl.pallas_call(
        body,
        in_specs=[pl.BlockSpec(memory_space=pltpu.SMEM)] + [vm] * (nslabs + 2),
        out_specs=[vm, vm, vm],
        out_shape=[
            jax.ShapeDtypeStruct((nx, ny, depth), F32),
            jax.ShapeDtypeStruct((RADIUS, ny, depth), BF16),
            jax.ShapeDtypeStruct((2 * cases, LANES), F32),
        ],
        scratch_shapes=[pltpu.VMEM((nslabs, 2 * cases, nx * ny + LANES), F32)],
        compiler_params=pltpu.CompilerParams(vmem_limit_bytes=32 * 2**20),
        name="couple",
    )(slots, *msgs, t_local, umap)


def yedge_kernel(nx, ny, depth, t_ref, xb_ref, xa_ref, first_ref, last_ref):
    lead = jnp.zeros((RADIUS + 2, depth), F32)
    for k in range(RADIUS):
        for ref, y in ((first_ref, k), (last_ref, ny - RADIUS + k)):
            mid = t_ref[:, y, :]
            before = xb_ref[:, y, :].astype(F32)
            after = xa_ref[:, y, :].astype(F32)
            ref[k] = jnp.concatenate([before, mid, after, jnp.zeros((10, depth), F32)], axis=0).astype(BF16)


YPAD = 8


def plane_kernel(nx, ny, depth, bx, *refs):
    (t_ref, xb_ref, xa_ref, yb_ref, ya_ref, density_ref, mask_ref, out_ref, pad, line) = refs
    step = pl.program_id(0)
    taps = taps_1d()

    @pl.when(step == 0)
    def _():
        pad[RADIUS:RADIUS + nx, YPAD:YPAD + ny, :] = t_ref[...]
        pad[0:RADIUS, YPAD:YPAD + ny, :] = xb_ref[...].astype(F32)
        pad[RADIUS + nx:, YPAD:YPAD + ny, :] = xa_ref[...].astype(F32)
        rows = nx + 2 * RADIUS
        for k in range(RADIUS):
            pad[:, YPAD - RADIUS + k, :] = yb_ref[k, 0:rows].astype(F32)
            pad[:, YPAD + ny + k, :] = ya_ref[k, 0:rows].astype(F32)

    def one(i, carry):
        x = step * bx + i
        acc = taps[RADIUS] * pad[x + RADIUS]
        for k in range(RADIUS):
            acc = acc + taps[k] * (pad[x + k] + pad[x + 2 * RADIUS - k])
        line[...] = acc
        res = taps[RADIUS] * line[YPAD:YPAD + ny, :]
        for k in range(RADIUS):
            off = RADIUS - k
            res = res + taps[k] * (line[YPAD - off:YPAD - off + ny, :] + line[YPAD + off:YPAD + off + ny, :])
        out_ref[i] = jnp.where(mask_ref[i] == 0, res / jnp.maximum(density_ref[i], 0.1), 0.0)
        return carry

    lax.fori_loop(0, bx, one, 0, unroll=2)


def plane_call(t, xb, xa, yb, ya, density, design_mask):
    nx, ny, depth = t.shape
    bx = 8
    whole = lambda a: pl.BlockSpec(a.shape, lambda i: (0,) * a.ndim)
    blk = pl.BlockSpec((bx, ny, depth), lambda i: (i, 0, 0))
    return pl.pallas_call(
        functools.partial(plane_kernel, nx, ny, depth, bx),
        grid=(nx // bx,),
        in_specs=[whole(t), whole(xb), whole(xa), whole(yb), whole(ya), blk, blk],
        out_specs=blk,
        out_shape=jax.ShapeDtypeStruct(t.shape, F32),
        scratch_shapes=[
            pltpu.VMEM((nx + 2 * RADIUS, ny + 2 * YPAD, depth), F32),
            pltpu.VMEM((ny + 2 * YPAD, depth), F32),
        ],
        compiler_params=pltpu.CompilerParams(
            dimension_semantics=("arbitrary",), vmem_limit_bytes=24 * 2**20),
        name="plane",
    )(t, xb, xa, yb, ya, density, design_mask)


def pairs_of(count, first):
    out = []
    for i in range(first, count - 1, 2):
        out += [(i, i + 1), (i + 1, i)]
    return out


def xor_pairs(count, m):
    return [(i, i ^ m) for i in range(count)]


def shards(density, design_mask, energy, decay, case_index, case_weight):
    cases = energy.shape[0]
    nx, ny, depth = density.shape
    nz, gx, gy = (lax.axis_size(a) for a in ("gz", "gx", "gy"))
    iz, ix, iy = (lax.axis_index(a) for a in ("gz", "gx", "gy"))
    t_local, states, umap = slab_call(density, design_mask, energy, decay, case_index, case_weight)
    if nz & (nz - 1) == 0 and nz <= 4:
        msgs = [states] + [lax.ppermute(states, "gz", xor_pairs(nz, m)) for m in range(1, nz)]
        order = [iz ^ j for j in range(nz)]
    else:
        every = lax.all_gather(states, "gz")
        msgs = [every[j] for j in range(nz)]
        order = [jnp.int32(j) for j in range(nz)]
    even_x, even_y = ix % 2 == 0, iy % 2 == 0
    slots = jnp.stack([iz, jnp.where(even_x, nx - RADIUS, 0)] + order).astype(jnp.int32)
    t, xedge, sums = couple_call(slots, msgs, t_local, umap, cases)
    totals = sums[0:cases, 2]
    none = jnp.zeros_like(xedge)
    if gx > 1:
        swap = lax.ppermute(xedge, "gx", pairs_of(gx, 0))
        other = none
        if gx > 2:
            far = jnp.where(even_x, t[0:RADIUS], t[nx - RADIUS:]).astype(BF16)
            other = lax.ppermute(far, "gx", pairs_of(gx, 1))
        before = jnp.where(even_x, other, swap)
        after = jnp.where(even_x, swap, other)
    else:
        before = after = none
    rows = nx + 16
    first, last = pl.pallas_call(
        functools.partial(yedge_kernel, nx, ny, depth),
        out_shape=[jax.ShapeDtypeStruct((RADIUS, rows, depth), BF16)] * 2,
        compiler_params=pltpu.CompilerParams(vmem_limit_bytes=16 * 2**20),
        name="yedge",
    )(t, before, after)
    none = jnp.zeros_like(first)
    if gy > 1:
        swap = lax.ppermute(jnp.where(even_y, last, first), "gy", pairs_of(gy, 0))
        other = none
        if gy > 2:
            other = lax.ppermute(jnp.where(even_y, first, last), "gy", pairs_of(gy, 1))
        y_before = jnp.where(even_y, other, swap)
        y_after = jnp.where(even_y, swap, other)
    else:
        y_before = y_after = none
    sensitivity = plane_call(t, before, after, y_before, y_after, density, design_mask)
    for axis, n in (("gx", gx), ("gy", gy)):
        step = 1
        while step < n:
            totals = totals + lax.ppermute(totals, axis, xor_pairs(n, step))
            step *= 2
    all_cells = nx * ny * depth * nz * gx * gy
    return sensitivity, totals / all_cells


def solution(mesh):
    placed = (
        P("gx", "gy", "gz"),
        P("gx", "gy", "gz"),
        P(None, "gx", "gy", "gz"),
        P(None, "gz"),
        P(),
        P(),
    )
    return jax.shard_map(
        shards, mesh=mesh, in_specs=placed, out_specs=(P("gx", "gy", "gz"), P()), check_vma=False
    )
```

time: 232 us -> 50.6 us (0.22)
  other arithmetic: 86 us -> 0.56 us
  blocking collectives: 82.4 us -> 0 us
  matrix products: 19.7 us -> 0 us
  local copies, waits for them, and re-layouts: 24.7 us -> 7.63 us
  Pallas kernels: 0 us -> 12 us
  waiting for transfers between devices: 5.3 us -> 16.5 us
    psum x1 -> x0, blocking collectives: 45.9 us -> none  [shards(): totals = lax.psum(partial_sums, ('gz', 'gx', 'gy'))]
    reduce_sum x4 -> x0, other arithmetic: 30.6 us -> none  [the longest x1 28.3 us: shards(): combined = jnp.sum(weights[:, None, None, None] * filtered, axis=0)]
    add x1 -> x2, other arithmetic: 30.3 us -> 0.01 us  [shards(): totals = totals + lax.ppermute(totals, axis, xor_pairs(n, step))]
    all_gather x2 -> x0, blocking collectives: 25.8 us -> none  [entering_2(): pieces = jax.tree.map(lambda part: lax.all_gather(part, axis), value)]
    dot_general x2 -> x0, matrix products: 19.7 us -> none  [the longest x1 11.1 us: slab_smooth(): jnp.einsum('cxyj,cij->cxyi', forward, backward_map, precision=lax.Precisi...]
    slice x7 -> x1, local copies, waits for them, and re-layouts: 17.2 us -> 0.18 us  [shards(): totals = sums[0:cases, 2]]
    convert_element_type x2 -> x0, other arithmetic: 14.4 us -> none  [the longest x1 8.41 us: shards(): with_halo(along_z.astype(jnp.bfloat16), (('gx', 1), ('gy', 2)), RADIUS)]
    pallas_call x0 -> x4, Pallas kernels: none -> 12 us  [the longest x1 5.91 us: slab_call(): pl.pallas_call(body, grid=(nsteps,), in_specs=[smem, smem, whole((cases,...]
  transfers between devices with their start and end apart: 4 -> 9, of which waited for: 2 -> 5; matrix products, arithmetic and copies ran while one was open for 2% -> 2% of each run, Pallas kernels for 0% -> 0%
where the time goes in v1:
time: 50.6 us; the launch traced here: 50.3 us
  waiting for transfers between devices  16.5 us (33%)
  starting transfers between devices  12.9 us (25%)
  Pallas kernels  12 us (24%)
  local copies, waits for them, and re-layouts  7.63 us (15%)
  between operations  0.72 us (1%)
  other arithmetic  0.56 us (1%)
    ppermute x3, waiting for transfers between devices, shards(): lax.ppermute(states, 'gz', xor_pairs(nz, m))  10.6 us
    unnamed x16, local copies, waits for them, and re-layouts  7.36 us
    pallas_call x1, Pallas kernels, slab_call(): pl.pallas_call(body, grid=(nsteps,), in_specs=[smem, smem, whole((cases,...  5.91 us
    pallas_call x1, Pallas kernels, plane_call(): pl.pallas_call(functools.partial(plane_kernel, nx, ny, depth, bx), grid=(...  4.7 us
    ppermute x3, starting transfers between devices, shards(): lax.ppermute(states, 'gz', xor_pairs(nz, m))  4.54 us
    ppermute x3, starting transfers between devices, shards(): totals = totals + lax.ppermute(totals, axis, xor_pairs(n, step))  4.33 us
    ppermute x3, waiting for transfers between devices, shards(): totals = totals + lax.ppermute(totals, axis, xor_pairs(n, step))  2.98 us
    ppermute x1, waiting for transfers between devices, shards(): other = lax.ppermute(jnp.where(even_y, first, last), 'gy', pairs_of(gy, 1))  2.96 us
  transfers between devices with their start and end apart: 9, of which 5 were waited for; matrix products, arithmetic and copies ran while one was open for 2% of the time, Pallas kernels for 0%

profile of v1, /device:TPU:1, one launch (start us, length us, event | category | flops | bytes accessed | tf_op | source)
XLA Modules:
  0.0 50.3 jit_solution(15473690664736216891)
XLA Ops:
  0.6 0.0 copy-start
  0.6 1.6 %copy-done = f32[64,64,128]{2,1,0:T(8,128)S(1)} copy-done((f32[64,64,128]{2,1,0:T(8,128)S(1)}, f32[64,64,128]{2,1,0:T(8,128)}, u32[]{:S(2)}) %copy-start) | copy-done | bytes 2097176
  2.2 0.0 copy-start.2
  2.2 1.6 %copy-done.2 = s32[64,64,128]{2,1,0:T(8,128)S(1)} copy-done((s32[64,64,128]{2,1,0:T(8,128)S(1)}, s32[64,64,128]{2,1,0:T(8,128)}, u32[]{:S(2)}) %copy-start.2) | copy-done | bytes 2097176
  3.8 0.0 copy-start.4
  3.8 2.2 %copy-done.4 = bf16[4,64,64,128]{3,2,1,0:T(8,128)(2,1)S(1)} copy-done((bf16[4,64,64,128]{3,2,1,0:T(8,128)(2,1)S(1)}, bf16[4,64,64,128]{3,2,1,0:T(8,128)(2,1)}, u32[]{:S(2)}) %copy-start.4) | copy-done | bytes 4194328
  6.0 0.0 copy-start.5
  6.0 0.7 %copy-done.5 = f32[4,128]{1,0:T(4,128)S(1)} copy-done((f32[4,128]{1,0:T(4,128)S(1)}, f32[4,128]{1,0:T(4,128)}, u32[]{:S(2)}) %copy-start.5) | copy-done | bytes 2072
  6.7 0.0 copy-start.6
  6.7 0.7 %copy-done.6 = s32[4]{0:T(128)S(1)} copy-done((s32[4]{0:T(128)S(1)}, s32[4]{0:T(128)}, u32[]{:S(2)}) %copy-start.6) | copy-done | bytes 40
  7.3 0.0 copy-start.7
  7.3 0.7 %copy-done.7 = f32[16]{0:T(128)S(1)} copy-done((f32[16]{0:T(128)S(1)}, f32[16]{0:T(128)}, u32[]{:S(2)}) %copy-start.7) | copy-done | bytes 88
  8.0 5.9 %slab.1 = (f32[64,64,128]{2,1,0:T(8,128)S(1)}, f32[8,4224]{1,0:T(8,128)S(1)}, f32[32,128]{1,0:T(8,128)S(1)}) custom-call(s32[4]{0:T(128)S(1)} %copy-done.6, f32[16]{0:T(128)S(1)} %copy-done.7, f32[4,128]{1,0:T(4,128)S(1)} %copy-done.5, f32[64,64,128]{2,1,0:T(8,128)S(1)} %copy-done, s32[64,64,128]{2,1,0:T(8,128)S(1)} %copy-done.2, ...), custom_call_target="tpu_custom_call" | custom-call | tf_op jit(solution)/shard_map/slab/pallas_call | solution.py:123
  13.9 4.2 %collective-permute-start.2 = (f32[8,4224]{1,0:T(8,128)S(1)}, f32[8,4224]{1,0:T(8,128)S(1)}, u32[]{:S(2)}, u32[]{:S(2)}) collective-permute-start(f32[8,4224]{1,0:T(8,128)S(1)} %get-tuple-element.10.refs_1_), channel_id=1, source_target_pairs={{0,24},{8,16},{16,8},{24,0},{1,25},{9,17},{17,9},{25,1},{2,26},{10... | collective-permute-start | bytes 405512 | tf_op jit(solution)/shard_map/ppermute | solution.py:300
  18.1 0.0 collective-permute-start.1
  18.1 0.4 collective-permute-start
  18.5 0.1 stack.24.refs_0_
  18.5 2.9 %collective-permute-done.2.refs_4_ = f32[8,4224]{1,0:T(8,128)S(1)} collective-permute-done((f32[8,4224]{1,0:T(8,128)S(1)}, f32[8,4224]{1,0:T(8,128)S(1)}, u32[]{:S(2)}, u32[]{:S(2)}) %collective-permute-start.2) | collective-permute-done | bytes 135200 | tf_op jit(solution)/shard_map/ppermute | solution.py:300
  21.4 7.7 %collective-permute-done.1.refs_3_ = f32[8,4224]{1,0:T(8,128)S(1)} collective-permute-done((f32[8,4224]{1,0:T(8,128)S(1)}, f32[8,4224]{1,0:T(8,128)S(1)}, u32[]{:S(2)}, u32[]{:S(2)}) %collective-permute-start.1) | collective-permute-done | bytes 135200 | tf_op jit(solution)/shard_map/ppermute | solution.py:300
  29.1 0.0 collective-permute-done.refs_2_
  29.1 0.0 copy-start.1
  29.1 0.0 copy-start.3
  29.1 1.2 %couple.1 = (f32[64,64,128]{2,1,0:T(8,128)S(1)}, bf16[3,64,128]{2,1,0:T(8,128)(2,1)S(1)}, f32[8,128]{1,0:T(8,128)S(1)}) custom-call(s32[6]{0:T(128)S(1)} %stack.24.refs_0_, f32[8,4224]{1,0:T(8,128)S(1)} %get-tuple-element.10.refs_1_, f32[8,4224]{1,0:T(8,128)S(1)} %collective-permute-done.refs_2_, f32[8,4224]{1,0:T(8,128)S(1)} %collective-permute-done.1.refs_3_, ...), custom_call_target="tpu_custom_call" | custom-call | tf_op jit(solution)/shard_map/couple/pallas_call | solution.py:202
  30.3 1.3 %collective-permute-start.3 = (bf16[3,64,128]{2,1,0:T(8,128)(2,1)S(1)}, bf16[3,64,128]{2,1,0:T(8,128)(2,1)S(1)}, u32[]{:S(2)}, u32[]{:S(2)}) collective-permute-start(bf16[3,64,128]{2,1,0:T(8,128)(2,1)S(1)} %get-tuple-element.14), channel_id=1, source_target_pairs={{0,4},{4,0},{1,5},{5,1},{2,6},{6,2},{3,7},{7,3},{8,12},{12,8},{9,1... | collective-permute-start | bytes 147464 | tf_op jit(solution)/shard_map/ppermute | solution.py:312
  31.6 0.2 slice_reduce_fusion
  31.8 0.3 collective-permute-start.6
  32.1 2.2 %collective-permute-done.6 = f32[4]{0:T(128)S(1)} collective-permute-done((f32[4]{0:T(128)S(1)}, f32[4]{0:T(128)S(1)}, u32[]{:S(2)}, u32[]{:S(2)}) %collective-permute-start.6) | collective-permute-done | bytes 48 | tf_op jit(solution)/shard_map/ppermute | solution.py:342
  34.3 2.8 %collective-permute-start.7 = (f32[4]{0:T(128)S(1)}, f32[4]{0:T(128)S(1)}, u32[]{:S(2)}, u32[]{:S(2)}) collective-permute-start(f32[4]{0:T(128)S(1)} %add.18), channel_id=1, source_target_pairs={{0,1},{1,0},{2,3},{3,2},{4,5},{5,4},{6,7},{7,6},{8,9},{9,8},{10,11... | collective-permute-start | bytes 56 | tf_op jit(solution)/shard_map/ppermute | solution.py:342
  37.1 0.8 %collective-permute-done.7 = f32[4]{0:T(128)S(1)} collective-permute-done((f32[4]{0:T(128)S(1)}, f32[4]{0:T(128)S(1)}, u32[]{:S(2)}, u32[]{:S(2)}) %collective-permute-start.7) | collective-permute-done | bytes 48 | tf_op jit(solution)/shard_map/ppermute | solution.py:342
  37.9 1.2 %collective-permute-start.8 = (f32[4]{0:T(128)S(1)}, f32[4]{0:T(128)S(1)}, u32[]{:S(2)}, u32[]{:S(2)}) collective-permute-start(f32[4]{0:T(128)S(1)} %add.19), channel_id=1, source_target_pairs={{0,2},{1,3},{2,0},{3,1},{4,6},{5,7},{6,4},{7,5},{8,10},{9,11},{10,... | collective-permute-start | bytes 56 | tf_op jit(solution)/shard_map/ppermute | solution.py:342
  39.1 0.0 collective-permute-done.3
  39.1 0.2 yedge.1
  39.3 0.7 %collective-permute-start.5 = (bf16[3,80,128]{2,1,0:T(8,128)(2,1)S(1)}, bf16[3,80,128]{2,1,0:T(8,128)(2,1)S(1)}, u32[]{:S(2)}, u32[]{:S(2)}) collective-permute-start(bf16[3,80,128]{2,1,0:T(8,128)(2,1)S(1)} %get-tuple-element.20), channel_id=1, source_target_pairs={{0,1},{1,0},{2,3},{3,2},{4,5},{5,4},{6,7},{7,6},{8,9},{9,8},{10,11... | collective-permute-start | bytes 184328 | tf_op jit(solution)/shard_map/ppermute | solution.py:330
  40.0 2.0 %collective-permute-start.4 = (bf16[3,80,128]{2,1,0:T(8,128)(2,1)S(1)}, bf16[3,80,128]{2,1,0:T(8,128)(2,1)S(1)}, u32[]{:S(2)}, u32[]{:S(2)}) collective-permute-start(bf16[3,80,128]{2,1,0:T(8,128)(2,1)S(1)} %get-tuple-element.21), channel_id=1, source_target_pairs={{1,2},{2,1},{5,6},{6,5},{9,10},{10,9},{13,14},{14,13},{17,18},{18,... | collective-permute-start | bytes 184328 | tf_op jit(solution)/shard_map/ppermute | solution.py:333
  42.1 0.0 collective-permute-done.8
  42.1 0.5 %add_multiply_fusion = f32[4]{0:T(128)} fusion(f32[4]{0:T(128)S(1)} %add.19, f32[4]{0:T(128)S(1)} %collective-permute-done.8), kind=kLoop, calls=%fused_computation.7 | loop fusion | flops 8 | bytes 48 | tf_op jit(solution)/shard_map/div | solution.py:345
  42.6 0.0 collective-permute-done.5
  42.6 3.0 %collective-permute-done.4 = bf16[3,80,128]{2,1,0:T(8,128)(2,1)S(1)} collective-permute-done((bf16[3,80,128]{2,1,0:T(8,128)(2,1)S(1)}, bf16[3,80,128]{2,1,0:T(8,128)(2,1)S(1)}, u32[]{:S(2)}, u32[]{:S(2)}) %collective-permute-start.4) | collective-permute-done | bytes 61472 | tf_op jit(solution)/shard_map/ppermute | solution.py:333
  45.6 0.0 copy-done.1
  45.6 0.0 copy-done.3
  45.6 4.7 %plane.1 = f32[64,64,128]{2,1,0:T(8,128)} custom-call(f32[64,64,128]{2,1,0:T(8,128)S(1)} %get-tuple-element.13.t_ref.refs_0_, bf16[3,64,128]{2,1,0:T(8,128)(2,1)S(1)} %get-tuple-element.23.xb_ref.refs_1_, bf16[3,64,128]{2,1,0:T(8,128)(2,1)S(1)} %get-tuple-element.22.xa_ref.refs_2_, bf16[3,80,128]{2,1,0:T(8,128)(2,1)S(1)} %get-tuple-element.19.refs_3_, ...), custom_call_target="tpu_custom_call" | custom-call | tf_op jit(solution)/shard_map/plane/pallas_call | solution.py:266
  (5 shorter events, 0.0 us)
Async XLA Ops:
  0.6 1.6 %copy-start = (f32[64,64,128]{2,1,0:T(8,128)S(1)}, f32[64,64,128]{2,1,0:T(8,128)}, u32[]{:S(2)}) copy-start(f32[64,64,128]{2,1,0:T(8,128)} %refs_5_.3) | copy-start | bytes 6291460
  2.2 1.6 %copy-start.2 = (s32[64,64,128]{2,1,0:T(8,128)S(1)}, s32[64,64,128]{2,1,0:T(8,128)}, u32[]{:S(2)}) copy-start(s32[64,64,128]{2,1,0:T(8,128)} %refs_6_.1) | copy-start | bytes 6291460
  3.8 2.2 %copy-start.4 = (bf16[4,64,64,128]{3,2,1,0:T(8,128)(2,1)S(1)}, bf16[4,64,64,128]{3,2,1,0:T(8,128)(2,1)}, u32[]{:S(2)}) copy-start(bf16[4,64,64,128]{3,2,1,0:T(8,128)(2,1)} %refs_5_.2) | copy-start | bytes 12582916
  6.0 0.7 %copy-start.5 = (f32[4,128]{1,0:T(4,128)S(1)}, f32[4,128]{1,0:T(4,128)}, u32[]{:S(2)}) copy-start(f32[4,128]{1,0:T(4,128)} %refs_2_.1) | copy-start | bytes 6148
  6.7 0.7 %copy-start.6 = (s32[4]{0:T(128)S(1)}, s32[4]{0:T(128)}, u32[]{:S(2)}) copy-start(s32[4]{0:T(128)} %refs_0_.1) | copy-start | bytes 52
  7.3 0.7 %copy-start.7 = (f32[16]{0:T(128)S(1)}, f32[16]{0:T(128)}, u32[]{:S(2)}) copy-start(f32[16]{0:T(128)} %refs_1_.1) | copy-start | bytes 196
  13.9 7.5 %collective-permute-start.2 = (f32[8,4224]{1,0:T(8,128)S(1)}, f32[8,4224]{1,0:T(8,128)S(1)}, u32[]{:S(2)}, u32[]{:S(2)}) collective-permute-start(f32[8,4224]{1,0:T(8,128)S(1)} %get-tuple-element.10.refs_1_), channel_id=1, source_target_pairs={{0,24},{8,16},{16,8},{24,0},{1,25},{9,17},{17,9},{25,1},{2,26},{10... | collective-permute-start | bytes 405512 | tf_op jit(solution)/shard_map/ppermute | solution.py:300
  18.1 11.0 %collective-permute-start.1 = (f32[8,4224]{1,0:T(8,128)S(1)}, f32[8,4224]{1,0:T(8,128)S(1)}, u32[]{:S(2)}, u32[]{:S(2)}) collective-permute-start(f32[8,4224]{1,0:T(8,128)S(1)} %get-tuple-element.10.refs_1_), channel_id=1, source_target_pairs={{0,16},{8,24},{16,0},{24,8},{1,17},{9,25},{17,1},{25,9},{2,18},{10... | collective-permute-start | bytes 405512 | tf_op jit(solution)/shard_map/ppermute | solution.py:300
  18.1 11.0 %collective-permute-start = (f32[8,4224]{1,0:T(8,128)S(1)}, f32[8,4224]{1,0:T(8,128)S(1)}, u32[]{:S(2)}, u32[]{:S(2)}) collective-permute-start(f32[8,4224]{1,0:T(8,128)S(1)} %get-tuple-element.10.refs_1_), channel_id=1, source_target_pairs={{0,8},{8,0},{16,24},{24,16},{1,9},{9,1},{17,25},{25,17},{2,10},{10... | collective-permute-start | bytes 405512 | tf_op jit(solution)/shard_map/ppermute | solution.py:300
  29.1 16.4 %copy-start.1 = (f32[64,64,128]{2,1,0:T(8,128)S(1)}, f32[64,64,128]{2,1,0:T(8,128)}, u32[]{:S(2)}) copy-start(f32[64,64,128]{2,1,0:T(8,128)} %refs_5_.3) | copy-start | bytes 6291460
  29.1 16.5 %copy-start.3 = (s32[64,64,128]{2,1,0:T(8,128)S(1)}, s32[64,64,128]{2,1,0:T(8,128)}, u32[]{:S(2)}) copy-start(s32[64,64,128]{2,1,0:T(8,128)} %refs_6_.1) | copy-start | bytes 6291460
  30.3 8.8 %collective-permute-start.3 = (bf16[3,64,128]{2,1,0:T(8,128)(2,1)S(1)}, bf16[3,64,128]{2,1,0:T(8,128)(2,1)S(1)}, u32[]{:S(2)}, u32[]{:S(2)}) collective-permute-start(bf16[3,64,128]{2,1,0:T(8,128)(2,1)S(1)} %get-tuple-element.14), channel_id=1, source_target_pairs={{0,4},{4,0},{1,5},{5,1},{2,6},{6,2},{3,7},{7,3},{8,12},{12,8},{9,1... | collective-permute-start | bytes 147464 | tf_op jit(solution)/shard_map/ppermute | solution.py:312
  31.8 2.5 %collective-permute-start.6 = (f32[4]{0:T(128)S(1)}, f32[4]{0:T(128)S(1)}, u32[]{:S(2)}, u32[]{:S(2)}) collective-permute-start(f32[4]{0:T(128)S(1)} %slice_reduce_fusion), channel_id=1, source_target_pairs={{0,4},{4,0},{1,5},{5,1},{2,6},{6,2},{3,7},{7,3},{8,12},{12,8},{9,1... | collective-permute-start | bytes 56 | tf_op jit(solution)/shard_map/ppermute | solution.py:342
  34.3 3.6 %collective-permute-start.7 = (f32[4]{0:T(128)S(1)}, f32[4]{0:T(128)S(1)}, u32[]{:S(2)}, u32[]{:S(2)}) collective-permute-start(f32[4]{0:T(128)S(1)} %add.18), channel_id=1, source_target_pairs={{0,1},{1,0},{2,3},{3,2},{4,5},{5,4},{6,7},{7,6},{8,9},{9,8},{10,11... | collective-permute-start | bytes 56 | tf_op jit(solution)/shard_map/ppermute | solution.py:342
  37.9 4.2 %collective-permute-start.8 = (f32[4]{0:T(128)S(1)}, f32[4]{0:T(128)S(1)}, u32[]{:S(2)}, u32[]{:S(2)}) collective-permute-start(f32[4]{0:T(128)S(1)} %add.19), channel_id=1, source_target_pairs={{0,2},{1,3},{2,0},{3,1},{4,6},{5,7},{6,4},{7,5},{8,10},{9,11},{10,... | collective-permute-start | bytes 56 | tf_op jit(solution)/shard_map/ppermute | solution.py:342
  39.3 3.3 %collective-permute-start.5 = (bf16[3,80,128]{2,1,0:T(8,128)(2,1)S(1)}, bf16[3,80,128]{2,1,0:T(8,128)(2,1)S(1)}, u32[]{:S(2)}, u32[]{:S(2)}) collective-permute-start(bf16[3,80,128]{2,1,0:T(8,128)(2,1)S(1)} %get-tuple-element.20), channel_id=1, source_target_pairs={{0,1},{1,0},{2,3},{3,2},{4,5},{5,4},{6,7},{7,6},{8,9},{9,8},{10,11... | collective-permute-start | bytes 184328 | tf_op jit(solution)/shard_map/ppermute | solution.py:330
  40.0 5.5 %collective-permute-start.4 = (bf16[3,80,128]{2,1,0:T(8,128)(2,1)S(1)}, bf16[3,80,128]{2,1,0:T(8,128)(2,1)S(1)}, u32[]{:S(2)}, u32[]{:S(2)}) collective-permute-start(bf16[3,80,128]{2,1,0:T(8,128)(2,1)S(1)} %get-tuple-element.21), channel_id=1, source_target_pairs={{1,2},{2,1},{5,6},{6,5},{9,10},{10,9},{13,14},{14,13},{17,18},{18,... | collective-permute-start | bytes 184328 | tf_op jit(solution)/shard_map/ppermute | solution.py:333

commit v2 on v0

v2 whole, which is shorter than its diff:
```python
import functools
import math
import jax
import jax.numpy as jnp
from jax import lax
from jax.experimental import pallas as pl
from jax.experimental.pallas import tpu as pltpu
from jax.sharding import PartitionSpec as P

RADIUS = 3
LANES = 128
MIB = 2**20
F32 = jnp.float32
BF16 = jnp.bfloat16
HIGH = lax.Precision.HIGHEST
HBM = pl.BlockSpec(memory_space=pltpu.HBM)
VMEM = pl.BlockSpec(memory_space=pltpu.VMEM)
SMEM = pl.BlockSpec(memory_space=pltpu.SMEM)


def taps_1d():
    raw = [math.exp(-2.0 * k * k / (RADIUS * RADIUS)) for k in range(-RADIUS, RADIUS + 1)]
    total = sum(raw)
    return [r / total for r in raw]


def dot_high(a, b, dims=((1,), (0,))):
    return lax.dot_general(a, b, (dims, ((), ())), precision=HIGH, preferred_element_type=F32)


def split2(v):
    hi = v.astype(BF16)
    return hi, (v - hi.astype(F32)).astype(BF16)


def split3(v):
    a = v.astype(BF16).astype(F32)
    b = (v - a).astype(BF16).astype(F32)
    return a, b, v - a - b


def put_lanes(columns):
    rows = columns[0].shape[0]
    lane = lax.broadcasted_iota(jnp.int32, (rows, LANES), 1)
    out = jnp.zeros((rows, LANES), F32)
    for k, col in enumerate(columns):
        out = jnp.where(lane == k, col, out)
    return out


def pad_rows(v, rows):
    return jnp.concatenate([v, jnp.zeros((rows - v.shape[0],) + v.shape[1:], v.dtype)], axis=0)


def sum3(block, at):
    return block[:, at : at + 1] + block[:, at + 1 : at + 2] + block[:, at + 2 : at + 3]


class Slab:
    def __init__(self, decay):
        cases, depth = decay.shape
        self.decay = decay
        self.row = lax.broadcasted_iota(jnp.int32, (depth, depth), 0)
        self.col = lax.broadcasted_iota(jnp.int32, (depth, depth), 1)
        logs = jnp.log(decay)
        self.up = dot_high(logs, (self.row <= self.col).astype(F32))
        self.up_ex = self.up - logs
        wide = lambda v: jnp.transpose(pad_rows(v, 8))
        self.up_t = wide(self.up)
        self.up_ex_t = wide(self.up_ex)
        self.keep_t = wide(1.0 - decay)
        self.total = self.up[:, depth - 1 : depth]

    def forward_t(self, c):
        gap = self.up[c : c + 1, :] - self.up_t[:, c : c + 1]
        weight = jnp.exp(jnp.minimum(gap, 0.0)) * self.keep_t[:, c : c + 1]
        return jnp.where(self.col >= self.row, weight, 0.0)

    def backward_t(self, c):
        gap = self.up_ex_t[:, c : c + 1] - self.up_ex[c : c + 1, :]
        weight = jnp.exp(jnp.minimum(gap, 0.0)) * self.keep_t[:, c : c + 1]
        return jnp.where(self.col <= self.row, weight, 0.0)


def case_scale(weight_ref, index_ref, c):
    return -3.0 * weight_ref[index_ref[c]]


def faces_kernel(shape, bx, *refs):
    cases, nx, ny, depth = shape
    (index_hbm, weight_hbm, decay_hbm, density_hbm, mask_hbm, energy_hbm,
     send_ref, own_ref, source_ref,
     index_ref, weight_ref, decay_ref, density_ref, mask_ref, energy_ref, small_sem, sem) = refs
    steps, cols = nx // bx, bx * ny
    small = [
        pltpu.make_async_copy(decay_hbm, decay_ref, small_sem.at[0]),
        pltpu.make_async_copy(index_hbm, index_ref, small_sem.at[1]),
        pltpu.make_async_copy(weight_hbm, weight_ref, small_sem.at[2]),
    ]
    big = []
    for s in range(steps):
        at = pl.ds(s * bx, bx)
        big.append([
            pltpu.make_async_copy(density_hbm.at[at], density_ref.at[at], sem.at[0, s]),
            pltpu.make_async_copy(mask_hbm.at[at], mask_ref.at[at], sem.at[1, s]),
            pltpu.make_async_copy(energy_hbm.at[:, at], energy_ref.at[:, at], sem.at[2, s]),
        ])
    for copy in small:
        copy.start()
    for group in big:
        for copy in group:
            copy.start()
    for copy in small:
        copy.wait()

    decay = decay_ref[...]
    slab = Slab(decay)
    zero_row = jnp.zeros((1, depth), F32)
    e_rows, h_rows, turns = [], [], []
    for c in range(cases):
        scale = case_scale(weight_ref, index_ref, c)
        f_t = slab.forward_t(c)
        keep = 1.0 - decay[c : c + 1, :]
        e_row = jnp.exp(slab.total[c : c + 1] - slab.up[c : c + 1, :]) * keep
        b_row = jnp.exp(slab.up_ex[c : c + 1, :]) * keep
        h_row = dot_high(b_row, f_t, ((1,), (1,)))
        turns.append(jnp.sum(b_row * jnp.exp(slab.up[c : c + 1, :]), axis=1, keepdims=True))
        place = lambda r: jnp.concatenate([zero_row] * c + [r * scale] + [zero_row] * (cases - 1 - c), axis=1)
        e_rows.append(place(e_row))
        h_rows.append(place(h_row))
    w_hi, w_lo = split2(jnp.concatenate(e_rows + h_rows, axis=0))
    wmat = jnp.concatenate([w_hi, w_lo], axis=0)

    sums = [jnp.zeros((8, depth), F32) for _ in range(cases)]
    for s in range(steps):
        for copy in big[s]:
            copy.wait()
        at = pl.ds(s * bx, bx)
        mask = mask_ref[at]
        dense = jnp.where(mask == 1, 0.001, jnp.where(mask == 2, 1.0, density_ref[at]))
        cube = dense * dense * dense
        span = pl.ds(s * cols, cols)
        for c in range(cases):
            work = cube * energy_ref[c, at].astype(F32)
            sums[c] = sums[c] + jnp.sum(work.reshape(cols // 8, 8, depth), axis=0)
            source_ref[span, c * depth : (c + 1) * depth] = work.astype(BF16).reshape(cols, depth)
        faces = lax.dot_general(
            wmat, source_ref[span, :], (((1,), (1,)), ((), ())), preferred_element_type=F32)
        faces = faces[0 : 2 * cases] + faces[2 * cases : 4 * cases]
        own_ref[:, span] = faces
        send_ref[:, span] = faces.astype(BF16)

    total = jnp.concatenate([jnp.sum(jnp.sum(v, axis=0, keepdims=True), axis=1, keepdims=True) for v in sums], axis=0)
    turn = jnp.concatenate(turns, axis=0)
    aux = put_lanes(split3(jnp.exp(slab.total)) + split3(turn) + split3(total))
    aux = pad_rows(aux, 2 * cases)
    tail = pl.ds(nx * ny, LANES)
    own_ref[:, tail] = aux
    send_ref[:, tail] = aux.astype(BF16)


def faces_call(density, design_mask, energy, decay, case_index, case_weight):
    cases, nx, ny, depth = energy.shape
    bx = 8
    width = nx * ny + LANES
    return pl.pallas_call(
        functools.partial(faces_kernel, energy.shape, bx),
        in_specs=[HBM] * 6,
        out_specs=[VMEM] * 3,
        out_shape=[
            jax.ShapeDtypeStruct((2 * cases, width), BF16),
            jax.ShapeDtypeStruct((2 * cases, width), F32),
            jax.ShapeDtypeStruct((nx * ny, cases * depth), BF16),
        ],
        scratch_shapes=[
            pltpu.SMEM(case_index.shape, case_index.dtype),
            pltpu.SMEM(case_weight.shape, F32),
            pltpu.VMEM(decay.shape, F32),
            pltpu.VMEM(density.shape, F32),
            pltpu.VMEM(density.shape, jnp.int32),
            pltpu.VMEM(energy.shape, BF16),
            pltpu.SemaphoreType.DMA((3,)),
            pltpu.SemaphoreType.DMA((3, nx // bx)),
        ],
        compiler_params=pltpu.CompilerParams(vmem_limit_bytes=20 * MIB),
        name="faces",
    )(case_index, case_weight, decay, density, design_mask, energy)


def local_kernel(shape, bx, *refs):
    cases, nx, ny, depth = shape
    (index_hbm, weight_hbm, decay_hbm, density_hbm, mask_hbm, source_ref,
     t_ref, factor_ref, umap_ref,
     index_ref, weight_ref, decay_ref, mask_ref, rmat, small_sem, sem) = refs
    steps, cols = nx // bx, bx * ny
    small = [
        pltpu.make_async_copy(decay_hbm, decay_ref, small_sem.at[0]),
        pltpu.make_async_copy(index_hbm, index_ref, small_sem.at[1]),
        pltpu.make_async_copy(weight_hbm, weight_ref, small_sem.at[2]),
    ]
    big = [
        pltpu.make_async_copy(density_hbm, factor_ref, sem.at[0]),
        pltpu.make_async_copy(mask_hbm, mask_ref, sem.at[1]),
    ]
    for copy in small + big:
        copy.start()
    for copy in small:
        copy.wait()
    slab = Slab(decay_ref[...])
    a_rows, c_rows = [], []
    for c in range(cases):
        f_t, b_t = slab.forward_t(c), slab.backward_t(c)
        hi, lo = split2(dot_high(f_t, b_t) * case_scale(weight_ref, index_ref, c))
        rmat[c * depth : (c + 1) * depth, 0:depth] = hi
        rmat[c * depth : (c + 1) * depth, depth : 2 * depth] = lo
        a_rows.append(dot_high(jnp.exp(slab.up[c : c + 1, :]), b_t))
        c_rows.append(jnp.exp(slab.total[c : c + 1] - slab.up_ex[c : c + 1, :]))
    u_all = jnp.concatenate(a_rows + c_rows, axis=0)
    u_hi = u_all.astype(BF16).astype(F32)
    umap_ref[...] = jnp.concatenate([u_hi, u_hi, u_all - u_hi, jnp.zeros_like(u_hi)], axis=0).astype(BF16)
    for copy in big:
        copy.wait()

    def one(s, carry):
        span = pl.ds(pl.multiple_of(s * cols, cols), cols)
        both = lax.dot_general(
            source_ref[span, :], rmat[...], (((1,), (0,)), ((), ())), preferred_element_type=F32)
        at = pl.ds(s * bx, bx)
        t_ref[at] = (both[:, 0:depth] + both[:, depth : 2 * depth]).reshape(bx, ny, depth)
        factor_ref[at] = jnp.where(mask_ref[at] == 0, 1.0 / jnp.maximum(factor_ref[at], 0.1), 0.0)
        return carry

    lax.fori_loop(0, steps, one, 0)


def local_call(density, design_mask, source, decay, case_index, case_weight):
    nx, ny, depth = density.shape
    cases = decay.shape[0]
    return pl.pallas_call(
        functools.partial(local_kernel, (cases, nx, ny, depth), 8),
        in_specs=[HBM] * 5 + [VMEM],
        out_specs=[VMEM] * 3,
        out_shape=[
            jax.ShapeDtypeStruct(density.shape, F32),
            jax.ShapeDtypeStruct(density.shape, F32),
            jax.ShapeDtypeStruct((8 * cases, depth), BF16),
        ],
        scratch_shapes=[
            pltpu.SMEM(case_index.shape, case_index.dtype),
            pltpu.SMEM(case_weight.shape, F32),
            pltpu.VMEM(decay.shape, F32),
            pltpu.VMEM(density.shape, jnp.int32),
            pltpu.VMEM((cases * depth, 2 * depth), BF16),
            pltpu.SemaphoreType.DMA((3,)),
            pltpu.SemaphoreType.DMA((2,)),
        ],
        compiler_params=pltpu.CompilerParams(vmem_limit_bytes=20 * MIB),
        name="local",
    )(case_index, case_weight, decay, density, design_mask, source)


def couple_kernel(shape, nslabs, nsends, *refs):
    cases, nx, ny, depth = shape
    slot_ref, own_ref = refs[0:2]
    msgs = refs[2 : 1 + nslabs]
    t_ref, umap_ref, out_ref = refs[1 + nslabs : 4 + nslabs]
    sends = refs[4 + nslabs : 4 + nslabs + nsends]
    stack = refs[-1]
    cols = nx * ny
    mine = slot_ref[0]
    stack[0] = own_ref[...]
    for m, msg in enumerate(msgs):
        stack[m + 1] = msg[...].astype(F32)
    total = jnp.zeros((cases, 1), F32)
    for m in range(nslabs):
        total = total + sum3(stack[m, 0:cases, cols : cols + LANES], 6)
    state = jnp.zeros((cases, cols), F32)
    entering, above = state, state
    tops, gains = [], []
    for j in range(nslabs):
        at = slot_ref[2 + j]
        aux = stack[at, 0:cases, cols : cols + LANES]
        gains.append(sum3(aux, 0))
        entering = jnp.where(mine == j, state, entering)
        tops.append(stack[at, cases : 2 * cases, 0:cols] + sum3(aux, 3) * state)
        state = gains[j] * state + stack[at, 0:cases, 0:cols]
    state = jnp.zeros((cases, cols), F32)
    for j in reversed(range(nslabs)):
        above = jnp.where(mine == j, state, above)
        state = tops[j] + gains[j] * state
    faces = jnp.concatenate([entering, above], axis=0)
    hi = faces.astype(BF16).astype(F32)
    lhs = jnp.concatenate([hi, faces - hi, hi, jnp.zeros_like(hi)], axis=0).astype(BF16)
    add = lax.dot_general(lhs, umap_ref[...], (((0,), (0,)), ((), ())), preferred_element_type=F32)
    out_ref[...] = t_ref[...] + add.reshape(nx, ny, depth)
    aux = pad_rows(put_lanes(split3(total)), 16).astype(BF16)
    for k, ref in enumerate(sends):
        edge = out_ref[pl.ds(slot_ref[1] if k == 0 else nx - RADIUS - slot_ref[1], RADIUS)]
        ref[0 : RADIUS * ny, :] = edge.reshape(RADIUS * ny, depth).astype(BF16)
        ref[RADIUS * ny :, :] = aux


def couple_call(slots, own, msgs, t_local, umap, nsends):
    nx, ny, depth = t_local.shape
    cases = own.shape[0] // 2
    nslabs = len(msgs) + 1
    return pl.pallas_call(
        functools.partial(couple_kernel, (cases, nx, ny, depth), nslabs, nsends),
        in_specs=[SMEM] + [VMEM] * (nslabs + 2),
        out_specs=[VMEM] * (1 + nsends),
        out_shape=[jax.ShapeDtypeStruct(t_local.shape, F32)]
        + [jax.ShapeDtypeStruct((RADIUS * ny + 16, depth), BF16)] * nsends,
        scratch_shapes=[pltpu.VMEM((nslabs,) + own.shape, F32)],
        compiler_params=pltpu.CompilerParams(vmem_limit_bytes=28 * MIB),
        name="couple",
    )(slots, own, *msgs, t_local, umap)


def sided(even, got):
    a = got[0]
    b = got[1] if len(got) > 1 else jnp.zeros_like(a)
    return jnp.where(even, b, a), jnp.where(even, a, b)


def edge_kernel(shape, nx_sends, ny_sends, *refs):
    cases, nx, ny, depth = shape
    slot_ref, t_ref = refs[0:2]
    got_refs = refs[2 : 2 + nx_sends]
    own_send = refs[2 + nx_sends]
    sends = refs[3 + nx_sends : 3 + nx_sends + ny_sends]
    xb_ref, xa_ref, sums_ref, line = refs[3 + nx_sends + ny_sends :]
    taps = taps_1d()
    edge = RADIUS * ny
    even_x = slot_ref[2] == 0
    flip_y = slot_ref[3] == 1
    blocks = [r[0:edge, :].astype(F32) for r in got_refs]
    before, after = sided(even_x, blocks)
    xb_ref[...] = before
    xa_ref[...] = after
    total = sum3(own_send[edge : edge + 16, :].astype(F32), 0)
    for ref in got_refs:
        total = total + sum3(ref[edge : edge + 16, :].astype(F32), 0)
    sums_ref[...] = jnp.broadcast_to(total[0:8], (8, LANES))
    aux = put_lanes(split3(total)).astype(BF16)
    flat = t_ref.reshape(nx * ny, depth)
    columns = []
    for k in range(2 * RADIUS):
        y = k if k < RADIUS else ny - 2 * RADIUS + k
        line[8 : 8 + nx, :] = flat[pl.ds(y, nx, stride=ny), :]
        line[8 - RADIUS : 8, :] = xb_ref[pl.ds(y, RADIUS, stride=ny), :]
        line[8 + nx : 8 + nx + RADIUS, :] = xa_ref[pl.ds(y, RADIUS, stride=ny), :]
        acc = taps[RADIUS] * line[8 : 8 + nx, :]
        for d in range(1, RADIUS + 1):
            acc = acc + taps[RADIUS + d] * (line[8 - d : 8 - d + nx, :] + line[8 + d : 8 + d + nx, :])
        columns.append(acc)
    for m, ref in enumerate(sends):
        for k in range(RADIUS):
            first, last = columns[k], columns[RADIUS + k]
            pick = jnp.where(flip_y == (m == 0), first, last)
            ref[k * nx : (k + 1) * nx, :] = pick.astype(BF16)
        ref[RADIUS * nx :, :] = aux


def edge_call(slots, t, got, own_send, ny_sends, cases):
    nx, ny, depth = t.shape
    return pl.pallas_call(
        functools.partial(edge_kernel, (cases, nx, ny, depth), len(got), ny_sends),
        in_specs=[SMEM] + [VMEM] * (2 + len(got)),
        out_specs=[VMEM] * (ny_sends + 3),
        out_shape=[jax.ShapeDtypeStruct((RADIUS * nx + 16, depth), BF16)] * ny_sends
        + [jax.ShapeDtypeStruct((RADIUS * ny, depth), F32)] * 2
        + [jax.ShapeDtypeStruct((8, LANES), F32)],
        scratch_shapes=[pltpu.VMEM((nx + 16, depth), F32)],
        compiler_params=pltpu.CompilerParams(vmem_limit_bytes=16 * MIB),
        name="edge",
    )(slots, t, *got, own_send)


def plane_kernel(shape, bx, *refs):
    nx, ny, depth = shape
    (t_ref, xb_ref, xa_ref, factor_ref, out_hbm, first_ref, last_ref,
     pad, line, out_ref, sem) = refs
    taps = taps_1d()
    steps = nx // bx
    pad[0:RADIUS] = xb_ref[...].reshape(RADIUS, ny, depth)
    pad[RADIUS : 2 * RADIUS] = t_ref[0:RADIUS]
    pad[2 * RADIUS : 3 * RADIUS] = t_ref[RADIUS : 2 * RADIUS]
    tail = 3 * RADIUS
    pad[tail : tail + 2 * RADIUS] = t_ref[nx - 2 * RADIUS : nx]
    pad[tail + 2 * RADIUS :] = xa_ref[...].reshape(RADIUS, ny, depth)
    zeros = jnp.zeros((8, depth), F32)
    for slot in range(2):
        line[slot, 0:8, :] = zeros
        line[slot, 8 + ny :, :] = zeros

    def row(ref, x, at, slot):
        acc = taps[RADIUS] * ref[at]
        for d in range(1, RADIUS + 1):
            acc = acc + taps[RADIUS + d] * (ref[at - d] + ref[at + d])
        line[slot, 8 : 8 + ny, :] = acc
        res = taps[RADIUS] * acc
        for d in range(1, RADIUS + 1):
            res = res + taps[RADIUS + d] * (line[slot, 8 - d : 8 - d + ny, :] + line[slot, 8 + d : 8 + d + ny, :])
        res = res * factor_ref[x]
        out_ref[x] = res
        first_ref[x] = res[0:8]
        last_ref[x] = res[ny - 8 : ny]

    copies = [
        pltpu.make_async_copy(out_ref.at[pl.ds(s * bx, bx)], out_hbm.at[pl.ds(s * bx, bx)], sem.at[s])
        for s in range(steps)
    ]
    for s in range(steps):
        lo, hi = s * bx, (s + 1) * bx
        if s == 0:
            for x in range(RADIUS):
                row(pad, x, x + RADIUS, x % 2)
            lo = RADIUS
        if s == steps - 1:
            for x in range(nx - RADIUS, nx):
                row(pad, x, x - (nx - RADIUS) + tail + RADIUS, x % 2)
            hi = nx - RADIUS

        def pair(i, carry):
            row(t_ref, i, i, i % 2)
            return carry

        lax.fori_loop(lo, hi, pair, 0)
        copies[s].start()
    for copy in copies:
        copy.wait()


def plane_call(t, xb, xa, factor):
    nx, ny, depth = t.shape
    bx = 8
    return pl.pallas_call(
        functools.partial(plane_kernel, t.shape, bx),
        in_specs=[VMEM] * 4,
        out_specs=[HBM, VMEM, VMEM],
        out_shape=[
            jax.ShapeDtypeStruct(t.shape, F32),
            jax.ShapeDtypeStruct((nx, 8, depth), F32),
            jax.ShapeDtypeStruct((nx, 8, depth), F32),
        ],
        scratch_shapes=[
            pltpu.VMEM((7 * RADIUS - RADIUS, ny, depth), F32),
            pltpu.VMEM((2, ny + 16, depth), F32),
            pltpu.VMEM(t.shape, F32),
            pltpu.SemaphoreType.DMA((nx // bx,)),
        ],
        compiler_params=pltpu.CompilerParams(vmem_limit_bytes=20 * MIB),
        name="plane",
    )(t, xb, xa, factor)


def finish_kernel(shape, cells, ngot, nextra, cases, *refs):
    nx, ny, depth = shape
    slot_ref = refs[0]
    got_refs = refs[1 : 1 + ngot]
    sums_ref = refs[1 + ngot]
    extra_refs = refs[2 + ngot : 2 + ngot + nextra]
    first_ref, last_ref, factor_ref, _, out_hbm, comp_ref, strip, sem = refs[2 + ngot + nextra :]
    taps = taps_1d()
    edge = RADIUS * nx
    even_y = slot_ref[3] == 0
    blocks = [r[0:edge, :].astype(F32) for r in got_refs]
    before, after = sided(even_y, blocks) if blocks else (jnp.zeros((edge, depth), F32),) * 2
    flat = factor_ref.reshape(nx * ny, depth)
    for ref, side in ((first_ref, 0), (last_ref, 1)):
        strip[side] = ref[...]
        view = strip.at[side].reshape(nx * 8, depth)
        for y in range(RADIUS):
            add = jnp.zeros((nx, depth), F32)
            for k in range(RADIUS):
                if side == 0:
                    d, halo, own = y + RADIUS - k, before[k * nx : (k + 1) * nx], y
                else:
                    d, halo, own = k + 1 + RADIUS - 1 - y, after[k * nx : (k + 1) * nx], ny - RADIUS + y
                if d <= RADIUS:
                    add = add + taps[RADIUS + d] * halo
            at = own if side == 0 else own - (ny - 8)
            view[pl.ds(at, nx, stride=8), :] += flat[pl.ds(own, nx, stride=ny), :] * add
    copies = [
        pltpu.make_async_copy(strip.at[0], out_hbm.at[:, 0:8, :], sem.at[0]),
        pltpu.make_async_copy(strip.at[1], out_hbm.at[:, ny - 8 : ny, :], sem.at[1]),
    ]
    for copy in copies:
        copy.start()
    total = sums_ref[...]
    for ref in extra_refs:
        total = total + ref[...]
    for c in range(cases):
        comp_ref[c] = total[c, 0] / cells
    for copy in copies:
        copy.wait()


def finish_call(slots, got, sums, extra, first, last, factor, out, cells, cases):
    nx, ny, depth = out.shape
    nin = 1 + len(got) + 1 + len(extra)
    return pl.pallas_call(
        functools.partial(finish_kernel, out.shape, cells, len(got), len(extra), cases),
        in_specs=[SMEM] + [VMEM] * (nin - 1 + 3) + [HBM],
        out_specs=[HBM, SMEM],
        out_shape=[jax.ShapeDtypeStruct(out.shape, F32), jax.ShapeDtypeStruct((cases,), F32)],
        input_output_aliases={nin + 3: 0},
        scratch_shapes=[pltpu.VMEM((2, nx, 8, depth), F32), pltpu.SemaphoreType.DMA((2,))],
        compiler_params=pltpu.CompilerParams(vmem_limit_bytes=16 * MIB),
        name="finish",
    )(slots, *got, sums, *extra, first, last, factor, out)


def swap_pairs(count, first):
    return [q for i in range(first, count - 1, 2) for q in ((i, i + 1), (i + 1, i))]


def swaps_of(count):
    return min(count - 1, 2)


def xor_pairs(count, m):
    return [(i, i ^ m) for i in range(count)]


def shards(density, design_mask, energy, decay, case_index, case_weight):
    cases = energy.shape[0]
    nx, ny, depth = density.shape
    nz, gx, gy = (lax.axis_size(a) for a in ("gz", "gx", "gy"))
    iz, ix, iy = (lax.axis_index(a) for a in ("gz", "gx", "gy"))
    send, own, source = faces_call(density, design_mask, energy, decay, case_index, case_weight)
    if nz in (1, 2, 4):
        msgs = [lax.ppermute(send, "gz", xor_pairs(nz, m)) for m in range(1, nz)]
        order = [iz ^ j for j in range(nz)]
    else:
        every = lax.all_gather(send, "gz")
        msgs = [every[j] for j in range(nz)]
        order = [jnp.int32(j) for j in range(nz)]
    t_local, factor, umap = local_call(density, design_mask, source, decay, case_index, case_weight)
    flip_x, flip_y = ix % 2, iy % 2
    slots = jnp.stack([iz, (1 - flip_x) * (nx - RADIUS)] + order).astype(jnp.int32)
    if nz not in (1, 2, 4):
        own, msgs = msgs[0].astype(F32), msgs[1:]
    t, *x_sends = couple_call(slots, own, msgs, t_local, umap, max(swaps_of(gx), 1))
    x_got = [lax.ppermute(x_sends[k], "gx", swap_pairs(gx, k)) for k in range(swaps_of(gx))]
    marks = jnp.stack([iz, ix, flip_x, flip_y]).astype(jnp.int32)
    *y_sends, xb, xa, sums = edge_call(marks, t, x_got, x_sends[0], swaps_of(gy), cases)
    y_got = [lax.ppermute(y_sends[k], "gy", swap_pairs(gy, k)) for k in range(swaps_of(gy))]
    extra = [lax.ppermute(sums, "gy", xor_pairs(gy, m)) for m in range(1, gy)]
    partial, first, last = plane_call(t, xb, xa, factor)
    cells = nx * ny * depth * nz * gx * gy
    return tuple(finish_call(marks, y_got, sums, extra, first, last, factor, partial, float(cells), cases))


def solution(mesh):
    placed = (
        P("gx", "gy", "gz"),
        P("gx", "gy", "gz"),
        P(None, "gx", "gy", "gz"),
        P(None, "gz"),
        P(),
        P(),
    )
    return jax.shard_map(
        shards, mesh=mesh, in_specs=placed, out_specs=(P("gx", "gy", "gz"), P()), check_vma=False
    )
```

time: 232 us -> 50.2 us (0.22)
  other arithmetic: 86 us -> 0.08 us
  blocking collectives: 82.4 us -> 0 us
  matrix products: 19.7 us -> 0 us
  Pallas kernels: 0 us -> 16.2 us
  local copies, waits for them, and re-layouts: 24.7 us -> 17.4 us
  waiting for transfers between devices: 5.3 us -> 1.72 us
    psum x1 -> x0, blocking collectives: 45.9 us -> none  [shards(): totals = lax.psum(partial_sums, ('gz', 'gx', 'gy'))]
    reduce_sum x4 -> x0, other arithmetic: 30.6 us -> none  [the longest x1 28.3 us: shards(): combined = jnp.sum(weights[:, None, None, None] * filtered, axis=0)]
    add x1 -> x0, other arithmetic: 30.3 us -> none  [planar_filter(): along_x = along_x + taps[offset] * padded[:, offset:offset + width_x]]
    all_gather x2 -> x0, blocking collectives: 25.8 us -> none  [entering_2(): pieces = jax.tree.map(lambda part: lax.all_gather(part, axis), value)]
    dot_general x2 -> x0, matrix products: 19.7 us -> none  [the longest x1 11.1 us: slab_smooth(): jnp.einsum('cxyj,cij->cxyi', forward, backward_map, precision=lax.Precisi...]
    slice x7 -> x0, local copies, waits for them, and re-layouts: 17.2 us -> none  [the longest x2 10.8 us: slab_smooth(): local_forward[..., -1]]
    pallas_call x0 -> x6, Pallas kernels: none -> 16.2 us  [the longest x1 4.94 us: faces_call(): pl.pallas_call(functools.partial(faces_kernel, energy.shape, bx), in_spec...]
    convert_element_type x2 -> x0, other arithmetic: 14.4 us -> none  [the longest x1 8.41 us: shards(): with_halo(along_z.astype(jnp.bfloat16), (('gx', 1), ('gy', 2)), RADIUS)]
  transfers between devices with their start and end apart: 4 -> 9, of which waited for: 2 -> 1; matrix products, arithmetic and copies ran while one was open for 2% -> 0% of each run, Pallas kernels for 0% -> 14%
where the time goes in v2:
time: 50.2 us; the launch traced here: 49.8 us
  local copies, waits for them, and re-layouts  17.4 us (35%)
  Pallas kernels  16.2 us (32%)
  starting transfers between devices  13.6 us (27%)
  waiting for transfers between devices  1.72 us (3%)
  between operations  0.81 us (2%)
    unnamed x34, local copies, waits for them, and re-layouts  17.3 us
    ppermute x2, starting transfers between devices, shards(): lax.ppermute(y_sends[k], 'gy', swap_pairs(gy, k))  5.7 us
    pallas_call x1, Pallas kernels, faces_call(): pl.pallas_call(functools.partial(faces_kernel, energy.shape, bx), in_spec...  4.94 us
    ppermute x3, starting transfers between devices, shards(): msgs = [lax.ppermute(send, 'gz', xor_pairs(nz, m)) for m in range(1, nz)]  4.43 us
    pallas_call x1, Pallas kernels, local_call(): pl.pallas_call(functools.partial(local_kernel, (cases, nx, ny, depth), 8)...  3.96 us
    pallas_call x1, Pallas kernels, plane_call(): pl.pallas_call(functools.partial(plane_kernel, t.shape, bx), in_specs=[VM...  3.05 us
    ppermute x3, starting transfers between devices, shards(): extra = [lax.ppermute(sums, 'gy', xor_pairs(gy, m)) for m in range(1, gy)]  2.2 us
    pallas_call x1, Pallas kernels, finish_call(): pl.pallas_call(functools.partial(finish_kernel, out.shape, cells, len(got...  2.17 us
  transfers between devices with their start and end apart: 9, of which 1 were waited for; matrix products, arithmetic and copies ran while one was open for 0% of the time, Pallas kernels for 14%

profile of v2, /device:TPU:1, one launch (start us, length us, event | category | flops | bytes accessed | tf_op | source)
XLA Modules:
  0.0 49.8 jit_solution(4196336543930747206)
XLA Ops:
  0.6 0.0 copy-start
  0.6 1.6 %copy-done = f32[64,64,128]{2,1,0:T(8,128)S(1)} copy-done((f32[64,64,128]{2,1,0:T(8,128)S(1)}, f32[64,64,128]{2,1,0:T(8,128)}, u32[]{:S(2)}) %copy-start) | copy-done | bytes 2097176
  2.2 0.0 copy-start.2
  2.2 1.6 %copy-done.2 = s32[64,64,128]{2,1,0:T(8,128)S(1)} copy-done((s32[64,64,128]{2,1,0:T(8,128)S(1)}, s32[64,64,128]{2,1,0:T(8,128)}, u32[]{:S(2)}) %copy-start.2) | copy-done | bytes 2097176
  3.8 0.0 copy-start.6
  3.8 2.2 %copy-done.6 = bf16[4,64,64,128]{3,2,1,0:T(8,128)(2,1)S(1)} copy-done((bf16[4,64,64,128]{3,2,1,0:T(8,128)(2,1)S(1)}, bf16[4,64,64,128]{3,2,1,0:T(8,128)(2,1)}, u32[]{:S(2)}) %copy-start.6) | copy-done | bytes 4194328
  6.0 0.0 copy-start.11
  6.0 0.7 %copy-done.11 = f32[4,128]{1,0:T(4,128)S(1)} copy-done((f32[4,128]{1,0:T(4,128)S(1)}, f32[4,128]{1,0:T(4,128)}, u32[]{:S(2)}) %copy-start.11) | copy-done | bytes 2072
  6.7 0.0 copy-start.13
  6.7 0.7 %copy-done.13 = s32[4]{0:T(128)S(1)} copy-done((s32[4]{0:T(128)S(1)}, s32[4]{0:T(128)}, u32[]{:S(2)}) %copy-start.13) | copy-done | bytes 40
  7.3 0.0 copy-start.15
  7.3 0.7 %copy-done.15 = f32[16]{0:T(128)S(1)} copy-done((f32[16]{0:T(128)S(1)}, f32[16]{0:T(128)}, u32[]{:S(2)}) %copy-start.15) | copy-done | bytes 88
  8.0 0.0 copy-start.1
  8.0 0.0 copy-start.12
  8.0 0.0 copy-start.14
  8.0 0.0 copy-start.16
  8.0 4.9 %faces.1 = (bf16[8,4224]{1,0:T(8,128)(2,1)S(1)}, f32[8,4224]{1,0:T(8,128)S(1)}, bf16[4096,512]{1,0:T(8,128)(2,1)S(1)}) custom-call(s32[4]{0:T(128)S(1)} %copy-done.13, f32[16]{0:T(128)S(1)} %copy-done.15, f32[4,128]{1,0:T(4,128)S(1)} %copy-done.11, f32[64,64,128]{2,1,0:T(8,128)S(1)} %copy-done, s32[64,64,128]{2,1,0:T(8,128)S(1)} %copy-done.2, ...), custom_call_target="tpu_custom_call" | custom-call | tf_op jit(solution)/shard_map/faces/pallas_call | solution.py:166
  13.0 0.0 copy-start.7
  13.0 1.9 %copy-done.7 = bf16[4096,512]{1,0:T(8,128)(2,1)} copy-done((bf16[4096,512]{1,0:T(8,128)(2,1)}, bf16[4096,512]{1,0:T(8,128)(2,1)S(1)}, u32[]{:S(2)}) %copy-start.7) | copy-done | bytes 4194328
  14.9 2.1 %collective-permute-start = (bf16[8,4224]{1,0:T(8,128)(2,1)S(1)}, bf16[8,4224]{1,0:T(8,128)(2,1)S(1)}, u32[]{:S(2)}, u32[]{:S(2)}) collective-permute-start(bf16[8,4224]{1,0:T(8,128)(2,1)S(1)} %get-tuple-element.19), channel_id=1, source_target_pairs={{0,8},{8,0},{16,24},{24,16},{1,9},{9,1},{17,25},{25,17},{2,10},{10... | collective-permute-start | bytes 202760 | tf_op jit(solution)/shard_map/ppermute | solution.py:533
  17.0 2.3 %collective-permute-start.1 = (bf16[8,4224]{1,0:T(8,128)(2,1)S(1)}, bf16[8,4224]{1,0:T(8,128)(2,1)S(1)}, u32[]{:S(2)}, u32[]{:S(2)}) collective-permute-start(bf16[8,4224]{1,0:T(8,128)(2,1)S(1)} %get-tuple-element.19), channel_id=1, source_target_pairs={{0,16},{8,24},{16,0},{24,8},{1,17},{9,25},{17,1},{25,9},{2,18},{10... | collective-permute-start | bytes 202760 | tf_op jit(solution)/shard_map/ppermute | solution.py:533
  19.3 0.0 collective-permute-start.2
  19.3 0.0 copy-done.1
  19.3 0.0 copy-done.12
  19.4 0.0 copy-done.14
  19.4 0.0 copy-done.16
  19.4 0.0 copy-start.3
  19.4 1.6 %copy-done.3 = s32[64,64,128]{2,1,0:T(8,128)S(1)} copy-done((s32[64,64,128]{2,1,0:T(8,128)S(1)}, s32[64,64,128]{2,1,0:T(8,128)}, u32[]{:S(2)}) %copy-start.3) | copy-done | bytes 2097176
  21.0 0.0 copy-start.8
  21.0 2.2 %copy-done.8 = bf16[4096,512]{1,0:T(8,128)(2,1)S(1)} copy-done((bf16[4096,512]{1,0:T(8,128)(2,1)S(1)}, bf16[4096,512]{1,0:T(8,128)(2,1)}, u32[]{:S(2)}) %copy-start.8) | copy-done | bytes 4194328
  23.2 4.0 %local.1 = (f32[64,64,128]{2,1,0:T(8,128)S(1)}, f32[64,64,128]{2,1,0:T(8,128)S(1)}, bf16[32,128]{1,0:T(8,128)(2,1)S(1)}) custom-call(s32[4]{0:T(128)S(1)} %copy-done.14, f32[16]{0:T(128)S(1)} %copy-done.16, f32[4,128]{1,0:T(4,128)S(1)} %copy-done.12, f32[64,64,128]{2,1,0:T(8,128)S(1)} %copy-done.1, s32[64,64,128]{2,1,0:T(8,128)S(1)} %copy-done.3, ...), custom_call_target="tpu_custom_call" | custom-call | tf_op jit(solution)/shard_map/local/pallas_call | solution.py:239
  27.1 0.0 copy-start.4
  27.1 1.3 %copy-done.4 = f32[64,64,128]{2,1,0:T(8,128)} copy-done((f32[64,64,128]{2,1,0:T(8,128)}, f32[64,64,128]{2,1,0:T(8,128)S(1)}, u32[]{:S(2)}) %copy-start.4) | copy-done | bytes 2097176
  28.5 0.0 copy-start.9
  28.5 1.3 %copy-done.9 = f32[64,64,128]{2,1,0:T(8,128)} copy-done((f32[64,64,128]{2,1,0:T(8,128)}, f32[64,64,128]{2,1,0:T(8,128)S(1)}, u32[]{:S(2)}) %copy-start.9) | copy-done | bytes 2097176
  29.8 0.1 stack.41.refs_0_
  29.9 0.0 collective-permute-done.refs_2_
  29.9 0.0 collective-permute-done.1.refs_3_
  29.9 0.0 collective-permute-done.2.refs_4_
  29.9 0.0 copy-start.10
  29.9 1.6 %copy-done.10 = f32[64,64,128]{2,1,0:T(8,128)S(1)} copy-done((f32[64,64,128]{2,1,0:T(8,128)S(1)}, f32[64,64,128]{2,1,0:T(8,128)}, u32[]{:S(2)}) %copy-start.10) | copy-done | bytes 2097176
  31.5 0.0 copy-start.5
  31.5 1.2 %couple.1 = (f32[64,64,128]{2,1,0:T(8,128)S(1)}, bf16[208,128]{1,0:T(8,128)(2,1)S(1)}) custom-call(s32[6]{0:T(128)S(1)} %stack.41.refs_0_, f32[8,4224]{1,0:T(8,128)S(1)} %get-tuple-element.18.refs_1_, bf16[8,4224]{1,0:T(8,128)(2,1)S(1)} %collective-permute-done.refs_2_, bf16[8,4224]{1,0:T(8,128)(2,1)S(1)} %collective-permute-done.1.refs_3_, ...), custom_call_target="tpu_custom_call" | custom-call | tf_op jit(solution)/shard_map/couple/pallas_call | solution.py:307
  32.7 1.3 %collective-permute-start.3 = (bf16[208,128]{1,0:T(8,128)(2,1)S(1)}, bf16[208,128]{1,0:T(8,128)(2,1)S(1)}, u32[]{:S(2)}, u32[]{:S(2)}) collective-permute-start(bf16[208,128]{1,0:T(8,128)(2,1)S(1)} %get-tuple-element.24.refs_3_), channel_id=1, source_target_pairs={{0,4},{4,0},{1,5},{5,1},{2,6},{6,2},{3,7},{7,3},{8,12},{12,8},{9,1... | collective-permute-start | bytes 159752 | tf_op jit(solution)/shard_map/ppermute | solution.py:545
  34.0 0.1 pad_add_fusion.refs_0_
  34.1 1.7 %collective-permute-done.3.refs_2_ = bf16[208,128]{1,0:T(8,128)(2,1)S(1)} collective-permute-done((bf16[208,128]{1,0:T(8,128)(2,1)S(1)}, bf16[208,128]{1,0:T(8,128)(2,1)S(1)}, u32[]{:S(2)}, u32[]{:S(2)}) %collective-permute-start.3) | collective-permute-done | bytes 53280 | tf_op jit(solution)/shard_map/ppermute | solution.py:545
  35.8 0.9 %edge.1 = (bf16[208,128]{1,0:T(8,128)(2,1)S(1)}, bf16[208,128]{1,0:T(8,128)(2,1)S(1)}, f32[192,128]{1,0:T(8,128)S(1)}, f32[192,128]{1,0:T(8,128)S(1)}, f32[8,128]{1,0:T(8,128)S(1)}) custom-call(s32[4]{0:T(128)S(1)} %pad_add_fusion.refs_0_, f32[64,64,128]{2,1,0:T(8,128)S(1)} %get-tuple-element.23.refs_1_.refs_0_, ...), custom_call_target="tpu_custom_call" | custom-call | tf_op jit(solution)/shard_map/edge/pallas_call | solution.py:366
  36.6 2.4 %collective-permute-start.4 = (bf16[208,128]{1,0:T(8,128)(2,1)S(1)}, bf16[208,128]{1,0:T(8,128)(2,1)S(1)}, u32[]{:S(2)}, u32[]{:S(2)}) collective-permute-start(bf16[208,128]{1,0:T(8,128)(2,1)S(1)} %get-tuple-element.25), channel_id=1, source_target_pairs={{0,1},{1,0},{2,3},{3,2},{4,5},{5,4},{6,7},{7,6},{8,9},{9,8},{10,11... | collective-permute-start | bytes 159752 | tf_op jit(solution)/shard_map/ppermute | solution.py:548
  39.1 3.3 %collective-permute-start.5 = (bf16[208,128]{1,0:T(8,128)(2,1)S(1)}, bf16[208,128]{1,0:T(8,128)(2,1)S(1)}, u32[]{:S(2)}, u32[]{:S(2)}) collective-permute-start(bf16[208,128]{1,0:T(8,128)(2,1)S(1)} %get-tuple-element.26), channel_id=1, source_target_pairs={{1,2},{2,1},{5,6},{6,5},{9,10},{10,9},{13,14},{14,13},{17,18},{18,... | collective-permute-start | bytes 159752 | tf_op jit(solution)/shard_map/ppermute | solution.py:548
  42.4 0.1 collective-permute-start.6
  42.4 0.5 collective-permute-start.7
  42.9 1.6 %collective-permute-start.8 = (f32[8,128]{1,0:T(8,128)S(1)}, f32[8,128]{1,0:T(8,128)S(1)}, u32[]{:S(2)}, u32[]{:S(2)}) collective-permute-start(f32[8,128]{1,0:T(8,128)S(1)} %get-tuple-element.27.refs_3_), channel_id=1, source_target_pairs={{0,3},{1,2},{2,1},{3,0},{4,7},{5,6},{6,5},{7,4},{8,11},{9,10},{10,... | collective-permute-start | bytes 12296 | tf_op jit(solution)/shard_map/ppermute | solution.py:549
  44.6 0.0 copy-done.5
  44.6 3.1 %plane.1 = (f32[64,64,128]{2,1,0:T(8,128)}, f32[64,8,128]{2,1,0:T(8,128)S(1)}, f32[64,8,128]{2,1,0:T(8,128)S(1)}) custom-call(f32[64,64,128]{2,1,0:T(8,128)S(1)} %get-tuple-element.23.refs_1_.refs_0_, f32[192,128]{1,0:T(8,128)S(1)} %get-tuple-element.28.refs_1_, f32[192,128]{1,0:T(8,128)S(1)} %get-tuple-element.29.refs_2_, f32[64,64,128]{2,1,0:T(8,128)S(1)} %copy-done.5), custom_call_target="tpu_custom_call" | custom-call | tf_op jit(solution)/shard_map/plane/pallas_call | solution.py:437
  47.6 0.0 collective-permute-done.6.refs_4_
  47.6 0.0 collective-permute-done.7.refs_5_
  47.7 0.0 collective-permute-done.8.refs_6_
  47.7 0.0 collective-permute-done.4.refs_1_
  47.7 0.0 collective-permute-done.5.refs_2_
  47.7 2.2 %finish.1 = (f32[64,64,128]{2,1,0:T(8,128)}, f32[4]{0:T(128)}) custom-call(s32[4]{0:T(128)S(1)} %pad_add_fusion.refs_0_, bf16[208,128]{1,0:T(8,128)(2,1)S(1)} %collective-permute-done.4.refs_1_, bf16[208,128]{1,0:T(8,128)(2,1)S(1)} %collective-permute-done.5.refs_2_, f32[8,128]{1,0:T(8,128)S(1)} %get-tuple-element.27.refs_3_, ...), custom_call_target="tpu_custom_call", output_to_operand_aliasing={{0}: (10, {})} | custom-call | tf_op jit(solution)/shard_map/finish/pallas_call | solution.py:502
Async XLA Ops:
  0.6 1.6 %copy-start = (f32[64,64,128]{2,1,0:T(8,128)S(1)}, f32[64,64,128]{2,1,0:T(8,128)}, u32[]{:S(2)}) copy-start(f32[64,64,128]{2,1,0:T(8,128)} %refs_3_.3) | copy-start | bytes 6291460
  2.2 1.6 %copy-start.2 = (s32[64,64,128]{2,1,0:T(8,128)S(1)}, s32[64,64,128]{2,1,0:T(8,128)}, u32[]{:S(2)}) copy-start(s32[64,64,128]{2,1,0:T(8,128)} %refs_4_.3) | copy-start | bytes 6291460
  3.8 2.2 %copy-start.6 = (bf16[4,64,64,128]{3,2,1,0:T(8,128)(2,1)S(1)}, bf16[4,64,64,128]{3,2,1,0:T(8,128)(2,1)}, u32[]{:S(2)}) copy-start(bf16[4,64,64,128]{3,2,1,0:T(8,128)(2,1)} %refs_5_.1) | copy-start | bytes 12582916
  6.0 0.7 %copy-start.11 = (f32[4,128]{1,0:T(4,128)S(1)}, f32[4,128]{1,0:T(4,128)}, u32[]{:S(2)}) copy-start(f32[4,128]{1,0:T(4,128)} %refs_2_.3) | copy-start | bytes 6148
  6.7 0.7 %copy-start.13 = (s32[4]{0:T(128)S(1)}, s32[4]{0:T(128)}, u32[]{:S(2)}) copy-start(s32[4]{0:T(128)} %refs_0_.3) | copy-start | bytes 52
  7.3 0.7 %copy-start.15 = (f32[16]{0:T(128)S(1)}, f32[16]{0:T(128)}, u32[]{:S(2)}) copy-start(f32[16]{0:T(128)} %refs_1_.3) | copy-start | bytes 196
  8.0 11.3 %copy-start.1 = (f32[64,64,128]{2,1,0:T(8,128)S(1)}, f32[64,64,128]{2,1,0:T(8,128)}, u32[]{:S(2)}) copy-start(f32[64,64,128]{2,1,0:T(8,128)} %refs_3_.3) | copy-start | bytes 6291460
  8.0 11.3 %copy-start.12 = (f32[4,128]{1,0:T(4,128)S(1)}, f32[4,128]{1,0:T(4,128)}, u32[]{:S(2)}) copy-start(f32[4,128]{1,0:T(4,128)} %refs_2_.3) | copy-start | bytes 6148
  8.0 11.4 %copy-start.14 = (s32[4]{0:T(128)S(1)}, s32[4]{0:T(128)}, u32[]{:S(2)}) copy-start(s32[4]{0:T(128)} %refs_0_.3) | copy-start | bytes 52
  8.0 11.4 %copy-start.16 = (f32[16]{0:T(128)S(1)}, f32[16]{0:T(128)}, u32[]{:S(2)}) copy-start(f32[16]{0:T(128)} %refs_1_.3) | copy-start | bytes 196
  13.0 2.0 %copy-start.7 = (bf16[4096,512]{1,0:T(8,128)(2,1)}, bf16[4096,512]{1,0:T(8,128)(2,1)S(1)}, u32[]{:S(2)}) copy-start(bf16[4096,512]{1,0:T(8,128)(2,1)S(1)} %get-tuple-element.20.refs_5_) | copy-start | bytes 12582916
  14.9 15.0 %collective-permute-start = (bf16[8,4224]{1,0:T(8,128)(2,1)S(1)}, bf16[8,4224]{1,0:T(8,128)(2,1)S(1)}, u32[]{:S(2)}, u32[]{:S(2)}) collective-permute-start(bf16[8,4224]{1,0:T(8,128)(2,1)S(1)} %get-tuple-element.19), channel_id=1, source_target_pairs={{0,8},{8,0},{16,24},{24,16},{1,9},{9,1},{17,25},{25,17},{2,10},{10... | collective-permute-start | bytes 202760 | tf_op jit(solution)/shard_map/ppermute | solution.py:533
  17.0 12.8 %collective-permute-start.1 = (bf16[8,4224]{1,0:T(8,128)(2,1)S(1)}, bf16[8,4224]{1,0:T(8,128)(2,1)S(1)}, u32[]{:S(2)}, u32[]{:S(2)}) collective-permute-start(bf16[8,4224]{1,0:T(8,128)(2,1)S(1)} %get-tuple-element.19), channel_id=1, source_target_pairs={{0,16},{8,24},{16,0},{24,8},{1,17},{9,25},{17,1},{25,9},{2,18},{10... | collective-permute-start | bytes 202760 | tf_op jit(solution)/shard_map/ppermute | solution.py:533
  19.3 10.5 %collective-permute-start.2 = (bf16[8,4224]{1,0:T(8,128)(2,1)S(1)}, bf16[8,4224]{1,0:T(8,128)(2,1)S(1)}, u32[]{:S(2)}, u32[]{:S(2)}) collective-permute-start(bf16[8,4224]{1,0:T(8,128)(2,1)S(1)} %get-tuple-element.19), channel_id=1, source_target_pairs={{0,24},{8,16},{16,8},{24,0},{1,25},{9,17},{17,9},{25,1},{2,26},{10... | collective-permute-start | bytes 202760 | tf_op jit(solution)/shard_map/ppermute | solution.py:533
  19.4 1.6 %copy-start.3 = (s32[64,64,128]{2,1,0:T(8,128)S(1)}, s32[64,64,128]{2,1,0:T(8,128)}, u32[]{:S(2)}) copy-start(s32[64,64,128]{2,1,0:T(8,128)} %refs_4_.3) | copy-start | bytes 6291460
  21.0 2.2 %copy-start.8 = (bf16[4096,512]{1,0:T(8,128)(2,1)S(1)}, bf16[4096,512]{1,0:T(8,128)(2,1)}, u32[]{:S(2)}) copy-start(bf16[4096,512]{1,0:T(8,128)(2,1)} %copy-done.7) | copy-start | bytes 12582916
  27.1 1.4 %copy-start.4 = (f32[64,64,128]{2,1,0:T(8,128)}, f32[64,64,128]{2,1,0:T(8,128)S(1)}, u32[]{:S(2)}) copy-start(f32[64,64,128]{2,1,0:T(8,128)S(1)} %get-tuple-element.30.refs_3_.refs_9_) | copy-start | bytes 6291460
  28.5 1.3 %copy-start.9 = (f32[64,64,128]{2,1,0:T(8,128)}, f32[64,64,128]{2,1,0:T(8,128)S(1)}, u32[]{:S(2)}) copy-start(f32[64,64,128]{2,1,0:T(8,128)S(1)} %get-tuple-element.21.refs_5_) | copy-start | bytes 6291460
  29.9 1.6 %copy-start.10 = (f32[64,64,128]{2,1,0:T(8,128)S(1)}, f32[64,64,128]{2,1,0:T(8,128)}, u32[]{:S(2)}) copy-start(f32[64,64,128]{2,1,0:T(8,128)} %copy-done.9) | copy-start | bytes 6291460
  31.5 13.1 %copy-start.5 = (f32[64,64,128]{2,1,0:T(8,128)S(1)}, f32[64,64,128]{2,1,0:T(8,128)}, u32[]{:S(2)}) copy-start(f32[64,64,128]{2,1,0:T(8,128)} %copy-done.4) | copy-start | bytes 6291460
  32.7 3.0 %collective-permute-start.3 = (bf16[208,128]{1,0:T(8,128)(2,1)S(1)}, bf16[208,128]{1,0:T(8,128)(2,1)S(1)}, u32[]{:S(2)}, u32[]{:S(2)}) collective-permute-start(bf16[208,128]{1,0:T(8,128)(2,1)S(1)} %get-tuple-element.24.refs_3_), channel_id=1, source_target_pairs={{0,4},{4,0},{1,5},{5,1},{2,6},{6,2},{3,7},{7,3},{8,12},{12,8},{9,1... | collective-permute-start | bytes 159752 | tf_op jit(solution)/shard_map/ppermute | solution.py:545
  36.6 11.0 %collective-permute-start.4 = (bf16[208,128]{1,0:T(8,128)(2,1)S(1)}, bf16[208,128]{1,0:T(8,128)(2,1)S(1)}, u32[]{:S(2)}, u32[]{:S(2)}) collective-permute-start(bf16[208,128]{1,0:T(8,128)(2,1)S(1)} %get-tuple-element.25), channel_id=1, source_target_pairs={{0,1},{1,0},{2,3},{3,2},{4,5},{5,4},{6,7},{7,6},{8,9},{9,8},{10,11... | collective-permute-start | bytes 159752 | tf_op jit(solution)/shard_map/ppermute | solution.py:548
  39.1 8.6 %collective-permute-start.5 = (bf16[208,128]{1,0:T(8,128)(2,1)S(1)}, bf16[208,128]{1,0:T(8,128)(2,1)S(1)}, u32[]{:S(2)}, u32[]{:S(2)}) collective-permute-start(bf16[208,128]{1,0:T(8,128)(2,1)S(1)} %get-tuple-element.26), channel_id=1, source_target_pairs={{1,2},{2,1},{5,6},{6,5},{9,10},{10,9},{13,14},{14,13},{17,18},{18,... | collective-permute-start | bytes 159752 | tf_op jit(solution)/shard_map/ppermute | solution.py:548
  42.4 5.3 %collective-permute-start.6 = (f32[8,128]{1,0:T(8,128)S(1)}, f32[8,128]{1,0:T(8,128)S(1)}, u32[]{:S(2)}, u32[]{:S(2)}) collective-permute-start(f32[8,128]{1,0:T(8,128)S(1)} %get-tuple-element.27.refs_3_), channel_id=1, source_target_pairs={{0,1},{1,0},{2,3},{3,2},{4,5},{5,4},{6,7},{7,6},{8,9},{9,8},{10,11... | collective-permute-start | bytes 12296 | tf_op jit(solution)/shard_map/ppermute | solution.py:549
  42.4 5.2 %collective-permute-start.7 = (f32[8,128]{1,0:T(8,128)S(1)}, f32[8,128]{1,0:T(8,128)S(1)}, u32[]{:S(2)}, u32[]{:S(2)}) collective-permute-start(f32[8,128]{1,0:T(8,128)S(1)} %get-tuple-element.27.refs_3_), channel_id=1, source_target_pairs={{0,2},{1,3},{2,0},{3,1},{4,6},{5,7},{6,4},{7,5},{8,10},{9,11},{10,... | collective-permute-start | bytes 12296 | tf_op jit(solution)/shard_map/ppermute | solution.py:549
  42.9 4.7 %collective-permute-start.8 = (f32[8,128]{1,0:T(8,128)S(1)}, f32[8,128]{1,0:T(8,128)S(1)}, u32[]{:S(2)}, u32[]{:S(2)}) collective-permute-start(f32[8,128]{1,0:T(8,128)S(1)} %get-tuple-element.27.refs_3_), channel_id=1, source_target_pairs={{0,3},{1,2},{2,1},{3,0},{4,7},{5,6},{6,5},{7,4},{8,11},{9,10},{10,... | collective-permute-start | bytes 12296 | tf_op jit(solution)/shard_map/ppermute | solution.py:549

commit v3 on v2

--- a/solution.py
+++ b/solution.py
@@ -16,6 +16,14 @@
 HBM = pl.BlockSpec(memory_space=pltpu.HBM)
 VMEM = pl.BlockSpec(memory_space=pltpu.VMEM)
 SMEM = pl.BlockSpec(memory_space=pltpu.SMEM)
+
+
+def in_hbm(*arrays):
+    return [pltpu.with_memory_space_constraint(a, pltpu.HBM) for a in arrays]
+
+
+def in_vmem(*arrays):
+    return [pltpu.with_memory_space_constraint(a, pltpu.VMEM) for a in arrays]
 
 
 def taps_1d():
@@ -168,9 +176,9 @@
         in_specs=[HBM] * 6,
         out_specs=[VMEM] * 3,
         out_shape=[
-            jax.ShapeDtypeStruct((2 * cases, width), BF16),
-            jax.ShapeDtypeStruct((2 * cases, width), F32),
-            jax.ShapeDtypeStruct((nx * ny, cases * depth), BF16),
+            pltpu.VMEM((2 * cases, width), BF16),
+            pltpu.VMEM((2 * cases, width), F32),
+            pltpu.VMEM((nx * ny, cases * depth), BF16),
         ],
         scratch_shapes=[
             pltpu.SMEM(case_index.shape, case_index.dtype),
@@ -184,7 +192,7 @@
         ],
         compiler_params=pltpu.CompilerParams(vmem_limit_bytes=20 * MIB),
         name="faces",
-    )(case_index, case_weight, decay, density, design_mask, energy)
+    )(*in_hbm(case_index, case_weight, decay, density, design_mask, energy))
 
 
 def local_kernel(shape, bx, *refs):
@@ -241,9 +249,9 @@
         in_specs=[HBM] * 5 + [VMEM],
         out_specs=[VMEM] * 3,
         out_shape=[
-            jax.ShapeDtypeStruct(density.shape, F32),
-            jax.ShapeDtypeStruct(density.shape, F32),
-            jax.ShapeDtypeStruct((8 * cases, depth), BF16),
+            pltpu.VMEM(density.shape, F32),
+            pltpu.VMEM(density.shape, F32),
+            pltpu.VMEM((8 * cases, depth), BF16),
         ],
         scratch_shapes=[
             pltpu.SMEM(case_index.shape, case_index.dtype),
@@ -256,19 +264,20 @@
         ],
         compiler_params=pltpu.CompilerParams(vmem_limit_bytes=20 * MIB),
         name="local",
-    )(case_index, case_weight, decay, density, design_mask, source)
-
-
-def couple_kernel(shape, nslabs, nsends, *refs):
+    )(*in_hbm(case_index, case_weight, decay, density, design_mask), *in_vmem(source))
+
+
+def couple_kernel(shape, nslabs, nsends, swapped, *refs):
     cases, nx, ny, depth = shape
-    slot_ref, own_ref = refs[0:2]
-    msgs = refs[2 : 1 + nslabs]
-    t_ref, umap_ref, out_ref = refs[1 + nslabs : 4 + nslabs]
-    sends = refs[4 + nslabs : 4 + nslabs + nsends]
+    own_ref = refs[0]
+    msgs = refs[1:nslabs]
+    t_ref, umap_ref, out_ref = refs[nslabs : 3 + nslabs]
+    sends = refs[3 + nslabs : 3 + nslabs + nsends]
     stack = refs[-1]
     cols = nx * ny
-    mine = slot_ref[0]
-    stack[0] = own_ref[...]
+    mine = lax.axis_index("gz")
+    high = (1 - lax.axis_index("gx") % 2) * (nx - RADIUS)
+    stack[0] = own_ref[...].astype(F32)
     for m, msg in enumerate(msgs):
         stack[m + 1] = msg[...].astype(F32)
     total = jnp.zeros((cases, 1), F32)
@@ -278,7 +287,7 @@
     entering, above = state, state
     tops, gains = [], []
     for j in range(nslabs):
-        at = slot_ref[2 + j]
+        at = mine ^ j if swapped else j
         aux = stack[at, 0:cases, cols : cols + LANES]
         gains.append(sum3(aux, 0))
         entering = jnp.where(mine == j, state, entering)
@@ -295,25 +304,25 @@
     out_ref[...] = t_ref[...] + add.reshape(nx, ny, depth)
     aux = pad_rows(put_lanes(split3(total)), 16).astype(BF16)
     for k, ref in enumerate(sends):
-        edge = out_ref[pl.ds(slot_ref[1] if k == 0 else nx - RADIUS - slot_ref[1], RADIUS)]
+        edge = out_ref[pl.ds(high if k == 0 else nx - RADIUS - high, RADIUS)]
         ref[0 : RADIUS * ny, :] = edge.reshape(RADIUS * ny, depth).astype(BF16)
         ref[RADIUS * ny :, :] = aux
 
 
-def couple_call(slots, own, msgs, t_local, umap, nsends):
+def couple_call(own, msgs, t_local, umap, nsends, swapped):
     nx, ny, depth = t_local.shape
     cases = own.shape[0] // 2
     nslabs = len(msgs) + 1
     return pl.pallas_call(
-        functools.partial(couple_kernel, (cases, nx, ny, depth), nslabs, nsends),
-        in_specs=[SMEM] + [VMEM] * (nslabs + 2),
+        functools.partial(couple_kernel, (cases, nx, ny, depth), nslabs, nsends, swapped),
+        in_specs=[VMEM] * (nslabs + 2),
         out_specs=[VMEM] * (1 + nsends),
         out_shape=[jax.ShapeDtypeStruct(t_local.shape, F32)]
         + [jax.ShapeDtypeStruct((RADIUS * ny + 16, depth), BF16)] * nsends,
         scratch_shapes=[pltpu.VMEM((nslabs,) + own.shape, F32)],
         compiler_params=pltpu.CompilerParams(vmem_limit_bytes=28 * MIB),
         name="couple",
-    )(slots, own, *msgs, t_local, umap)
+    )(own, *msgs, *in_vmem(t_local), umap)
 
 
 def sided(even, got):
@@ -324,15 +333,15 @@
 
 def edge_kernel(shape, nx_sends, ny_sends, *refs):
     cases, nx, ny, depth = shape
-    slot_ref, t_ref = refs[0:2]
-    got_refs = refs[2 : 2 + nx_sends]
-    own_send = refs[2 + nx_sends]
-    sends = refs[3 + nx_sends : 3 + nx_sends + ny_sends]
-    xb_ref, xa_ref, sums_ref, line = refs[3 + nx_sends + ny_sends :]
+    t_ref = refs[0]
+    got_refs = refs[1 : 1 + nx_sends]
+    own_send = refs[1 + nx_sends]
+    sends = refs[2 + nx_sends : 2 + nx_sends + ny_sends]
+    xb_ref, xa_ref, sums_ref, line = refs[2 + nx_sends + ny_sends :]
     taps = taps_1d()
     edge = RADIUS * ny
-    even_x = slot_ref[2] == 0
-    flip_y = slot_ref[3] == 1
+    even_x = lax.axis_index("gx") % 2 == 0
+    flip_y = lax.axis_index("gy") % 2 == 1
     blocks = [r[0:edge, :].astype(F32) for r in got_refs]
     before, after = sided(even_x, blocks)
     xb_ref[...] = before
@@ -361,11 +370,11 @@
         ref[RADIUS * nx :, :] = aux
 
 
-def edge_call(slots, t, got, own_send, ny_sends, cases):
+def edge_call(t, got, own_send, ny_sends, cases):
     nx, ny, depth = t.shape
     return pl.pallas_call(
         functools.partial(edge_kernel, (cases, nx, ny, depth), len(got), ny_sends),
-        in_specs=[SMEM] + [VMEM] * (2 + len(got)),
+        in_specs=[VMEM] * (2 + len(got)),
         out_specs=[VMEM] * (ny_sends + 3),
         out_shape=[jax.ShapeDtypeStruct((RADIUS * nx + 16, depth), BF16)] * ny_sends
         + [jax.ShapeDtypeStruct((RADIUS * ny, depth), F32)] * 2
@@ -373,7 +382,7 @@
         scratch_shapes=[pltpu.VMEM((nx + 16, depth), F32)],
         compiler_params=pltpu.CompilerParams(vmem_limit_bytes=16 * MIB),
         name="edge",
-    )(slots, t, *got, own_send)
+    )(t, *got, own_send)
 
 
 def plane_kernel(shape, bx, *refs):
@@ -451,19 +460,18 @@
         ],
         compiler_params=pltpu.CompilerParams(vmem_limit_bytes=20 * MIB),
         name="plane",
-    )(t, xb, xa, factor)
+    )(*in_vmem(t, xb, xa, factor))
 
 
 def finish_kernel(shape, cells, ngot, nextra, cases, *refs):
     nx, ny, depth = shape
-    slot_ref = refs[0]
-    got_refs = refs[1 : 1 + ngot]
-    sums_ref = refs[1 + ngot]
-    extra_refs = refs[2 + ngot : 2 + ngot + nextra]
-    first_ref, last_ref, factor_ref, _, out_hbm, comp_ref, strip, sem = refs[2 + ngot + nextra :]
+    got_refs = refs[:ngot]
+    sums_ref = refs[ngot]
+    extra_refs = refs[1 + ngot : 1 + ngot + nextra]
+    first_ref, last_ref, factor_ref, _, out_hbm, comp_ref, strip, sem = refs[1 + ngot + nextra :]
     taps = taps_1d()
     edge = RADIUS * nx
-    even_y = slot_ref[3] == 0
+    even_y = lax.axis_index("gy") % 2 == 0
     blocks = [r[0:edge, :].astype(F32) for r in got_refs]
     before, after = sided(even_y, blocks) if blocks else (jnp.zeros((edge, depth), F32),) * 2
     flat = factor_ref.reshape(nx * ny, depth)
@@ -496,19 +504,19 @@
         copy.wait()
 
 
-def finish_call(slots, got, sums, extra, first, last, factor, out, cells, cases):
+def finish_call(got, sums, extra, first, last, factor, out, cells, cases):
     nx, ny, depth = out.shape
-    nin = 1 + len(got) + 1 + len(extra)
+    nin = len(got) + 1 + len(extra)
     return pl.pallas_call(
         functools.partial(finish_kernel, out.shape, cells, len(got), len(extra), cases),
-        in_specs=[SMEM] + [VMEM] * (nin - 1 + 3) + [HBM],
+        in_specs=[VMEM] * (nin + 3) + [HBM],
         out_specs=[HBM, SMEM],
         out_shape=[jax.ShapeDtypeStruct(out.shape, F32), jax.ShapeDtypeStruct((cases,), F32)],
         input_output_aliases={nin + 3: 0},
         scratch_shapes=[pltpu.VMEM((2, nx, 8, depth), F32), pltpu.SemaphoreType.DMA((2,))],
         compiler_params=pltpu.CompilerParams(vmem_limit_bytes=16 * MIB),
         name="finish",
-    )(slots, *got, sums, *extra, first, last, factor, out)
+    )(*got, sums, *extra, *in_vmem(first, last, factor), *in_hbm(out))
 
 
 def swap_pairs(count, first):
@@ -527,29 +535,22 @@
     cases = energy.shape[0]
     nx, ny, depth = density.shape
     nz, gx, gy = (lax.axis_size(a) for a in ("gz", "gx", "gy"))
-    iz, ix, iy = (lax.axis_index(a) for a in ("gz", "gx", "gy"))
     send, own, source = faces_call(density, design_mask, energy, decay, case_index, case_weight)
-    if nz in (1, 2, 4):
+    swapped = nz in (1, 2, 4)
+    if swapped:
         msgs = [lax.ppermute(send, "gz", xor_pairs(nz, m)) for m in range(1, nz)]
-        order = [iz ^ j for j in range(nz)]
     else:
         every = lax.all_gather(send, "gz")
-        msgs = [every[j] for j in range(nz)]
-        order = [jnp.int32(j) for j in range(nz)]
+        own, *msgs = [every[j] for j in range(nz)]
     t_local, factor, umap = local_call(density, design_mask, source, decay, case_index, case_weight)
-    flip_x, flip_y = ix % 2, iy % 2
-    slots = jnp.stack([iz, (1 - flip_x) * (nx - RADIUS)] + order).astype(jnp.int32)
-    if nz not in (1, 2, 4):
-        own, msgs = msgs[0].astype(F32), msgs[1:]
-    t, *x_sends = couple_call(slots, own, msgs, t_local, umap, max(swaps_of(gx), 1))
+    t, *x_sends = couple_call(own, msgs, t_local, umap, max(swaps_of(gx), 1), swapped)
     x_got = [lax.ppermute(x_sends[k], "gx", swap_pairs(gx, k)) for k in range(swaps_of(gx))]
-    marks = jnp.stack([iz, ix, flip_x, flip_y]).astype(jnp.int32)
-    *y_sends, xb, xa, sums = edge_call(marks, t, x_got, x_sends[0], swaps_of(gy), cases)
+    *y_sends, xb, xa, sums = edge_call(t, x_got, x_sends[0], swaps_of(gy), cases)
     y_got = [lax.ppermute(y_sends[k], "gy", swap_pairs(gy, k)) for k in range(swaps_of(gy))]
     extra = [lax.ppermute(sums, "gy", xor_pairs(gy, m)) for m in range(1, gy)]
     partial, first, last = plane_call(t, xb, xa, factor)
     cells = nx * ny * depth * nz * gx * gy
-    return tuple(finish_call(marks, y_got, sums, extra, first, last, factor, partial, float(cells), cases))
+    return tuple(finish_call(y_got, sums, extra, first, last, factor, partial, float(cells), cases))
 
 
 def solution(mesh):

time: 50.2 us -> 35.2 us (0.70)
  local copies, waits for them, and re-layouts: 17.4 us -> 0 us
  Pallas kernels: 16.2 us -> 17.6 us
  starting transfers between devices: 13.6 us -> 14.6 us
    unnamed x34 -> x0, local copies, waits for them, and re-layouts: 17.3 us -> none
    pallas_call x1, Pallas kernels: 4.94 us -> 7.12 us  [faces_call(): pl.pallas_call(functools.partial(faces_kernel, energy.shape, bx), in_spec...]
    ppermute x2, starting transfers between devices: 5.7 us -> 6.64 us  [shards(): lax.ppermute(y_sends[k], 'gy', swap_pairs(gy, k))]
    pallas_call x1, Pallas kernels: 3.96 us -> 4.71 us  [local_call(): pl.pallas_call(functools.partial(local_kernel, (cases, nx, ny, depth), 8)...]
    pallas_call x1, Pallas kernels: 2.17 us -> 1.63 us  [finish_call(): pl.pallas_call(functools.partial(finish_kernel, out.shape, cells, len(got...]
    pallas_call x1, Pallas kernels: 1.24 us -> 0.73 us  [couple_call(): pl.pallas_call(functools.partial(couple_kernel, (cases, nx, ny, depth), n...]
    pallas_call x1, Pallas kernels: 0.86 us -> 0.35 us  [edge_call(): pl.pallas_call(functools.partial(edge_kernel, (cases, nx, ny, depth), len...]
  transfers between devices with their start and end apart: 9 -> 9, of which waited for: 1 -> 2; matrix products, arithmetic and copies ran while one was open for 0% -> 0% of each run, Pallas kernels for 14% -> 22%
where the time goes in v3:
time: 35.2 us; the launch traced here: 35 us
  Pallas kernels  17.6 us (50%)
  starting transfers between devices  14.6 us (41%)
  waiting for transfers between devices  2.1 us (6%)
  between operations  0.74 us (2%)
    pallas_call x1, Pallas kernels, faces_call(): pl.pallas_call(functools.partial(faces_kernel, energy.shape, bx), in_spec...  7.12 us
    ppermute x2, starting transfers between devices, shards(): lax.ppermute(y_sends[k], 'gy', swap_pairs(gy, k))  6.64 us
    pallas_call x1, Pallas kernels, local_call(): pl.pallas_call(functools.partial(local_kernel, (cases, nx, ny, depth), 8)...  4.71 us
    ppermute x3, starting transfers between devices, shards(): msgs = [lax.ppermute(send, 'gz', xor_pairs(nz, m)) for m in range(1, nz)]  4.49 us
    pallas_call x1, Pallas kernels, plane_call(): pl.pallas_call(functools.partial(plane_kernel, t.shape, bx), in_specs=[VM...  3.05 us
    ppermute x3, starting transfers between devices, shards(): extra = [lax.ppermute(sums, 'gy', xor_pairs(gy, m)) for m in range(1, gy)]  2.2 us
    ppermute x1, waiting for transfers between devices, shards(): lax.ppermute(x_sends[k], 'gx', swap_pairs(gx, k))  1.78 us
    pallas_call x1, Pallas kernels, finish_call(): pl.pallas_call(functools.partial(finish_kernel, out.shape, cells, len(got...  1.63 us
  transfers between devices with their start and end apart: 9, of which 2 were waited for; matrix products, arithmetic and copies ran while one was open for 0% of the time, Pallas kernels for 22%

profile of v3, /device:TPU:1, one launch (start us, length us, event | category | flops | bytes accessed | tf_op | source)
XLA Modules:
  0.0 35.0 jit_solution(8728076196523495105)
XLA Ops:
  0.6 7.1 %faces.1 = (bf16[8,4224]{1,0:T(8,128)(2,1)S(1)}, f32[8,4224]{1,0:T(8,128)S(1)}, bf16[4096,512]{1,0:T(8,128)(2,1)S(1)}) custom-call(s32[4]{0:T(128)} %refs_0_.3, f32[16]{0:T(128)} %refs_1_.3, f32[4,128]{1,0:T(4,128)} %refs_2_.3, f32[64,64,128]{2,1,0:T(8,128)} %refs_3_.3, s32[64,64,128]{2,1,0:T(8,128)} %refs_4_.3, bf16[4,64,64,128]{3,2,1,0:T(8,128)(2,1)} %refs_5_.1), custom_call_target="tpu_custom_call" | custom-call | tf_op jit(solution)/shard_map/faces/pallas_call | solution.py:174
  7.8 2.2 %collective-permute-start = (bf16[8,4224]{1,0:T(8,128)(2,1)S(1)}, bf16[8,4224]{1,0:T(8,128)(2,1)S(1)}, u32[]{:S(2)}, u32[]{:S(2)}) collective-permute-start(bf16[8,4224]{1,0:T(8,128)(2,1)S(1)} %get-tuple-element.19), channel_id=1, source_target_pairs={{0,8},{8,0},{16,24},{24,16},{1,9},{9,1},{17,25},{25,17},{2,10},{10... | collective-permute-start | bytes 202760 | tf_op jit(solution)/shard_map/ppermute | solution.py:541
  9.9 2.3 %collective-permute-start.1 = (bf16[8,4224]{1,0:T(8,128)(2,1)S(1)}, bf16[8,4224]{1,0:T(8,128)(2,1)S(1)}, u32[]{:S(2)}, u32[]{:S(2)}) collective-permute-start(bf16[8,4224]{1,0:T(8,128)(2,1)S(1)} %get-tuple-element.19), channel_id=1, source_target_pairs={{0,16},{8,24},{16,0},{24,8},{1,17},{9,25},{17,1},{25,9},{2,18},{10... | collective-permute-start | bytes 202760 | tf_op jit(solution)/shard_map/ppermute | solution.py:541
  12.2 0.0 collective-permute-start.2
  12.3 4.7 %local.1 = (f32[64,64,128]{2,1,0:T(8,128)S(1)}, f32[64,64,128]{2,1,0:T(8,128)S(1)}, bf16[32,128]{1,0:T(8,128)(2,1)S(1)}) custom-call(s32[4]{0:T(128)} %refs_0_.3, f32[16]{0:T(128)} %refs_1_.3, f32[4,128]{1,0:T(4,128)} %refs_2_.3, f32[64,64,128]{2,1,0:T(8,128)} %refs_3_.3, s32[64,64,128]{2,1,0:T(8,128)} %refs_4_.3, ...), custom_call_target="tpu_custom_call" | custom-call | tf_op jit(solution)/shard_map/local/pallas_call | solution.py:247
  17.0 0.0 collective-permute-done.refs_1_
  17.0 0.0 collective-permute-done.1.refs_2_
  17.0 0.3 collective-permute-done.2.refs_3_
  17.3 0.7 %couple.1 = (f32[64,64,128]{2,1,0:T(8,128)S(1)}, bf16[208,128]{1,0:T(8,128)(2,1)S(1)}) custom-call(f32[8,4224]{1,0:T(8,128)S(1)} %get-tuple-element.18.refs_0_, bf16[8,4224]{1,0:T(8,128)(2,1)S(1)} %collective-permute-done.refs_1_, bf16[8,4224]{1,0:T(8,128)(2,1)S(1)} %collective-permute-done.1.refs_2_, bf16[8,4224]{1,0:T(8,128)(2,1)S(1)} %collective-permute-done.2.refs_3_, ...), custom_call_target="tpu_custom_call" | custom-call | tf_op jit(solution)/shard_map/couple/pallas_call | solution.py:316
  18.0 1.3 %collective-permute-start.3 = (bf16[208,128]{1,0:T(8,128)(2,1)S(1)}, bf16[208,128]{1,0:T(8,128)(2,1)S(1)}, u32[]{:S(2)}, u32[]{:S(2)}) collective-permute-start(bf16[208,128]{1,0:T(8,128)(2,1)S(1)} %get-tuple-element.24.refs_2_), channel_id=1, source_target_pairs={{0,4},{4,0},{1,5},{5,1},{2,6},{6,2},{3,7},{7,3},{8,12},{12,8},{9,1... | collective-permute-start | bytes 159752 | tf_op jit(solution)/shard_map/ppermute | solution.py:547
  19.3 1.8 %collective-permute-done.3.refs_1_ = bf16[208,128]{1,0:T(8,128)(2,1)S(1)} collective-permute-done((bf16[208,128]{1,0:T(8,128)(2,1)S(1)}, bf16[208,128]{1,0:T(8,128)(2,1)S(1)}, u32[]{:S(2)}, u32[]{:S(2)}) %collective-permute-start.3) | collective-permute-done | bytes 53280 | tf_op jit(solution)/shard_map/ppermute | solution.py:547
  21.1 0.4 %edge.1 = (bf16[208,128]{1,0:T(8,128)(2,1)S(1)}, bf16[208,128]{1,0:T(8,128)(2,1)S(1)}, f32[192,128]{1,0:T(8,128)S(1)}, f32[192,128]{1,0:T(8,128)S(1)}, f32[8,128]{1,0:T(8,128)S(1)}) custom-call(f32[64,64,128]{2,1,0:T(8,128)S(1)} %get-tuple-element.23.refs_0_, bf16[208,128]{1,0:T(8,128)(2,1)S(1)} %collective-permute-done.3.refs_1_, ...), custom_call_target="tpu_custom_call" | custom-call | tf_op jit(solution)/shard_map/edge/pallas_call | solution.py:375
  21.4 3.6 %collective-permute-start.4 = (bf16[208,128]{1,0:T(8,128)(2,1)S(1)}, bf16[208,128]{1,0:T(8,128)(2,1)S(1)}, u32[]{:S(2)}, u32[]{:S(2)}) collective-permute-start(bf16[208,128]{1,0:T(8,128)(2,1)S(1)} %get-tuple-element.25), channel_id=1, source_target_pairs={{0,1},{1,0},{2,3},{3,2},{4,5},{5,4},{6,7},{7,6},{8,9},{9,8},{10,11... | collective-permute-start | bytes 159752 | tf_op jit(solution)/shard_map/ppermute | solution.py:549
  25.0 3.0 %collective-permute-start.5 = (bf16[208,128]{1,0:T(8,128)(2,1)S(1)}, bf16[208,128]{1,0:T(8,128)(2,1)S(1)}, u32[]{:S(2)}, u32[]{:S(2)}) collective-permute-start(bf16[208,128]{1,0:T(8,128)(2,1)S(1)} %get-tuple-element.26), channel_id=1, source_target_pairs={{1,2},{2,1},{5,6},{6,5},{9,10},{10,9},{13,14},{14,13},{17,18},{18,... | collective-permute-start | bytes 159752 | tf_op jit(solution)/shard_map/ppermute | solution.py:549
  28.1 0.1 collective-permute-start.6
  28.1 0.7 %collective-permute-start.7 = (f32[8,128]{1,0:T(8,128)S(1)}, f32[8,128]{1,0:T(8,128)S(1)}, u32[]{:S(2)}, u32[]{:S(2)}) collective-permute-start(f32[8,128]{1,0:T(8,128)S(1)} %get-tuple-element.27.refs_2_), channel_id=1, source_target_pairs={{0,2},{1,3},{2,0},{3,1},{4,6},{5,7},{6,4},{7,5},{8,10},{9,11},{10,... | collective-permute-start | bytes 12296 | tf_op jit(solution)/shard_map/ppermute | solution.py:550
  28.9 1.4 %collective-permute-start.8 = (f32[8,128]{1,0:T(8,128)S(1)}, f32[8,128]{1,0:T(8,128)S(1)}, u32[]{:S(2)}, u32[]{:S(2)}) collective-permute-start(f32[8,128]{1,0:T(8,128)S(1)} %get-tuple-element.27.refs_2_), channel_id=1, source_target_pairs={{0,3},{1,2},{2,1},{3,0},{4,7},{5,6},{6,5},{7,4},{8,11},{9,10},{10,... | collective-permute-start | bytes 12296 | tf_op jit(solution)/shard_map/ppermute | solution.py:550
  30.3 3.1 %plane.1 = (f32[64,64,128]{2,1,0:T(8,128)}, f32[64,8,128]{2,1,0:T(8,128)S(1)}, f32[64,8,128]{2,1,0:T(8,128)S(1)}) custom-call(f32[64,64,128]{2,1,0:T(8,128)S(1)} %get-tuple-element.23.refs_0_, f32[192,128]{1,0:T(8,128)S(1)} %get-tuple-element.28.refs_1_, f32[192,128]{1,0:T(8,128)S(1)} %get-tuple-element.29.refs_2_, ...), custom_call_target="tpu_custom_call" | custom-call | tf_op jit(solution)/shard_map/plane/pallas_call | solution.py:446
  33.3 0.0 collective-permute-done.6.refs_3_
  33.3 0.0 collective-permute-done.7.refs_4_
  33.4 0.0 collective-permute-done.8.refs_5_
  33.4 0.0 collective-permute-done.4.refs_0_
  33.4 0.0 collective-permute-done.5.refs_1_
  33.4 1.6 %finish.1 = (f32[64,64,128]{2,1,0:T(8,128)}, f32[4]{0:T(128)}) custom-call(bf16[208,128]{1,0:T(8,128)(2,1)S(1)} %collective-permute-done.4.refs_0_, bf16[208,128]{1,0:T(8,128)(2,1)S(1)} %collective-permute-done.5.refs_1_, f32[8,128]{1,0:T(8,128)S(1)} %get-tuple-element.27.refs_2_, ...), custom_call_target="tpu_custom_call", output_to_operand_aliasing={{0}: (9, {})} | custom-call | tf_op jit(solution)/shard_map/finish/pallas_call | solution.py:510
Async XLA Ops:
  7.8 9.2 %collective-permute-start = (bf16[8,4224]{1,0:T(8,128)(2,1)S(1)}, bf16[8,4224]{1,0:T(8,128)(2,1)S(1)}, u32[]{:S(2)}, u32[]{:S(2)}) collective-permute-start(bf16[8,4224]{1,0:T(8,128)(2,1)S(1)} %get-tuple-element.19), channel_id=1, source_target_pairs={{0,8},{8,0},{16,24},{24,16},{1,9},{9,1},{17,25},{25,17},{2,10},{10... | collective-permute-start | bytes 202760 | tf_op jit(solution)/shard_map/ppermute | solution.py:541
  9.9 7.0 %collective-permute-start.1 = (bf16[8,4224]{1,0:T(8,128)(2,1)S(1)}, bf16[8,4224]{1,0:T(8,128)(2,1)S(1)}, u32[]{:S(2)}, u32[]{:S(2)}) collective-permute-start(bf16[8,4224]{1,0:T(8,128)(2,1)S(1)} %get-tuple-element.19), channel_id=1, source_target_pairs={{0,16},{8,24},{16,0},{24,8},{1,17},{9,25},{17,1},{25,9},{2,18},{10... | collective-permute-start | bytes 202760 | tf_op jit(solution)/shard_map/ppermute | solution.py:541
  12.2 5.0 %collective-permute-start.2 = (bf16[8,4224]{1,0:T(8,128)(2,1)S(1)}, bf16[8,4224]{1,0:T(8,128)(2,1)S(1)}, u32[]{:S(2)}, u32[]{:S(2)}) collective-permute-start(bf16[8,4224]{1,0:T(8,128)(2,1)S(1)} %get-tuple-element.19), channel_id=1, source_target_pairs={{0,24},{8,16},{16,8},{24,0},{1,25},{9,17},{17,9},{25,1},{2,26},{10... | collective-permute-start | bytes 202760 | tf_op jit(solution)/shard_map/ppermute | solution.py:541
  18.0 3.0 %collective-permute-start.3 = (bf16[208,128]{1,0:T(8,128)(2,1)S(1)}, bf16[208,128]{1,0:T(8,128)(2,1)S(1)}, u32[]{:S(2)}, u32[]{:S(2)}) collective-permute-start(bf16[208,128]{1,0:T(8,128)(2,1)S(1)} %get-tuple-element.24.refs_2_), channel_id=1, source_target_pairs={{0,4},{4,0},{1,5},{5,1},{2,6},{6,2},{3,7},{7,3},{8,12},{12,8},{9,1... | collective-permute-start | bytes 159752 | tf_op jit(solution)/shard_map/ppermute | solution.py:547
  21.4 12.0 %collective-permute-start.4 = (bf16[208,128]{1,0:T(8,128)(2,1)S(1)}, bf16[208,128]{1,0:T(8,128)(2,1)S(1)}, u32[]{:S(2)}, u32[]{:S(2)}) collective-permute-start(bf16[208,128]{1,0:T(8,128)(2,1)S(1)} %get-tuple-element.25), channel_id=1, source_target_pairs={{0,1},{1,0},{2,3},{3,2},{4,5},{5,4},{6,7},{7,6},{8,9},{9,8},{10,11... | collective-permute-start | bytes 159752 | tf_op jit(solution)/shard_map/ppermute | solution.py:549
  25.0 8.4 %collective-permute-start.5 = (bf16[208,128]{1,0:T(8,128)(2,1)S(1)}, bf16[208,128]{1,0:T(8,128)(2,1)S(1)}, u32[]{:S(2)}, u32[]{:S(2)}) collective-permute-start(bf16[208,128]{1,0:T(8,128)(2,1)S(1)} %get-tuple-element.26), channel_id=1, source_target_pairs={{1,2},{2,1},{5,6},{6,5},{9,10},{10,9},{13,14},{14,13},{17,18},{18,... | collective-permute-start | bytes 159752 | tf_op jit(solution)/shard_map/ppermute | solution.py:549
  28.1 5.3 %collective-permute-start.6 = (f32[8,128]{1,0:T(8,128)S(1)}, f32[8,128]{1,0:T(8,128)S(1)}, u32[]{:S(2)}, u32[]{:S(2)}) collective-permute-start(f32[8,128]{1,0:T(8,128)S(1)} %get-tuple-element.27.refs_2_), channel_id=1, source_target_pairs={{0,1},{1,0},{2,3},{3,2},{4,5},{5,4},{6,7},{7,6},{8,9},{9,8},{10,11... | collective-permute-start | bytes 12296 | tf_op jit(solution)/shard_map/ppermute | solution.py:550
  28.1 5.2 %collective-permute-start.7 = (f32[8,128]{1,0:T(8,128)S(1)}, f32[8,128]{1,0:T(8,128)S(1)}, u32[]{:S(2)}, u32[]{:S(2)}) collective-permute-start(f32[8,128]{1,0:T(8,128)S(1)} %get-tuple-element.27.refs_2_), channel_id=1, source_target_pairs={{0,2},{1,3},{2,0},{3,1},{4,6},{5,7},{6,4},{7,5},{8,10},{9,11},{10,... | collective-permute-start | bytes 12296 | tf_op jit(solution)/shard_map/ppermute | solution.py:550
  28.9 4.5 %collective-permute-start.8 = (f32[8,128]{1,0:T(8,128)S(1)}, f32[8,128]{1,0:T(8,128)S(1)}, u32[]{:S(2)}, u32[]{:S(2)}) collective-permute-start(f32[8,128]{1,0:T(8,128)S(1)} %get-tuple-element.27.refs_2_), channel_id=1, source_target_pairs={{0,3},{1,2},{2,1},{3,0},{4,7},{5,6},{6,5},{7,4},{8,11},{9,10},{10,... | collective-permute-start | bytes 12296 | tf_op jit(solution)/shard_map/ppermute | solution.py:550

commit v4 on v3

--- a/solution.py
+++ b/solution.py
@@ -8,6 +8,7 @@
 from jax.sharding import PartitionSpec as P
 
 RADIUS = 3
+AHEAD = 2
 LANES = 128
 MIB = 2**20
 F32 = jnp.float32
@@ -115,7 +116,7 @@
         ])
     for copy in small:
         copy.start()
-    for group in big:
+    for group in big[:AHEAD]:
         for copy in group:
             copy.start()
     for copy in small:
@@ -123,6 +124,9 @@
 
     decay = decay_ref[...]
     slab = Slab(decay)
+    for group in big[AHEAD : AHEAD + 1]:
+        for copy in group:
+            copy.start()
     zero_row = jnp.zeros((1, depth), F32)
     e_rows, h_rows, turns = [], [], []
     for c in range(cases):
@@ -140,9 +144,21 @@
     wmat = jnp.concatenate([w_hi, w_lo], axis=0)
 
     sums = [jnp.zeros((8, depth), F32) for _ in range(cases)]
+
+    def faces_of(s):
+        span = pl.ds(s * cols, cols)
+        faces = lax.dot_general(
+            wmat, source_ref[span, :], (((1,), (1,)), ((), ())), preferred_element_type=F32)
+        faces = faces[0 : 2 * cases] + faces[2 * cases : 4 * cases]
+        own_ref[:, span] = faces
+        send_ref[:, span] = faces.astype(BF16)
+
     for s in range(steps):
         for copy in big[s]:
             copy.wait()
+        for group in big[s + AHEAD + 1 : s + AHEAD + 2]:
+            for copy in group:
+                copy.start()
         at = pl.ds(s * bx, bx)
         mask = mask_ref[at]
         dense = jnp.where(mask == 1, 0.001, jnp.where(mask == 2, 1.0, density_ref[at]))
@@ -152,11 +168,9 @@
             work = cube * energy_ref[c, at].astype(F32)
             sums[c] = sums[c] + jnp.sum(work.reshape(cols // 8, 8, depth), axis=0)
             source_ref[span, c * depth : (c + 1) * depth] = work.astype(BF16).reshape(cols, depth)
-        faces = lax.dot_general(
-            wmat, source_ref[span, :], (((1,), (1,)), ((), ())), preferred_element_type=F32)
-        faces = faces[0 : 2 * cases] + faces[2 * cases : 4 * cases]
-        own_ref[:, span] = faces
-        send_ref[:, span] = faces.astype(BF16)
+        if s > 0:
+            faces_of(s - 1)
+    faces_of(steps - 1)
 
     total = jnp.concatenate([jnp.sum(jnp.sum(v, axis=0, keepdims=True), axis=1, keepdims=True) for v in sums], axis=0)
     turn = jnp.concatenate(turns, axis=0)
@@ -169,7 +183,7 @@
 
 def faces_call(density, design_mask, energy, decay, case_index, case_weight):
     cases, nx, ny, depth = energy.shape
-    bx = 8
+    bx = 16
     width = nx * ny + LANES
     return pl.pallas_call(
         functools.partial(faces_kernel, energy.shape, bx),
@@ -336,8 +350,8 @@
     t_ref = refs[0]
     got_refs = refs[1 : 1 + nx_sends]
     own_send = refs[1 + nx_sends]
-    sends = refs[2 + nx_sends : 2 + nx_sends + ny_sends]
-    xb_ref, xa_ref, sums_ref, line = refs[2 + nx_sends + ny_sends :]
+    sends = refs[3 + nx_sends : 3 + nx_sends + ny_sends]
+    xb_ref, xa_ref, sums_ref, line = refs[3 + nx_sends + ny_sends :]
     taps = taps_1d()
     edge = RADIUS * ny
     even_x = lax.axis_index("gx") % 2 == 0
@@ -370,11 +384,11 @@
         ref[RADIUS * nx :, :] = aux
 
 
-def edge_call(t, got, own_send, ny_sends, cases):
+def edge_call(t, got, own_send, behind, ny_sends, cases):
     nx, ny, depth = t.shape
     return pl.pallas_call(
         functools.partial(edge_kernel, (cases, nx, ny, depth), len(got), ny_sends),
-        in_specs=[VMEM] * (2 + len(got)),
+        in_specs=[VMEM] * (3 + len(got)),
         out_specs=[VMEM] * (ny_sends + 3),
         out_shape=[jax.ShapeDtypeStruct((RADIUS * nx + 16, depth), BF16)] * ny_sends
         + [jax.ShapeDtypeStruct((RADIUS * ny, depth), F32)] * 2
@@ -382,70 +396,57 @@
         scratch_shapes=[pltpu.VMEM((nx + 16, depth), F32)],
         compiler_params=pltpu.CompilerParams(vmem_limit_bytes=16 * MIB),
         name="edge",
-    )(t, *got, own_send)
-
-
-def plane_kernel(shape, bx, *refs):
+    )(t, *got, own_send, behind)
+
+
+def filter_row(ny, read, line, factor):
+    taps = taps_1d()
+    acc = taps[RADIUS] * read(0)
+    for d in range(1, RADIUS + 1):
+        acc = acc + taps[RADIUS + d] * (read(-d) + read(d))
+    line[8 : 8 + ny, :] = acc
+    res = taps[RADIUS] * acc
+    for d in range(1, RADIUS + 1):
+        res = res + taps[RADIUS + d] * (line[8 - d : 8 - d + ny, :] + line[8 + d : 8 + d + ny, :])
+    return res * factor
+
+
+def clear_line(line, ny):
+    zeros = jnp.zeros((8, line.shape[-1]), F32)
+    for k in range(line.shape[0]):
+        line[k, 0:8, :] = zeros
+        line[k, 8 + ny :, :] = zeros
+
+
+def inner_kernel(shape, bx, t_ref, factor_ref, out_hbm, first_ref, last_ref, line, out_ref, sem):
     nx, ny, depth = shape
-    (t_ref, xb_ref, xa_ref, factor_ref, out_hbm, first_ref, last_ref,
-     pad, line, out_ref, sem) = refs
-    taps = taps_1d()
     steps = nx // bx
-    pad[0:RADIUS] = xb_ref[...].reshape(RADIUS, ny, depth)
-    pad[RADIUS : 2 * RADIUS] = t_ref[0:RADIUS]
-    pad[2 * RADIUS : 3 * RADIUS] = t_ref[RADIUS : 2 * RADIUS]
-    tail = 3 * RADIUS
-    pad[tail : tail + 2 * RADIUS] = t_ref[nx - 2 * RADIUS : nx]
-    pad[tail + 2 * RADIUS :] = xa_ref[...].reshape(RADIUS, ny, depth)
-    zeros = jnp.zeros((8, depth), F32)
-    for slot in range(2):
-        line[slot, 0:8, :] = zeros
-        line[slot, 8 + ny :, :] = zeros
-
-    def row(ref, x, at, slot):
-        acc = taps[RADIUS] * ref[at]
-        for d in range(1, RADIUS + 1):
-            acc = acc + taps[RADIUS + d] * (ref[at - d] + ref[at + d])
-        line[slot, 8 : 8 + ny, :] = acc
-        res = taps[RADIUS] * acc
-        for d in range(1, RADIUS + 1):
-            res = res + taps[RADIUS + d] * (line[slot, 8 - d : 8 - d + ny, :] + line[slot, 8 + d : 8 + d + ny, :])
-        res = res * factor_ref[x]
-        out_ref[x] = res
-        first_ref[x] = res[0:8]
-        last_ref[x] = res[ny - 8 : ny]
-
-    copies = [
-        pltpu.make_async_copy(out_ref.at[pl.ds(s * bx, bx)], out_hbm.at[pl.ds(s * bx, bx)], sem.at[s])
-        for s in range(steps)
-    ]
+    clear_line(line, ny)
+    copies = []
     for s in range(steps):
-        lo, hi = s * bx, (s + 1) * bx
-        if s == 0:
-            for x in range(RADIUS):
-                row(pad, x, x + RADIUS, x % 2)
-            lo = RADIUS
-        if s == steps - 1:
-            for x in range(nx - RADIUS, nx):
-                row(pad, x, x - (nx - RADIUS) + tail + RADIUS, x % 2)
-            hi = nx - RADIUS
-
-        def pair(i, carry):
-            row(t_ref, i, i, i % 2)
+        lo, hi = max(s * bx, RADIUS), min((s + 1) * bx, nx - RADIUS)
+        span = pl.ds(lo, hi - lo)
+        copies.append(pltpu.make_async_copy(out_ref.at[span], out_hbm.at[span], sem.at[s]))
+
+        def row(x, carry):
+            res = filter_row(ny, lambda d: t_ref[x + d], line.at[x % 2], factor_ref[x])
+            out_ref[x] = res
+            first_ref[x] = res[0:8]
+            last_ref[x] = res[ny - 8 : ny]
             return carry
 
-        lax.fori_loop(lo, hi, pair, 0)
+        lax.fori_loop(lo, hi, row, 0)
         copies[s].start()
     for copy in copies:
         copy.wait()
 
 
-def plane_call(t, xb, xa, factor):
+def inner_call(t, factor):
     nx, ny, depth = t.shape
     bx = 8
     return pl.pallas_call(
-        functools.partial(plane_kernel, t.shape, bx),
-        in_specs=[VMEM] * 4,
+        functools.partial(inner_kernel, t.shape, bx),
+        in_specs=[VMEM] * 2,
         out_specs=[HBM, VMEM, VMEM],
         out_shape=[
             jax.ShapeDtypeStruct(t.shape, F32),
@@ -453,17 +454,61 @@
             jax.ShapeDtypeStruct((nx, 8, depth), F32),
         ],
         scratch_shapes=[
-            pltpu.VMEM((7 * RADIUS - RADIUS, ny, depth), F32),
             pltpu.VMEM((2, ny + 16, depth), F32),
             pltpu.VMEM(t.shape, F32),
             pltpu.SemaphoreType.DMA((nx // bx,)),
         ],
         compiler_params=pltpu.CompilerParams(vmem_limit_bytes=20 * MIB),
-        name="plane",
-    )(*in_vmem(t, xb, xa, factor))
-
-
-def finish_kernel(shape, cells, ngot, nextra, cases, *refs):
+        name="inner",
+    )(*in_vmem(t, factor))
+
+
+def outer_kernel(shape, t_ref, xb_ref, xa_ref, factor_ref, _, __, ___, out_hbm, first_ref, last_ref, line, pad, out_ref, sem):
+    nx, ny, depth = shape
+    clear_line(line, ny)
+    pad[0:RADIUS] = xb_ref[...].reshape(RADIUS, ny, depth)
+    pad[RADIUS : 3 * RADIUS] = t_ref[0 : 2 * RADIUS]
+    pad[3 * RADIUS : 5 * RADIUS] = t_ref[nx - 2 * RADIUS : nx]
+    pad[5 * RADIUS :] = xa_ref[...].reshape(RADIUS, ny, depth)
+    copies = []
+    for side, start in ((0, 0), (1, nx - RADIUS)):
+        for k in range(RADIUS):
+            x = start + k
+            mid = (RADIUS if side == 0 else 4 * RADIUS) + k
+            res = filter_row(ny, lambda d: pad[mid + d], line.at[x % 2], factor_ref[x])
+            out_ref[side, k] = res
+            first_ref[x] = res[0:8]
+            last_ref[x] = res[ny - 8 : ny]
+        copies.append(pltpu.make_async_copy(out_ref.at[side], out_hbm.at[pl.ds(start, RADIUS)], sem.at[side]))
+        copies[side].start()
+    for copy in copies:
+        copy.wait()
+
+
+def outer_call(t, xb, xa, factor, out, first, last):
+    nx, ny, depth = t.shape
+    return pl.pallas_call(
+        functools.partial(outer_kernel, t.shape),
+        in_specs=[VMEM] * 4 + [HBM, VMEM, VMEM],
+        out_specs=[HBM, VMEM, VMEM],
+        out_shape=[
+            jax.ShapeDtypeStruct(out.shape, F32),
+            jax.ShapeDtypeStruct(first.shape, F32),
+            jax.ShapeDtypeStruct(last.shape, F32),
+        ],
+        input_output_aliases={4: 0, 5: 1, 6: 2},
+        scratch_shapes=[
+            pltpu.VMEM((2, ny + 16, depth), F32),
+            pltpu.VMEM((6 * RADIUS, ny, depth), F32),
+            pltpu.VMEM((2, RADIUS, ny, depth), F32),
+            pltpu.SemaphoreType.DMA((2,)),
+        ],
+        compiler_params=pltpu.CompilerParams(vmem_limit_bytes=16 * MIB),
+        name="outer",
+    )(*in_vmem(t, xb, xa, factor), *in_hbm(out), *in_vmem(first, last))
+
+
+def finish_kernel(shape, cells, ngot, nextra, cases, ring, *refs):
     nx, ny, depth = shape
     got_refs = refs[:ngot]
     sums_ref = refs[ngot]
@@ -471,10 +516,13 @@
     first_ref, last_ref, factor_ref, _, out_hbm, comp_ref, strip, sem = refs[1 + ngot + nextra :]
     taps = taps_1d()
     edge = RADIUS * nx
-    even_y = lax.axis_index("gy") % 2 == 0
+    place, count = lax.axis_index("gy"), lax.axis_size("gy")
     blocks = [r[0:edge, :].astype(F32) for r in got_refs]
-    before, after = sided(even_y, blocks) if blocks else (jnp.zeros((edge, depth), F32),) * 2
+    before, after = sided(place % 2 == 0, blocks) if blocks else (jnp.zeros((edge, depth), F32),) * 2
+    before = jnp.where(place == 0, 0.0, before)
+    after = jnp.where(place == count - 1, 0.0, after)
     flat = factor_ref.reshape(nx * ny, depth)
+    copies = []
     for ref, side in ((first_ref, 0), (last_ref, 1)):
         strip[side] = ref[...]
         view = strip.at[side].reshape(nx * 8, depth)
@@ -484,31 +532,31 @@
                 if side == 0:
                     d, halo, own = y + RADIUS - k, before[k * nx : (k + 1) * nx], y
                 else:
-                    d, halo, own = k + 1 + RADIUS - 1 - y, after[k * nx : (k + 1) * nx], ny - RADIUS + y
+                    d, halo, own = k + RADIUS - y, after[k * nx : (k + 1) * nx], ny - RADIUS + y
                 if d <= RADIUS:
                     add = add + taps[RADIUS + d] * halo
             at = own if side == 0 else own - (ny - 8)
             view[pl.ds(at, nx, stride=8), :] += flat[pl.ds(own, nx, stride=ny), :] * add
-    copies = [
-        pltpu.make_async_copy(strip.at[0], out_hbm.at[:, 0:8, :], sem.at[0]),
-        pltpu.make_async_copy(strip.at[1], out_hbm.at[:, ny - 8 : ny, :], sem.at[1]),
-    ]
-    for copy in copies:
-        copy.start()
+        target = out_hbm.at[:, 0:8, :] if side == 0 else out_hbm.at[:, ny - 8 : ny, :]
+        copies.append(pltpu.make_async_copy(strip.at[side], target, sem.at[side]))
+        copies[side].start()
     total = sums_ref[...]
     for ref in extra_refs:
         total = total + ref[...]
+    if ring:
+        for ref in got_refs:
+            total = total + sum3(ref[edge : edge + 16, :].astype(F32), 0)[0:8]
     for c in range(cases):
         comp_ref[c] = total[c, 0] / cells
     for copy in copies:
         copy.wait()
 
 
-def finish_call(got, sums, extra, first, last, factor, out, cells, cases):
+def finish_call(got, sums, extra, first, last, factor, out, cells, cases, ring):
     nx, ny, depth = out.shape
     nin = len(got) + 1 + len(extra)
     return pl.pallas_call(
-        functools.partial(finish_kernel, out.shape, cells, len(got), len(extra), cases),
+        functools.partial(finish_kernel, out.shape, cells, len(got), len(extra), cases, ring),
         in_specs=[VMEM] * (nin + 3) + [HBM],
         out_specs=[HBM, SMEM],
         out_shape=[jax.ShapeDtypeStruct(out.shape, F32), jax.ShapeDtypeStruct((cases,), F32)],
@@ -545,12 +593,15 @@
     t_local, factor, umap = local_call(density, design_mask, source, decay, case_index, case_weight)
     t, *x_sends = couple_call(own, msgs, t_local, umap, max(swaps_of(gx), 1), swapped)
     x_got = [lax.ppermute(x_sends[k], "gx", swap_pairs(gx, k)) for k in range(swaps_of(gx))]
-    *y_sends, xb, xa, sums = edge_call(t, x_got, x_sends[0], swaps_of(gy), cases)
-    y_got = [lax.ppermute(y_sends[k], "gy", swap_pairs(gy, k)) for k in range(swaps_of(gy))]
-    extra = [lax.ppermute(sums, "gy", xor_pairs(gy, m)) for m in range(1, gy)]
-    partial, first, last = plane_call(t, xb, xa, factor)
+    partial, first, last = inner_call(t, factor)
+    *y_sends, xb, xa, sums = edge_call(t, x_got, x_sends[0], first, swaps_of(gy), cases)
+    ring = gy == 4
+    ends = [(0, gy - 1), (gy - 1, 0)] if ring else []
+    y_got = [lax.ppermute(y_sends[k], "gy", swap_pairs(gy, k) + (ends if k else [])) for k in range(swaps_of(gy))]
+    extra = [lax.ppermute(sums, "gy", xor_pairs(gy, m)) for m in ([2] if ring else range(1, gy))]
+    partial, first, last = outer_call(t, xb, xa, factor, partial, first, last)
     cells = nx * ny * depth * nz * gx * gy
-    return tuple(finish_call(y_got, sums, extra, first, last, factor, partial, float(cells), cases))
+    return tuple(finish_call(y_got, sums, extra, first, last, factor, partial, float(cells), cases, ring))
 
 
 def solution(mesh):

time: 35.2 us -> 29.1 us (0.83)
  the two profiles are of different devices: /device:TPU:1 before, /device:TPU:0 now
where the time goes in v4:
time: 29.1 us; the launch traced here: 29 us
  Pallas kernels  16.1 us (55%)
  starting transfers between devices  9.54 us (33%)
  waiting for transfers between devices  2.62 us (9%)
  between operations  0.7 us (2%)
    ppermute x3, starting transfers between devices, shards(): msgs = [lax.ppermute(send, 'gz', xor_pairs(nz, m)) for m in range(1, nz)]  5.78 us
    pallas_call x1, Pallas kernels, faces_call(): pl.pallas_call(functools.partial(faces_kernel, energy.shape, bx), in_spec...  5.04 us
    pallas_call x1, Pallas kernels, local_call(): pl.pallas_call(functools.partial(local_kernel, (cases, nx, ny, depth), 8)...  4.71 us
    pallas_call x1, Pallas kernels, inner_call(): pl.pallas_call(functools.partial(inner_kernel, t.shape, bx), in_specs=[VM...  2.82 us
    ppermute x1, waiting for transfers between devices, shards(): lax.ppermute(sums, 'gy', xor_pairs(gy, m))  2.22 us
    ppermute x2, starting transfers between devices, shards(): lax.ppermute(y_sends[k], 'gy', swap_pairs(gy, k) + (ends if k else []))  1.69 us
    pallas_call x1, Pallas kernels, finish_call(): pl.pallas_call(functools.partial(finish_kernel, out.shape, cells, len(got...  1.6 us
    ppermute x1, starting transfers between devices, shards(): lax.ppermute(x_sends[k], 'gx', swap_pairs(gx, k))  1.55 us
  transfers between devices with their start and end apart: 7, of which 2 were waited for; matrix products, arithmetic and copies ran while one was open for 0% of the time, Pallas kernels for 29%

profile of v4, /device:TPU:0, one launch (start us, length us, event | category | flops | bytes accessed | tf_op | source)
XLA Modules:
  0.0 29.0 jit_solution(789703882531798501)
XLA Ops:
  0.6 5.0 %faces.1 = (bf16[8,4224]{1,0:T(8,128)(2,1)S(1)}, f32[8,4224]{1,0:T(8,128)S(1)}, bf16[4096,512]{1,0:T(8,128)(2,1)S(1)}) custom-call(s32[4]{0:T(128)} %refs_0_.3, f32[16]{0:T(128)} %refs_1_.3, f32[4,128]{1,0:T(4,128)} %refs_2_.3, f32[64,64,128]{2,1,0:T(8,128)} %refs_3_.3, s32[64,64,128]{2,1,0:T(8,128)} %refs_4_.3, bf16[4,64,64,128]{3,2,1,0:T(8,128)(2,1)} %refs_5_.1), custom_call_target="tpu_custom_call" | custom-call | tf_op jit(solution)/shard_map/faces/pallas_call | solution.py:188
  5.7 5.1 %collective-permute-start.2 = (bf16[8,4224]{1,0:T(8,128)(2,1)S(1)}, bf16[8,4224]{1,0:T(8,128)(2,1)S(1)}, u32[]{:S(2)}, u32[]{:S(2)}) collective-permute-start(bf16[8,4224]{1,0:T(8,128)(2,1)S(1)} %get-tuple-element.22), channel_id=1, source_target_pairs={{0,24},{8,16},{16,8},{24,0},{1,25},{9,17},{17,9},{25,1},{2,26},{10... | collective-permute-start | bytes 202760 | tf_op jit(solution)/shard_map/ppermute | solution.py:589
  10.8 0.0 collective-permute-start.1
  10.8 0.6 %collective-permute-start = (bf16[8,4224]{1,0:T(8,128)(2,1)S(1)}, bf16[8,4224]{1,0:T(8,128)(2,1)S(1)}, u32[]{:S(2)}, u32[]{:S(2)}) collective-permute-start(bf16[8,4224]{1,0:T(8,128)(2,1)S(1)} %get-tuple-element.22), channel_id=1, source_target_pairs={{0,8},{8,0},{16,24},{24,16},{1,9},{9,1},{17,25},{25,17},{2,10},{10... | collective-permute-start | bytes 202760 | tf_op jit(solution)/shard_map/ppermute | solution.py:589
  11.5 4.7 %local.1 = (f32[64,64,128]{2,1,0:T(8,128)S(1)}, f32[64,64,128]{2,1,0:T(8,128)S(1)}, bf16[32,128]{1,0:T(8,128)(2,1)S(1)}) custom-call(s32[4]{0:T(128)} %refs_0_.3, f32[16]{0:T(128)} %refs_1_.3, f32[4,128]{1,0:T(4,128)} %refs_2_.3, f32[64,64,128]{2,1,0:T(8,128)} %refs_3_.3, s32[64,64,128]{2,1,0:T(8,128)} %refs_4_.3, ...), custom_call_target="tpu_custom_call" | custom-call | tf_op jit(solution)/shard_map/local/pallas_call | solution.py:261
  16.2 0.0 collective-permute-done.2.refs_3_
  16.2 0.4 %collective-permute-done.1.refs_2_ = bf16[8,4224]{1,0:T(8,128)(2,1)S(1)} collective-permute-done((bf16[8,4224]{1,0:T(8,128)(2,1)S(1)}, bf16[8,4224]{1,0:T(8,128)(2,1)S(1)}, u32[]{:S(2)}, u32[]{:S(2)}) %collective-permute-start.1) | collective-permute-done | bytes 67616 | tf_op jit(solution)/shard_map/ppermute | solution.py:589
  16.6 0.0 collective-permute-done.refs_1_
  16.6 0.7 %couple.1 = (f32[64,64,128]{2,1,0:T(8,128)S(1)}, bf16[208,128]{1,0:T(8,128)(2,1)S(1)}) custom-call(f32[8,4224]{1,0:T(8,128)S(1)} %get-tuple-element.21.refs_0_, bf16[8,4224]{1,0:T(8,128)(2,1)S(1)} %collective-permute-done.refs_1_, bf16[8,4224]{1,0:T(8,128)(2,1)S(1)} %collective-permute-done.1.refs_2_, bf16[8,4224]{1,0:T(8,128)(2,1)S(1)} %collective-permute-done.2.refs_3_, ...), custom_call_target="tpu_custom_call" | custom-call | tf_op jit(solution)/shard_map/couple/pallas_call | solution.py:330
  17.3 1.6 %collective-permute-start.3 = (bf16[208,128]{1,0:T(8,128)(2,1)S(1)}, bf16[208,128]{1,0:T(8,128)(2,1)S(1)}, u32[]{:S(2)}, u32[]{:S(2)}) collective-permute-start(bf16[208,128]{1,0:T(8,128)(2,1)S(1)} %get-tuple-element.27.refs_2_), channel_id=1, source_target_pairs={{0,4},{4,0},{1,5},{5,1},{2,6},{6,2},{3,7},{7,3},{8,12},{12,8},{9,1... | collective-permute-start | bytes 159752 | tf_op jit(solution)/shard_map/ppermute | solution.py:595
  18.9 2.8 %inner.1 = (f32[64,64,128]{2,1,0:T(8,128)}, f32[64,8,128]{2,1,0:T(8,128)S(1)}, f32[64,8,128]{2,1,0:T(8,128)S(1)}) custom-call(f32[64,64,128]{2,1,0:T(8,128)S(1)} %get-tuple-element.26.t_ref.refs_0_, f32[64,64,128]{2,1,0:T(8,128)S(1)} %get-tuple-element.28.factor_ref.refs_6_), custom_call_target="tpu_custom_call" | custom-call | tf_op jit(solution)/shard_map/inner/pallas_call | solution.py:447
  21.7 0.0 collective-permute-done.3.refs_1_
  21.7 0.4 %edge.1 = (bf16[208,128]{1,0:T(8,128)(2,1)S(1)}, bf16[208,128]{1,0:T(8,128)(2,1)S(1)}, f32[192,128]{1,0:T(8,128)S(1)}, f32[192,128]{1,0:T(8,128)S(1)}, f32[8,128]{1,0:T(8,128)S(1)}) custom-call(f32[64,64,128]{2,1,0:T(8,128)S(1)} %get-tuple-element.26.t_ref.refs_0_, bf16[208,128]{1,0:T(8,128)(2,1)S(1)} %collective-permute-done.3.refs_1_, ...), custom_call_target="tpu_custom_call" | custom-call | tf_op jit(solution)/shard_map/edge/pallas_call | solution.py:389
  22.1 0.1 collective-permute-start.4
  22.1 1.6 %collective-permute-start.5 = (bf16[208,128]{1,0:T(8,128)(2,1)S(1)}, bf16[208,128]{1,0:T(8,128)(2,1)S(1)}, u32[]{:S(2)}, u32[]{:S(2)}) collective-permute-start(bf16[208,128]{1,0:T(8,128)(2,1)S(1)} %get-tuple-element.31), channel_id=1, source_target_pairs={{1,2},{2,1},{0,3},{3,0},{5,6},{6,5},{4,7},{7,4},{9,10},{10,9},{8,1... | collective-permute-start | bytes 159752 | tf_op jit(solution)/shard_map/ppermute | solution.py:600
  23.8 0.5 %collective-permute-start.6 = (f32[8,128]{1,0:T(8,128)S(1)}, f32[8,128]{1,0:T(8,128)S(1)}, u32[]{:S(2)}, u32[]{:S(2)}) collective-permute-start(f32[8,128]{1,0:T(8,128)S(1)} %get-tuple-element.32.refs_2_), channel_id=1, source_target_pairs={{0,2},{1,3},{2,0},{3,1},{4,6},{5,7},{6,4},{7,5},{8,10},{9,11},{10,... | collective-permute-start | bytes 12296 | tf_op jit(solution)/shard_map/ppermute | solution.py:601
  24.3 0.9 %outer.1 = (f32[64,64,128]{2,1,0:T(8,128)}, f32[64,8,128]{2,1,0:T(8,128)S(1)}, f32[64,8,128]{2,1,0:T(8,128)S(1)}) custom-call(f32[64,64,128]{2,1,0:T(8,128)S(1)} %get-tuple-element.26.t_ref.refs_0_, f32[192,128]{1,0:T(8,128)S(1)} %get-tuple-element.33.xb_ref, ...), custom_call_target="tpu_custom_call", output_to_operand_aliasing={{0}: (4, {}), {1}: (5, {}), {2}: (6, {})} | custom-call | tf_op jit(solution)/shard_map/outer/pallas_call | solution.py:490
  25.1 2.2 %collective-permute-done.6.refs_3_ = f32[8,128]{1,0:T(8,128)S(1)} collective-permute-done((f32[8,128]{1,0:T(8,128)S(1)}, f32[8,128]{1,0:T(8,128)S(1)}, u32[]{:S(2)}, u32[]{:S(2)}) %collective-permute-start.6) | collective-permute-done | bytes 4128 | tf_op jit(solution)/shard_map/ppermute | solution.py:601
  27.4 0.0 collective-permute-done.4.refs_0_
  27.4 0.0 collective-permute-done.5.refs_1_
  27.4 1.6 %finish.1 = (f32[64,64,128]{2,1,0:T(8,128)}, f32[4]{0:T(128)}) custom-call(bf16[208,128]{1,0:T(8,128)(2,1)S(1)} %collective-permute-done.4.refs_0_, bf16[208,128]{1,0:T(8,128)(2,1)S(1)} %collective-permute-done.5.refs_1_, f32[8,128]{1,0:T(8,128)S(1)} %get-tuple-element.32.refs_2_, ...), custom_call_target="tpu_custom_call", output_to_operand_aliasing={{0}: (7, {})} | custom-call | tf_op jit(solution)/shard_map/finish/pallas_call | solution.py:558
Async XLA Ops:
  5.7 10.5 %collective-permute-start.2 = (bf16[8,4224]{1,0:T(8,128)(2,1)S(1)}, bf16[8,4224]{1,0:T(8,128)(2,1)S(1)}, u32[]{:S(2)}, u32[]{:S(2)}) collective-permute-start(bf16[8,4224]{1,0:T(8,128)(2,1)S(1)} %get-tuple-element.22), channel_id=1, source_target_pairs={{0,24},{8,16},{16,8},{24,0},{1,25},{9,17},{17,9},{25,1},{2,26},{10... | collective-permute-start | bytes 202760 | tf_op jit(solution)/shard_map/ppermute | solution.py:589
  10.8 5.8 %collective-permute-start.1 = (bf16[8,4224]{1,0:T(8,128)(2,1)S(1)}, bf16[8,4224]{1,0:T(8,128)(2,1)S(1)}, u32[]{:S(2)}, u32[]{:S(2)}) collective-permute-start(bf16[8,4224]{1,0:T(8,128)(2,1)S(1)} %get-tuple-element.22), channel_id=1, source_target_pairs={{0,16},{8,24},{16,0},{24,8},{1,17},{9,25},{17,1},{25,9},{2,18},{10... | collective-permute-start | bytes 202760 | tf_op jit(solution)/shard_map/ppermute | solution.py:589
  10.8 5.8 %collective-permute-start = (bf16[8,4224]{1,0:T(8,128)(2,1)S(1)}, bf16[8,4224]{1,0:T(8,128)(2,1)S(1)}, u32[]{:S(2)}, u32[]{:S(2)}) collective-permute-start(bf16[8,4224]{1,0:T(8,128)(2,1)S(1)} %get-tuple-element.22), channel_id=1, source_target_pairs={{0,8},{8,0},{16,24},{24,16},{1,9},{9,1},{17,25},{25,17},{2,10},{10... | collective-permute-start | bytes 202760 | tf_op jit(solution)/shard_map/ppermute | solution.py:589
  17.3 4.4 %collective-permute-start.3 = (bf16[208,128]{1,0:T(8,128)(2,1)S(1)}, bf16[208,128]{1,0:T(8,128)(2,1)S(1)}, u32[]{:S(2)}, u32[]{:S(2)}) collective-permute-start(bf16[208,128]{1,0:T(8,128)(2,1)S(1)} %get-tuple-element.27.refs_2_), channel_id=1, source_target_pairs={{0,4},{4,0},{1,5},{5,1},{2,6},{6,2},{3,7},{7,3},{8,12},{12,8},{9,1... | collective-permute-start | bytes 159752 | tf_op jit(solution)/shard_map/ppermute | solution.py:595
  22.1 5.3 %collective-permute-start.4 = (bf16[208,128]{1,0:T(8,128)(2,1)S(1)}, bf16[208,128]{1,0:T(8,128)(2,1)S(1)}, u32[]{:S(2)}, u32[]{:S(2)}) collective-permute-start(bf16[208,128]{1,0:T(8,128)(2,1)S(1)} %get-tuple-element.30), channel_id=1, source_target_pairs={{0,1},{1,0},{2,3},{3,2},{4,5},{5,4},{6,7},{7,6},{8,9},{9,8},{10,11... | collective-permute-start | bytes 159752 | tf_op jit(solution)/shard_map/ppermute | solution.py:600
  22.1 5.2 %collective-permute-start.5 = (bf16[208,128]{1,0:T(8,128)(2,1)S(1)}, bf16[208,128]{1,0:T(8,128)(2,1)S(1)}, u32[]{:S(2)}, u32[]{:S(2)}) collective-permute-start(bf16[208,128]{1,0:T(8,128)(2,1)S(1)} %get-tuple-element.31), channel_id=1, source_target_pairs={{1,2},{2,1},{0,3},{3,0},{5,6},{6,5},{4,7},{7,4},{9,10},{10,9},{8,1... | collective-permute-start | bytes 159752 | tf_op jit(solution)/shard_map/ppermute | solution.py:600
  23.8 3.6 %collective-permute-start.6 = (f32[8,128]{1,0:T(8,128)S(1)}, f32[8,128]{1,0:T(8,128)S(1)}, u32[]{:S(2)}, u32[]{:S(2)}) collective-permute-start(f32[8,128]{1,0:T(8,128)S(1)} %get-tuple-element.32.refs_2_), channel_id=1, source_target_pairs={{0,2},{1,3},{2,0},{3,1},{4,6},{5,7},{6,4},{7,5},{8,10},{9,11},{10,... | collective-permute-start | bytes 12296 | tf_op jit(solution)/shard_map/ppermute | solution.py:601

commit v5 on v4

--- a/solution.py
+++ b/solution.py
@@ -85,11 +85,6 @@
         weight = jnp.exp(jnp.minimum(gap, 0.0)) * self.keep_t[:, c : c + 1]
         return jnp.where(self.col >= self.row, weight, 0.0)
 
-    def backward_t(self, c):
-        gap = self.up_ex_t[:, c : c + 1] - self.up_ex[c : c + 1, :]
-        weight = jnp.exp(jnp.minimum(gap, 0.0)) * self.keep_t[:, c : c + 1]
-        return jnp.where(self.col <= self.row, weight, 0.0)
-
 
 def case_scale(weight_ref, index_ref, c):
     return -3.0 * weight_ref[index_ref[c]]
@@ -98,8 +93,8 @@
 def faces_kernel(shape, bx, *refs):
     cases, nx, ny, depth = shape
     (index_hbm, weight_hbm, decay_hbm, density_hbm, mask_hbm, energy_hbm,
-     send_ref, own_ref, source_ref,
-     index_ref, weight_ref, decay_ref, density_ref, mask_ref, energy_ref, small_sem, sem) = refs
+     send_ref, own_ref, source_ref, density_ref, mask_ref, map_ref, rows_ref,
+     index_ref, weight_ref, decay_ref, energy_ref, small_sem, sem) = refs
     steps, cols = nx // bx, bx * ny
     small = [
         pltpu.make_async_copy(decay_hbm, decay_ref, small_sem.at[0]),
@@ -131,17 +126,19 @@
     e_rows, h_rows, turns = [], [], []
     for c in range(cases):
         scale = case_scale(weight_ref, index_ref, c)
-        f_t = slab.forward_t(c)
+        f_t = slab.forward_t(c) * scale
+        map_ref[c] = f_t
         keep = 1.0 - decay[c : c + 1, :]
-        e_row = jnp.exp(slab.total[c : c + 1] - slab.up[c : c + 1, :]) * keep
+        e_row = jnp.exp(slab.total[c : c + 1] - slab.up[c : c + 1, :]) * keep * scale
         b_row = jnp.exp(slab.up_ex[c : c + 1, :]) * keep
         h_row = dot_high(b_row, f_t, ((1,), (1,)))
         turns.append(jnp.sum(b_row * jnp.exp(slab.up[c : c + 1, :]), axis=1, keepdims=True))
-        place = lambda r: jnp.concatenate([zero_row] * c + [r * scale] + [zero_row] * (cases - 1 - c), axis=1)
+        place = lambda r: jnp.concatenate([zero_row] * c + [r] + [zero_row] * (cases - 1 - c), axis=1)
         e_rows.append(place(e_row))
         h_rows.append(place(h_row))
     w_hi, w_lo = split2(jnp.concatenate(e_rows + h_rows, axis=0))
     wmat = jnp.concatenate([w_hi, w_lo], axis=0)
+    rows_ref[...] = jnp.concatenate([pad_rows(v, 8) for v in (slab.up, slab.up_ex, 1.0 - decay)], axis=0)
 
     sums = [jnp.zeros((8, depth), F32) for _ in range(cases)]
 
@@ -188,18 +185,20 @@
     return pl.pallas_call(
         functools.partial(faces_kernel, energy.shape, bx),
         in_specs=[HBM] * 6,
-        out_specs=[VMEM] * 3,
+        out_specs=[VMEM] * 7,
         out_shape=[
             pltpu.VMEM((2 * cases, width), BF16),
             pltpu.VMEM((2 * cases, width), F32),
             pltpu.VMEM((nx * ny, cases * depth), BF16),
+            pltpu.VMEM(density.shape, F32),
+            pltpu.VMEM(density.shape, jnp.int32),
+            pltpu.VMEM((cases, depth, depth), F32),
+            pltpu.VMEM((24, depth), F32),
         ],
         scratch_shapes=[
             pltpu.SMEM(case_index.shape, case_index.dtype),
             pltpu.SMEM(case_weight.shape, F32),
             pltpu.VMEM(decay.shape, F32),
-            pltpu.VMEM(density.shape, F32),
-            pltpu.VMEM(density.shape, jnp.int32),
             pltpu.VMEM(energy.shape, BF16),
             pltpu.SemaphoreType.DMA((3,)),
             pltpu.SemaphoreType.DMA((3, nx // bx)),
@@ -209,88 +208,66 @@
     )(*in_hbm(case_index, case_weight, decay, density, design_mask, energy))
 
 
-def local_kernel(shape, bx, *refs):
+def local_kernel(shape, bx, source_ref, density_ref, mask_ref, map_ref, rows_ref, t_ref, factor_ref, umap_ref, rmat):
     cases, nx, ny, depth = shape
-    (index_hbm, weight_hbm, decay_hbm, density_hbm, mask_hbm, source_ref,
-     t_ref, factor_ref, umap_ref,
-     index_ref, weight_ref, decay_ref, mask_ref, rmat, small_sem, sem) = refs
     steps, cols = nx // bx, bx * ny
-    small = [
-        pltpu.make_async_copy(decay_hbm, decay_ref, small_sem.at[0]),
-        pltpu.make_async_copy(index_hbm, index_ref, small_sem.at[1]),
-        pltpu.make_async_copy(weight_hbm, weight_ref, small_sem.at[2]),
-    ]
-    big = [
-        pltpu.make_async_copy(density_hbm, factor_ref, sem.at[0]),
-        pltpu.make_async_copy(mask_hbm, mask_ref, sem.at[1]),
-    ]
-    for copy in small + big:
-        copy.start()
-    for copy in small:
-        copy.wait()
-    slab = Slab(decay_ref[...])
-    a_rows, c_rows = [], []
+    row = lax.broadcasted_iota(jnp.int32, (depth, depth), 0)
+    col = lax.broadcasted_iota(jnp.int32, (depth, depth), 1)
+    up, up_ex = rows_ref[0:8, :], rows_ref[8:16, :]
+    up_ex_t, keep_t = jnp.transpose(up_ex), jnp.transpose(rows_ref[16:24, :])
+    total = up[:, depth - 1 : depth]
+    lead = jnp.exp(up)
+    a_rows = []
     for c in range(cases):
-        f_t, b_t = slab.forward_t(c), slab.backward_t(c)
-        hi, lo = split2(dot_high(f_t, b_t) * case_scale(weight_ref, index_ref, c))
+        gap = up_ex_t[:, c : c + 1] - up_ex[c : c + 1, :]
+        weight = jnp.exp(jnp.minimum(gap, 0.0)) * keep_t[:, c : c + 1]
+        b_t = jnp.where(col <= row, weight, 0.0)
+        both = dot_high(jnp.concatenate([map_ref[c], lead], axis=0), b_t)
+        hi, lo = split2(both[0:depth])
         rmat[c * depth : (c + 1) * depth, 0:depth] = hi
         rmat[c * depth : (c + 1) * depth, depth : 2 * depth] = lo
-        a_rows.append(dot_high(jnp.exp(slab.up[c : c + 1, :]), b_t))
-        c_rows.append(jnp.exp(slab.total[c : c + 1] - slab.up_ex[c : c + 1, :]))
-    u_all = jnp.concatenate(a_rows + c_rows, axis=0)
+        a_rows.append(both[depth + c : depth + c + 1])
+    u_all = jnp.concatenate(a_rows + [jnp.exp(total - up_ex)[0:cases]], axis=0)
     u_hi = u_all.astype(BF16).astype(F32)
     umap_ref[...] = jnp.concatenate([u_hi, u_hi, u_all - u_hi, jnp.zeros_like(u_hi)], axis=0).astype(BF16)
-    for copy in big:
-        copy.wait()
-
-    def one(s, carry):
-        span = pl.ds(pl.multiple_of(s * cols, cols), cols)
+
+    for s in range(steps):
         both = lax.dot_general(
-            source_ref[span, :], rmat[...], (((1,), (0,)), ((), ())), preferred_element_type=F32)
-        at = pl.ds(s * bx, bx)
+            source_ref[s * cols : (s + 1) * cols, :], rmat[...], (((1,), (0,)), ((), ())),
+            preferred_element_type=F32)
+        at = slice(s * bx, (s + 1) * bx)
         t_ref[at] = (both[:, 0:depth] + both[:, depth : 2 * depth]).reshape(bx, ny, depth)
-        factor_ref[at] = jnp.where(mask_ref[at] == 0, 1.0 / jnp.maximum(factor_ref[at], 0.1), 0.0)
-        return carry
-
-    lax.fori_loop(0, steps, one, 0)
-
-
-def local_call(density, design_mask, source, decay, case_index, case_weight):
+        factor_ref[at] = jnp.where(mask_ref[at] == 0, 1.0 / jnp.maximum(density_ref[at], 0.1), 0.0)
+
+
+def local_call(source, density, mask, maps, rows):
     nx, ny, depth = density.shape
-    cases = decay.shape[0]
-    return pl.pallas_call(
-        functools.partial(local_kernel, (cases, nx, ny, depth), 8),
-        in_specs=[HBM] * 5 + [VMEM],
+    cases = maps.shape[0]
+    return pl.pallas_call(
+        functools.partial(local_kernel, (cases, nx, ny, depth), 16),
+        in_specs=[VMEM] * 5,
         out_specs=[VMEM] * 3,
         out_shape=[
             pltpu.VMEM(density.shape, F32),
             pltpu.VMEM(density.shape, F32),
             pltpu.VMEM((8 * cases, depth), BF16),
         ],
-        scratch_shapes=[
-            pltpu.SMEM(case_index.shape, case_index.dtype),
-            pltpu.SMEM(case_weight.shape, F32),
-            pltpu.VMEM(decay.shape, F32),
-            pltpu.VMEM(density.shape, jnp.int32),
-            pltpu.VMEM((cases * depth, 2 * depth), BF16),
-            pltpu.SemaphoreType.DMA((3,)),
-            pltpu.SemaphoreType.DMA((2,)),
-        ],
-        compiler_params=pltpu.CompilerParams(vmem_limit_bytes=20 * MIB),
+        scratch_shapes=[pltpu.VMEM((cases * depth, 2 * depth), BF16)],
+        compiler_params=pltpu.CompilerParams(vmem_limit_bytes=16 * MIB),
         name="local",
-    )(*in_hbm(case_index, case_weight, decay, density, design_mask), *in_vmem(source))
-
-
-def couple_kernel(shape, nslabs, nsends, swapped, *refs):
+    )(*in_vmem(source, density, mask, maps, rows))
+
+
+def head_kernel(shape, nslabs, nsends, swapped, *refs):
     cases, nx, ny, depth = shape
     own_ref = refs[0]
     msgs = refs[1:nslabs]
-    t_ref, umap_ref, out_ref = refs[nslabs : 3 + nslabs]
+    t_ref, umap_ref, lhs_ref = refs[nslabs : 3 + nslabs]
     sends = refs[3 + nslabs : 3 + nslabs + nsends]
     stack = refs[-1]
     cols = nx * ny
     mine = lax.axis_index("gz")
-    high = (1 - lax.axis_index("gx") % 2) * (nx - RADIUS)
+    low = lax.axis_index("gx") % 2 == 1
     stack[0] = own_ref[...].astype(F32)
     for m, msg in enumerate(msgs):
         stack[m + 1] = msg[...].astype(F32)
@@ -313,29 +290,33 @@
         state = tops[j] + gains[j] * state
     faces = jnp.concatenate([entering, above], axis=0)
     hi = faces.astype(BF16).astype(F32)
-    lhs = jnp.concatenate([hi, faces - hi, hi, jnp.zeros_like(hi)], axis=0).astype(BF16)
-    add = lax.dot_general(lhs, umap_ref[...], (((0,), (0,)), ((), ())), preferred_element_type=F32)
-    out_ref[...] = t_ref[...] + add.reshape(nx, ny, depth)
+    lhs_ref[...] = jnp.concatenate([hi, faces - hi, hi, jnp.zeros_like(hi)], axis=0).astype(BF16)
     aux = pad_rows(put_lanes(split3(total)), 16).astype(BF16)
+    rows = RADIUS + 1
+    wide, edge = rows * ny, RADIUS * ny
     for k, ref in enumerate(sends):
-        edge = out_ref[pl.ds(high if k == 0 else nx - RADIUS - high, RADIUS)]
-        ref[0 : RADIUS * ny, :] = edge.reshape(RADIUS * ny, depth).astype(BF16)
-        ref[RADIUS * ny :, :] = aux
-
-
-def couple_call(own, msgs, t_local, umap, nsends, swapped):
+        bottom = low if k == 0 else jnp.logical_not(low)
+        start = jnp.where(bottom, 0, nx - rows)
+        part = lhs_ref[:, pl.ds(pl.multiple_of(start * ny, wide), wide)]
+        add = lax.dot_general(part, umap_ref[...], (((0,), (0,)), ((), ())), preferred_element_type=F32)
+        full = t_ref[pl.ds(start, rows)].reshape(wide, depth) + add
+        ref[0:edge, :] = jnp.where(bottom, full[0:edge], full[ny:wide]).astype(BF16)
+        ref[edge:, :] = aux
+
+
+def head_call(own, msgs, t_local, umap, nsends, swapped):
     nx, ny, depth = t_local.shape
     cases = own.shape[0] // 2
     nslabs = len(msgs) + 1
     return pl.pallas_call(
-        functools.partial(couple_kernel, (cases, nx, ny, depth), nslabs, nsends, swapped),
+        functools.partial(head_kernel, (cases, nx, ny, depth), nslabs, nsends, swapped),
         in_specs=[VMEM] * (nslabs + 2),
         out_specs=[VMEM] * (1 + nsends),
-        out_shape=[jax.ShapeDtypeStruct(t_local.shape, F32)]
+        out_shape=[pltpu.VMEM((8 * cases, nx * ny), BF16)]
         + [jax.ShapeDtypeStruct((RADIUS * ny + 16, depth), BF16)] * nsends,
         scratch_shapes=[pltpu.VMEM((nslabs,) + own.shape, F32)],
-        compiler_params=pltpu.CompilerParams(vmem_limit_bytes=28 * MIB),
-        name="couple",
+        compiler_params=pltpu.CompilerParams(vmem_limit_bytes=20 * MIB),
+        name="head",
     )(own, *msgs, *in_vmem(t_local), umap)
 
 
@@ -350,8 +331,8 @@
     t_ref = refs[0]
     got_refs = refs[1 : 1 + nx_sends]
     own_send = refs[1 + nx_sends]
-    sends = refs[3 + nx_sends : 3 + nx_sends + ny_sends]
-    xb_ref, xa_ref, sums_ref, line = refs[3 + nx_sends + ny_sends :]
+    sends = refs[2 + nx_sends : 2 + nx_sends + ny_sends]
+    xb_ref, xa_ref, sums_ref, line = refs[2 + nx_sends + ny_sends :]
     taps = taps_1d()
     edge = RADIUS * ny
     even_x = lax.axis_index("gx") % 2 == 0
@@ -384,11 +365,11 @@
         ref[RADIUS * nx :, :] = aux
 
 
-def edge_call(t, got, own_send, behind, ny_sends, cases):
+def edge_call(t, got, own_send, ny_sends, cases):
     nx, ny, depth = t.shape
     return pl.pallas_call(
         functools.partial(edge_kernel, (cases, nx, ny, depth), len(got), ny_sends),
-        in_specs=[VMEM] * (3 + len(got)),
+        in_specs=[VMEM] * (2 + len(got)),
         out_specs=[VMEM] * (ny_sends + 3),
         out_shape=[jax.ShapeDtypeStruct((RADIUS * nx + 16, depth), BF16)] * ny_sends
         + [jax.ShapeDtypeStruct((RADIUS * ny, depth), F32)] * 2
@@ -396,7 +377,7 @@
         scratch_shapes=[pltpu.VMEM((nx + 16, depth), F32)],
         compiler_params=pltpu.CompilerParams(vmem_limit_bytes=16 * MIB),
         name="edge",
-    )(t, *got, own_send, behind)
+    )(t, *got, own_send)
 
 
 def filter_row(ny, read, line, factor):
@@ -418,52 +399,66 @@
         line[k, 8 + ny :, :] = zeros
 
 
-def inner_kernel(shape, bx, t_ref, factor_ref, out_hbm, first_ref, last_ref, line, out_ref, sem):
+def filter_rows(lo, hi, chunk, read, line, factor_ref, first_ref, last_ref, out_ref, out_hbm, sem):
+    ny = factor_ref.shape[1]
+    copies = []
+
+    def row(x, carry):
+        res = filter_row(ny, lambda d: read(x + d), line.at[x % 2], factor_ref[x])
+        out_ref[x] = res
+        first_ref[x] = res[0:8]
+        last_ref[x] = res[ny - 8 : ny]
+        return carry
+
+    for s, start in enumerate(range(lo, hi, chunk)):
+        stop = min(start + chunk, hi)
+        lax.fori_loop(start, stop, row, 0)
+        span = pl.ds(start, stop - start)
+        copies.append(pltpu.make_async_copy(out_ref.at[span], out_hbm.at[span], sem.at[s]))
+        copies[s].start()
+    return copies
+
+
+def split_row(nx):
+    return nx * 9 // 16
+
+
+def body_kernel(shape, chunk, lhs_ref, umap_ref, part_ref, factor_ref, t_ref, out_hbm, first_ref, last_ref, line, out_ref, sem):
     nx, ny, depth = shape
-    steps = nx // bx
+    add = lax.dot_general(lhs_ref[...], umap_ref[...], (((0,), (0,)), ((), ())), preferred_element_type=F32)
+    t_ref[...] = part_ref[...] + add.reshape(nx, ny, depth)
     clear_line(line, ny)
-    copies = []
-    for s in range(steps):
-        lo, hi = max(s * bx, RADIUS), min((s + 1) * bx, nx - RADIUS)
-        span = pl.ds(lo, hi - lo)
-        copies.append(pltpu.make_async_copy(out_ref.at[span], out_hbm.at[span], sem.at[s]))
-
-        def row(x, carry):
-            res = filter_row(ny, lambda d: t_ref[x + d], line.at[x % 2], factor_ref[x])
-            out_ref[x] = res
-            first_ref[x] = res[0:8]
-            last_ref[x] = res[ny - 8 : ny]
-            return carry
-
-        lax.fori_loop(lo, hi, row, 0)
-        copies[s].start()
+    copies = filter_rows(
+        RADIUS, split_row(nx), chunk, lambda x: t_ref[x], line, factor_ref, first_ref, last_ref, out_ref, out_hbm, sem)
     for copy in copies:
         copy.wait()
 
 
-def inner_call(t, factor):
-    nx, ny, depth = t.shape
-    bx = 8
-    return pl.pallas_call(
-        functools.partial(inner_kernel, t.shape, bx),
-        in_specs=[VMEM] * 2,
-        out_specs=[HBM, VMEM, VMEM],
+def body_call(lhs, umap, part, factor):
+    nx, ny, depth = part.shape
+    chunk = 11
+    return pl.pallas_call(
+        functools.partial(body_kernel, part.shape, chunk),
+        in_specs=[VMEM] * 4,
+        out_specs=[VMEM, HBM, VMEM, VMEM],
         out_shape=[
-            jax.ShapeDtypeStruct(t.shape, F32),
-            jax.ShapeDtypeStruct((nx, 8, depth), F32),
-            jax.ShapeDtypeStruct((nx, 8, depth), F32),
+            pltpu.VMEM(part.shape, F32),
+            jax.ShapeDtypeStruct(part.shape, F32),
+            pltpu.VMEM((nx, 8, depth), F32),
+            pltpu.VMEM((nx, 8, depth), F32),
         ],
         scratch_shapes=[
             pltpu.VMEM((2, ny + 16, depth), F32),
-            pltpu.VMEM(t.shape, F32),
-            pltpu.SemaphoreType.DMA((nx // bx,)),
+            pltpu.VMEM(part.shape, F32),
+            pltpu.SemaphoreType.DMA((-(-nx // chunk),)),
         ],
         compiler_params=pltpu.CompilerParams(vmem_limit_bytes=20 * MIB),
-        name="inner",
-    )(*in_vmem(t, factor))
-
-
-def outer_kernel(shape, t_ref, xb_ref, xa_ref, factor_ref, _, __, ___, out_hbm, first_ref, last_ref, line, pad, out_ref, sem):
+        name="body",
+    )(*in_vmem(lhs, umap, part, factor))
+
+
+def rest_kernel(shape, chunk, t_ref, xb_ref, xa_ref, factor_ref, _, __, ___, out_hbm, first_ref, last_ref,
+                line, pad, out_ref, sem, side_sem):
     nx, ny, depth = shape
     clear_line(line, ny)
     pad[0:RADIUS] = xb_ref[...].reshape(RADIUS, ny, depth)
@@ -476,44 +471,47 @@
             x = start + k
             mid = (RADIUS if side == 0 else 4 * RADIUS) + k
             res = filter_row(ny, lambda d: pad[mid + d], line.at[x % 2], factor_ref[x])
-            out_ref[side, k] = res
+            out_ref[x] = res
             first_ref[x] = res[0:8]
             last_ref[x] = res[ny - 8 : ny]
-        copies.append(pltpu.make_async_copy(out_ref.at[side], out_hbm.at[pl.ds(start, RADIUS)], sem.at[side]))
+        span = pl.ds(start, RADIUS)
+        copies.append(pltpu.make_async_copy(out_ref.at[span], out_hbm.at[span], side_sem.at[side]))
         copies[side].start()
+    copies += filter_rows(
+        split_row(nx), nx - RADIUS, chunk, lambda x: t_ref[x], line, factor_ref, first_ref, last_ref, out_ref, out_hbm, sem)
     for copy in copies:
         copy.wait()
 
 
-def outer_call(t, xb, xa, factor, out, first, last):
+def rest_call(t, xb, xa, factor, out, first, last):
     nx, ny, depth = t.shape
-    return pl.pallas_call(
-        functools.partial(outer_kernel, t.shape),
+    chunk = 9
+    return pl.pallas_call(
+        functools.partial(rest_kernel, t.shape, chunk),
         in_specs=[VMEM] * 4 + [HBM, VMEM, VMEM],
         out_specs=[HBM, VMEM, VMEM],
         out_shape=[
             jax.ShapeDtypeStruct(out.shape, F32),
-            jax.ShapeDtypeStruct(first.shape, F32),
-            jax.ShapeDtypeStruct(last.shape, F32),
+            pltpu.VMEM(first.shape, F32),
+            pltpu.VMEM(last.shape, F32),
         ],
         input_output_aliases={4: 0, 5: 1, 6: 2},
         scratch_shapes=[
             pltpu.VMEM((2, ny + 16, depth), F32),
             pltpu.VMEM((6 * RADIUS, ny, depth), F32),
-            pltpu.VMEM((2, RADIUS, ny, depth), F32),
+            pltpu.VMEM(t.shape, F32),
+            pltpu.SemaphoreType.DMA((-(-nx // chunk),)),
             pltpu.SemaphoreType.DMA((2,)),
         ],
-        compiler_params=pltpu.CompilerParams(vmem_limit_bytes=16 * MIB),
-        name="outer",
+        compiler_params=pltpu.CompilerParams(vmem_limit_bytes=20 * MIB),
+        name="rest",
     )(*in_vmem(t, xb, xa, factor), *in_hbm(out), *in_vmem(first, last))
 
 
-def finish_kernel(shape, cells, ngot, nextra, cases, ring, *refs):
+def finish_kernel(shape, ngot, *refs):
     nx, ny, depth = shape
     got_refs = refs[:ngot]
-    sums_ref = refs[ngot]
-    extra_refs = refs[1 + ngot : 1 + ngot + nextra]
-    first_ref, last_ref, factor_ref, _, out_hbm, comp_ref, strip, sem = refs[1 + ngot + nextra :]
+    first_ref, last_ref, factor_ref, _, out_hbm, done_ref, strip, sem = refs[ngot:]
     taps = taps_1d()
     edge = RADIUS * nx
     place, count = lax.axis_index("gy"), lax.axis_size("gy")
@@ -540,31 +538,44 @@
         target = out_hbm.at[:, 0:8, :] if side == 0 else out_hbm.at[:, ny - 8 : ny, :]
         copies.append(pltpu.make_async_copy(strip.at[side], target, sem.at[side]))
         copies[side].start()
-    total = sums_ref[...]
-    for ref in extra_refs:
-        total = total + ref[...]
-    if ring:
-        for ref in got_refs:
-            total = total + sum3(ref[edge : edge + 16, :].astype(F32), 0)[0:8]
-    for c in range(cases):
-        comp_ref[c] = total[c, 0] / cells
+    done_ref[...] = jnp.zeros_like(done_ref)
     for copy in copies:
         copy.wait()
 
 
-def finish_call(got, sums, extra, first, last, factor, out, cells, cases, ring):
+def finish_call(got, first, last, factor, out):
     nx, ny, depth = out.shape
-    nin = len(got) + 1 + len(extra)
-    return pl.pallas_call(
-        functools.partial(finish_kernel, out.shape, cells, len(got), len(extra), cases, ring),
+    nin = len(got)
+    return pl.pallas_call(
+        functools.partial(finish_kernel, out.shape, len(got)),
         in_specs=[VMEM] * (nin + 3) + [HBM],
-        out_specs=[HBM, SMEM],
-        out_shape=[jax.ShapeDtypeStruct(out.shape, F32), jax.ShapeDtypeStruct((cases,), F32)],
+        out_specs=[HBM, VMEM],
+        out_shape=[jax.ShapeDtypeStruct(out.shape, F32), pltpu.VMEM((8, LANES), F32)],
         input_output_aliases={nin + 3: 0},
         scratch_shapes=[pltpu.VMEM((2, nx, 8, depth), F32), pltpu.SemaphoreType.DMA((2,))],
         compiler_params=pltpu.CompilerParams(vmem_limit_bytes=16 * MIB),
         name="finish",
-    )(*got, sums, *extra, *in_vmem(first, last, factor), *in_hbm(out))
+    )(*got, *in_vmem(first, last, factor), *in_hbm(out))
+
+
+def mean_kernel(cells, cases, *refs):
+    total = refs[0][...]
+    for ref in refs[2:-1]:
+        block = ref[...] if ref.shape[0] == 8 else sum3(ref[ref.shape[0] - 16 :, :].astype(F32), 0)[0:8]
+        total = total + block
+    for c in range(cases):
+        refs[-1][c] = total[c, 0] / cells
+
+
+def mean_call(sums, behind, got, cells, cases):
+    return pl.pallas_call(
+        functools.partial(mean_kernel, cells, cases),
+        in_specs=[VMEM] * (2 + len(got)),
+        out_specs=SMEM,
+        out_shape=jax.ShapeDtypeStruct((cases,), F32),
+        compiler_params=pltpu.CompilerParams(vmem_limit_bytes=4 * MIB),
+        name="mean",
+    )(sums, behind, *got)
 
 
 def swap_pairs(count, first):
@@ -583,25 +594,31 @@
     cases = energy.shape[0]
     nx, ny, depth = density.shape
     nz, gx, gy = (lax.axis_size(a) for a in ("gz", "gx", "gy"))
-    send, own, source = faces_call(density, design_mask, energy, decay, case_index, case_weight)
+    send, own, source, density_v, mask_v, maps, rows = faces_call(
+        density, design_mask, energy, decay, case_index, case_weight)
     swapped = nz in (1, 2, 4)
     if swapped:
         msgs = [lax.ppermute(send, "gz", xor_pairs(nz, m)) for m in range(1, nz)]
     else:
         every = lax.all_gather(send, "gz")
         own, *msgs = [every[j] for j in range(nz)]
-    t_local, factor, umap = local_call(density, design_mask, source, decay, case_index, case_weight)
-    t, *x_sends = couple_call(own, msgs, t_local, umap, max(swaps_of(gx), 1), swapped)
+    part, factor, umap = local_call(source, density_v, mask_v, maps, rows)
+    lhs, *x_sends = head_call(own, msgs, part, umap, max(swaps_of(gx), 1), swapped)
     x_got = [lax.ppermute(x_sends[k], "gx", swap_pairs(gx, k)) for k in range(swaps_of(gx))]
-    partial, first, last = inner_call(t, factor)
-    *y_sends, xb, xa, sums = edge_call(t, x_got, x_sends[0], first, swaps_of(gy), cases)
+    t, out, first, last = body_call(lhs, umap, part, factor)
+    *y_sends, xb, xa, sums = edge_call(t, x_got, x_sends[0], swaps_of(gy), cases)
     ring = gy == 4
     ends = [(0, gy - 1), (gy - 1, 0)] if ring else []
     y_got = [lax.ppermute(y_sends[k], "gy", swap_pairs(gy, k) + (ends if k else [])) for k in range(swaps_of(gy))]
-    extra = [lax.ppermute(sums, "gy", xor_pairs(gy, m)) for m in ([2] if ring else range(1, gy))]
-    partial, first, last = outer_call(t, xb, xa, factor, partial, first, last)
+    out, first, last = rest_call(t, xb, xa, factor, out, first, last)
+    if ring:
+        y_got[1], first = lax.optimization_barrier((y_got[1], first))
+        more = y_got + [lax.ppermute(y_got[1], "gy", swap_pairs(gy, 0))]
+    else:
+        more = [lax.ppermute(sums, "gy", xor_pairs(gy, m)) for m in range(1, gy)]
+    out, behind = finish_call(y_got, first, last, factor, out)
     cells = nx * ny * depth * nz * gx * gy
-    return tuple(finish_call(y_got, sums, extra, first, last, factor, partial, float(cells), cases, ring))
+    return out, mean_call(sums, behind, more, float(cells), cases)
 
 
 def solution(mesh):

time: 29.1 us -> 29.1 us (level)
  the two profiles are of different devices: /device:TPU:0 before, /device:TPU:1 now
where the time goes in v5:
time: 29.1 us; the launch traced here: 28.8 us
  Pallas kernels  14.4 us (49%)
  starting transfers between devices  10.2 us (35%)
  waiting for transfers between devices  3.45 us (12%)
  between operations  0.71 us (2%)
    pallas_call x1, Pallas kernels, faces_call(): pl.pallas_call(functools.partial(faces_kernel, energy.shape, bx), in_spec...  5.26 us
    ppermute x3, starting transfers between devices, shards(): msgs = [lax.ppermute(send, 'gz', xor_pairs(nz, m)) for m in range(1, nz)]  4.49 us
    ppermute x2, starting transfers between devices, shards(): lax.ppermute(y_sends[k], 'gy', swap_pairs(gy, k) + (ends if k else []))  4.03 us
    ppermute x3, waiting for transfers between devices, shards(): msgs = [lax.ppermute(send, 'gz', xor_pairs(nz, m)) for m in range(1, nz)]  2.79 us
    pallas_call x1, Pallas kernels, body_call(): pl.pallas_call(functools.partial(body_kernel, part.shape, chunk), in_spec...  2.45 us
    pallas_call x1, Pallas kernels, local_call(): pl.pallas_call(functools.partial(local_kernel, (cases, nx, ny, depth), 16...  2.23 us
    pallas_call x1, Pallas kernels, rest_call(): pl.pallas_call(functools.partial(rest_kernel, t.shape, chunk), in_specs=[...  1.87 us
    ppermute x1, starting transfers between devices, shards(): lax.ppermute(x_sends[k], 'gx', swap_pairs(gx, k))  1.27 us
  transfers between devices with their start and end apart: 7, of which 3 were waited for; matrix products, arithmetic and copies ran while one was open for 0% of the time, Pallas kernels for 26%

profile of v5, /device:TPU:1, one launch (start us, length us, event | category | flops | bytes accessed | tf_op | source)
XLA Modules:
  0.0 28.8 jit_solution(4505181169276172636)
XLA Ops:
  0.6 5.3 %faces.1 = (bf16[8,4224]{1,0:T(8,128)(2,1)S(1)}, f32[8,4224]{1,0:T(8,128)S(1)}, bf16[4096,512]{1,0:T(8,128)(2,1)S(1)}, f32[64,64,128]{2,1,0:T(8,128)S(1)}, s32[6...) custom-call(s32[4]{0:T(128)} %refs_0_.1, f32[16]{0:T(128)} %refs_1_.1, f32[4,128]{1,0:T(4,128)} %refs_2_.1, ...), custom_call_target="tpu_custom_call" | custom-call | tf_op jit(solution)/shard_map/faces/pallas_call | solution.py:185
  5.9 2.2 %collective-permute-start = (bf16[8,4224]{1,0:T(8,128)(2,1)S(1)}, bf16[8,4224]{1,0:T(8,128)(2,1)S(1)}, u32[]{:S(2)}, u32[]{:S(2)}) collective-permute-start(bf16[8,4224]{1,0:T(8,128)(2,1)S(1)} %get-tuple-element.31), channel_id=1, source_target_pairs={{0,8},{8,0},{16,24},{24,16},{1,9},{9,1},{17,25},{25,17},{2,10},{10... | collective-permute-start | bytes 202760 | tf_op jit(solution)/shard_map/ppermute | solution.py:601
  8.1 2.3 %collective-permute-start.1 = (bf16[8,4224]{1,0:T(8,128)(2,1)S(1)}, bf16[8,4224]{1,0:T(8,128)(2,1)S(1)}, u32[]{:S(2)}, u32[]{:S(2)}) collective-permute-start(bf16[8,4224]{1,0:T(8,128)(2,1)S(1)} %get-tuple-element.31), channel_id=1, source_target_pairs={{0,16},{8,24},{16,0},{24,8},{1,17},{9,25},{17,1},{25,9},{2,18},{10... | collective-permute-start | bytes 202760 | tf_op jit(solution)/shard_map/ppermute | solution.py:601
  10.4 0.0 collective-permute-start.2
  10.4 2.2 %local.1 = (f32[64,64,128]{2,1,0:T(8,128)S(1)}, f32[64,64,128]{2,1,0:T(8,128)S(1)}, bf16[32,128]{1,0:T(8,128)(2,1)S(1)}) custom-call(bf16[4096,512]{1,0:T(8,128)(2,1)S(1)} %get-tuple-element.32.source_ref, f32[64,64,128]{2,1,0:T(8,128)S(1)} %get-tuple-element.33.density_ref, s32[64,64,128]{2,1,0:T(8,128)S(1)} %get-tuple-element.34.mask_ref, ...), custom_call_target="tpu_custom_call" | custom-call | tf_op jit(solution)/shard_map/local/pallas_call | solution.py:246
  12.6 0.0 collective-permute-done.refs_1_
  12.6 0.1 collective-permute-done.1.refs_2_
  12.7 2.7 %collective-permute-done.2.refs_3_ = bf16[8,4224]{1,0:T(8,128)(2,1)S(1)} collective-permute-done((bf16[8,4224]{1,0:T(8,128)(2,1)S(1)}, bf16[8,4224]{1,0:T(8,128)(2,1)S(1)}, u32[]{:S(2)}, u32[]{:S(2)}) %collective-permute-start.2) | collective-permute-done | bytes 67616 | tf_op jit(solution)/shard_map/ppermute | solution.py:601
  15.4 0.5 %head.1 = (bf16[32,4096]{1,0:T(8,128)(2,1)S(1)}, bf16[208,128]{1,0:T(8,128)(2,1)S(1)}) custom-call(f32[8,4224]{1,0:T(8,128)S(1)} %get-tuple-element.30.refs_0_, bf16[8,4224]{1,0:T(8,128)(2,1)S(1)} %collective-permute-done.refs_1_, bf16[8,4224]{1,0:T(8,128)(2,1)S(1)} %collective-permute-done.1.refs_2_, bf16[8,4224]{1,0:T(8,128)(2,1)S(1)} %collective-permute-done.2.refs_3_, ...), custom_call_target="tpu_custom_call" | custom-call | tf_op jit(solution)/shard_map/head/pallas_call | solution.py:311
  16.0 1.3 %collective-permute-start.3 = (bf16[208,128]{1,0:T(8,128)(2,1)S(1)}, bf16[208,128]{1,0:T(8,128)(2,1)S(1)}, u32[]{:S(2)}, u32[]{:S(2)}) collective-permute-start(bf16[208,128]{1,0:T(8,128)(2,1)S(1)} %get-tuple-element.42.refs_2_), channel_id=1, source_target_pairs={{0,4},{4,0},{1,5},{5,1},{2,6},{6,2},{3,7},{7,3},{8,12},{12,8},{9,1... | collective-permute-start | bytes 159752 | tf_op jit(solution)/shard_map/ppermute | solution.py:607
  17.2 2.4 %body.1 = (f32[64,64,128]{2,1,0:T(8,128)S(1)}, f32[64,64,128]{2,1,0:T(8,128)}, f32[64,8,128]{2,1,0:T(8,128)S(1)}, f32[64,8,128]{2,1,0:T(8,128)S(1)}) custom-call(bf16[32,4096]{1,0:T(8,128)(2,1)S(1)} %get-tuple-element.39.lhs_ref, bf16[32,128]{1,0:T(8,128)(2,1)S(1)} %get-tuple-element.38.refs_5_.umap_ref, ...), custom_call_target="tpu_custom_call" | custom-call | tf_op jit(solution)/shard_map/body/pallas_call | solution.py:440
  19.7 0.0 collective-permute-done.3.refs_1_
  19.7 0.3 %edge.1 = (bf16[208,128]{1,0:T(8,128)(2,1)S(1)}, bf16[208,128]{1,0:T(8,128)(2,1)S(1)}, f32[192,128]{1,0:T(8,128)S(1)}, f32[192,128]{1,0:T(8,128)S(1)}, f32[8,128]{1,0:T(8,128)S(1)}) custom-call(f32[64,64,128]{2,1,0:T(8,128)S(1)} %get-tuple-element.41.refs_0_.t_ref, bf16[208,128]{1,0:T(8,128)(2,1)S(1)} %collective-permute-done.3.refs_1_, ...), custom_call_target="tpu_custom_call" | custom-call | tf_op jit(solution)/shard_map/edge/pallas_call | solution.py:370
  20.1 4.0 %collective-permute-start.5 = (bf16[208,128]{1,0:T(8,128)(2,1)S(1)}, bf16[208,128]{1,0:T(8,128)(2,1)S(1)}, u32[]{:S(2)}, u32[]{:S(2)}) collective-permute-start(bf16[208,128]{1,0:T(8,128)(2,1)S(1)} %get-tuple-element.44), channel_id=1, source_target_pairs={{1,2},{2,1},{0,3},{3,0},{5,6},{6,5},{4,7},{7,4},{9,10},{10,9},{8,1... | collective-permute-start | bytes 159752 | tf_op jit(solution)/shard_map/ppermute | solution.py:612
  24.1 0.0 collective-permute-start.4
  24.1 1.9 %rest.1 = (f32[64,64,128]{2,1,0:T(8,128)}, f32[64,8,128]{2,1,0:T(8,128)S(1)}, f32[64,8,128]{2,1,0:T(8,128)S(1)}) custom-call(f32[64,64,128]{2,1,0:T(8,128)S(1)} %get-tuple-element.41.refs_0_.t_ref, f32[192,128]{1,0:T(8,128)S(1)} %get-tuple-element.45.xb_ref, ...), custom_call_target="tpu_custom_call", output_to_operand_aliasing={{0}: (4, {}), {1}: (5, {}), {2}: (6, {})} | custom-call | tf_op jit(solution)/shard_map/rest/pallas_call | solution.py:489
  26.0 0.7 %collective-permute-done.5.refs_1_.refs_3_ = bf16[208,128]{1,0:T(8,128)(2,1)S(1)} collective-permute-done((bf16[208,128]{1,0:T(8,128)(2,1)S(1)}, bf16[208,128]{1,0:T(8,128)(2,1)S(1)}, u32[]{:S(2)}, u32[]{:S(2)}) %collective-permute-start.5) | collective-permute-done | bytes 53280 | tf_op jit(solution)/shard_map/ppermute | solution.py:612
  26.6 0.4 %collective-permute-start.6 = (bf16[208,128]{1,0:T(8,128)(2,1)S(1)}, bf16[208,128]{1,0:T(8,128)(2,1)S(1)}, u32[]{:S(2)}, u32[]{:S(2)}) collective-permute-start(bf16[208,128]{1,0:T(8,128)(2,1)S(1)} %collective-permute-done.5.refs_1_.refs_3_), channel_id=1, source_target_pairs={{0,1},{1,0},{2,3},{3,2},{4,5},{5,4},{6,7},{7,6},{8,9},{9,8},{10,11... | collective-permute-start | bytes 159752 | tf_op jit(solution)/shard_map/ppermute | solution.py:616
  27.0 0.0 collective-permute-done.4.refs_0_.refs_2_
  27.0 1.0 %finish.1 = (f32[64,64,128]{2,1,0:T(8,128)}, f32[8,128]{1,0:T(8,128)S(1)}) custom-call(bf16[208,128]{1,0:T(8,128)(2,1)S(1)} %collective-permute-done.4.refs_0_.refs_2_, bf16[208,128]{1,0:T(8,128)(2,1)S(1)} %collective-permute-done.5.refs_1_.refs_3_, f32[64,8,128]{2,1,0:T(8,128)S(1)} %get-tuple-element.52.refs_2_, ...), custom_call_target="tpu_custom_call", output_to_operand_aliasing={{0}: (5, {})} | custom-call | tf_op jit(solution)/shard_map/finish/pallas_call | solution.py:549
  28.1 0.0 collective-permute-done.6.refs_4_
  28.1 0.7 %mean.1 = f32[4]{0:T(128)} custom-call(f32[8,128]{1,0:T(8,128)S(1)} %get-tuple-element.56.refs_0_, f32[8,128]{1,0:T(8,128)S(1)} %get-tuple-element.57.refs_1_, bf16[208,128]{1,0:T(8,128)(2,1)S(1)} %collective-permute-done.4.refs_0_.refs_2_, bf16[208,128]{1,0:T(8,128)(2,1)S(1)} %collective-permute-done.5.refs_1_.refs_3_, ...), custom_call_target="tpu_custom_call" | custom-call | tf_op jit(solution)/shard_map/mean/pallas_call | solution.py:571
Async XLA Ops:
  5.9 6.7 %collective-permute-start = (bf16[8,4224]{1,0:T(8,128)(2,1)S(1)}, bf16[8,4224]{1,0:T(8,128)(2,1)S(1)}, u32[]{:S(2)}, u32[]{:S(2)}) collective-permute-start(bf16[8,4224]{1,0:T(8,128)(2,1)S(1)} %get-tuple-element.31), channel_id=1, source_target_pairs={{0,8},{8,0},{16,24},{24,16},{1,9},{9,1},{17,25},{25,17},{2,10},{10... | collective-permute-start | bytes 202760 | tf_op jit(solution)/shard_map/ppermute | solution.py:601
  8.1 4.6 %collective-permute-start.1 = (bf16[8,4224]{1,0:T(8,128)(2,1)S(1)}, bf16[8,4224]{1,0:T(8,128)(2,1)S(1)}, u32[]{:S(2)}, u32[]{:S(2)}) collective-permute-start(bf16[8,4224]{1,0:T(8,128)(2,1)S(1)} %get-tuple-element.31), channel_id=1, source_target_pairs={{0,16},{8,24},{16,0},{24,8},{1,17},{9,25},{17,1},{25,9},{2,18},{10... | collective-permute-start | bytes 202760 | tf_op jit(solution)/shard_map/ppermute | solution.py:601
  10.4 5.0 %collective-permute-start.2 = (bf16[8,4224]{1,0:T(8,128)(2,1)S(1)}, bf16[8,4224]{1,0:T(8,128)(2,1)S(1)}, u32[]{:S(2)}, u32[]{:S(2)}) collective-permute-start(bf16[8,4224]{1,0:T(8,128)(2,1)S(1)} %get-tuple-element.31), channel_id=1, source_target_pairs={{0,24},{8,16},{16,8},{24,0},{1,25},{9,17},{17,9},{25,1},{2,26},{10... | collective-permute-start | bytes 202760 | tf_op jit(solution)/shard_map/ppermute | solution.py:601
  16.0 3.7 %collective-permute-start.3 = (bf16[208,128]{1,0:T(8,128)(2,1)S(1)}, bf16[208,128]{1,0:T(8,128)(2,1)S(1)}, u32[]{:S(2)}, u32[]{:S(2)}) collective-permute-start(bf16[208,128]{1,0:T(8,128)(2,1)S(1)} %get-tuple-element.42.refs_2_), channel_id=1, source_target_pairs={{0,4},{4,0},{1,5},{5,1},{2,6},{6,2},{3,7},{7,3},{8,12},{12,8},{9,1... | collective-permute-start | bytes 159752 | tf_op jit(solution)/shard_map/ppermute | solution.py:607
  20.1 6.6 %collective-permute-start.5 = (bf16[208,128]{1,0:T(8,128)(2,1)S(1)}, bf16[208,128]{1,0:T(8,128)(2,1)S(1)}, u32[]{:S(2)}, u32[]{:S(2)}) collective-permute-start(bf16[208,128]{1,0:T(8,128)(2,1)S(1)} %get-tuple-element.44), channel_id=1, source_target_pairs={{1,2},{2,1},{0,3},{3,0},{5,6},{6,5},{4,7},{7,4},{9,10},{10,9},{8,1... | collective-permute-start | bytes 159752 | tf_op jit(solution)/shard_map/ppermute | solution.py:612
  24.1 2.9 %collective-permute-start.4 = (bf16[208,128]{1,0:T(8,128)(2,1)S(1)}, bf16[208,128]{1,0:T(8,128)(2,1)S(1)}, u32[]{:S(2)}, u32[]{:S(2)}) collective-permute-start(bf16[208,128]{1,0:T(8,128)(2,1)S(1)} %get-tuple-element.43), channel_id=1, source_target_pairs={{0,1},{1,0},{2,3},{3,2},{4,5},{5,4},{6,7},{7,6},{8,9},{9,8},{10,11... | collective-permute-start | bytes 159752 | tf_op jit(solution)/shard_map/ppermute | solution.py:612
  26.6 1.4 %collective-permute-start.6 = (bf16[208,128]{1,0:T(8,128)(2,1)S(1)}, bf16[208,128]{1,0:T(8,128)(2,1)S(1)}, u32[]{:S(2)}, u32[]{:S(2)}) collective-permute-start(bf16[208,128]{1,0:T(8,128)(2,1)S(1)} %collective-permute-done.5.refs_1_.refs_3_), channel_id=1, source_target_pairs={{0,1},{1,0},{2,3},{3,2},{4,5},{5,4},{6,7},{7,6},{8,9},{9,8},{10,11... | collective-permute-start | bytes 159752 | tf_op jit(solution)/shard_map/ppermute | solution.py:616

commit v6 on v5

--- a/solution.py
+++ b/solution.py
@@ -72,7 +72,10 @@
         self.row = lax.broadcasted_iota(jnp.int32, (depth, depth), 0)
         self.col = lax.broadcasted_iota(jnp.int32, (depth, depth), 1)
         logs = jnp.log(decay)
-        self.up = dot_high(logs, (self.row <= self.col).astype(F32))
+        upto = (self.row <= self.col).astype(BF16)
+        parts = jnp.concatenate(split3(pad_rows(logs, 8)), axis=0).astype(BF16)
+        sums = lax.dot_general(parts, upto, (((1,), (0,)), ((), ())), preferred_element_type=F32)
+        self.up = (sums[0:8] + sums[8:16] + sums[16:24])[0:cases]
         self.up_ex = self.up - logs
         wide = lambda v: jnp.transpose(pad_rows(v, 8))
         self.up_t = wide(self.up)
@@ -90,20 +93,18 @@
     return -3.0 * weight_ref[index_ref[c]]
 
 
-def faces_kernel(shape, bx, *refs):
+def faces_kernel(shape, cuts, *refs):
     cases, nx, ny, depth = shape
     (index_hbm, weight_hbm, decay_hbm, density_hbm, mask_hbm, energy_hbm,
      send_ref, own_ref, source_ref, density_ref, mask_ref, map_ref, rows_ref,
      index_ref, weight_ref, decay_ref, energy_ref, small_sem, sem) = refs
-    steps, cols = nx // bx, bx * ny
     small = [
         pltpu.make_async_copy(decay_hbm, decay_ref, small_sem.at[0]),
         pltpu.make_async_copy(index_hbm, index_ref, small_sem.at[1]),
         pltpu.make_async_copy(weight_hbm, weight_ref, small_sem.at[2]),
     ]
     big = []
-    for s in range(steps):
-        at = pl.ds(s * bx, bx)
+    for s, at in enumerate(pl.ds(*cut) for cut in cuts):
         big.append([
             pltpu.make_async_copy(density_hbm.at[at], density_ref.at[at], sem.at[0, s]),
             pltpu.make_async_copy(mask_hbm.at[at], mask_ref.at[at], sem.at[1, s]),
@@ -131,7 +132,12 @@
         keep = 1.0 - decay[c : c + 1, :]
         e_row = jnp.exp(slab.total[c : c + 1] - slab.up[c : c + 1, :]) * keep * scale
         b_row = jnp.exp(slab.up_ex[c : c + 1, :]) * keep
-        h_row = dot_high(b_row, f_t, ((1,), (1,)))
+        b_hi = b_row.astype(BF16).astype(F32)
+        b_two = jnp.concatenate([b_hi, b_row - b_hi] + [zero_row] * 6, axis=0).astype(BF16)
+        f_hi, f_lo = split2(f_t)
+        twice = lax.dot_general(b_two, f_hi, (((1,), (1,)), ((), ())), preferred_element_type=F32)
+        once = lax.dot_general(b_two, f_lo, (((1,), (1,)), ((), ())), preferred_element_type=F32)
+        h_row = twice[0:1] + twice[1:2] + once[0:1]
         turns.append(jnp.sum(b_row * jnp.exp(slab.up[c : c + 1, :]), axis=1, keepdims=True))
         place = lambda r: jnp.concatenate([zero_row] * c + [r] + [zero_row] * (cases - 1 - c), axis=1)
         e_rows.append(place(e_row))
@@ -142,32 +148,30 @@
 
     sums = [jnp.zeros((8, depth), F32) for _ in range(cases)]
 
-    def faces_of(s):
-        span = pl.ds(s * cols, cols)
+    def faces_of(at, span):
         faces = lax.dot_general(
             wmat, source_ref[span, :], (((1,), (1,)), ((), ())), preferred_element_type=F32)
         faces = faces[0 : 2 * cases] + faces[2 * cases : 4 * cases]
         own_ref[:, span] = faces
         send_ref[:, span] = faces.astype(BF16)
 
-    for s in range(steps):
+    for s, (first, bx) in enumerate(cuts):
+        cols = bx * ny
         for copy in big[s]:
             copy.wait()
         for group in big[s + AHEAD + 1 : s + AHEAD + 2]:
             for copy in group:
                 copy.start()
-        at = pl.ds(s * bx, bx)
+        at = pl.ds(first, bx)
         mask = mask_ref[at]
         dense = jnp.where(mask == 1, 0.001, jnp.where(mask == 2, 1.0, density_ref[at]))
         cube = dense * dense * dense
-        span = pl.ds(s * cols, cols)
+        span = pl.ds(first * ny, cols)
         for c in range(cases):
             work = cube * energy_ref[c, at].astype(F32)
             sums[c] = sums[c] + jnp.sum(work.reshape(cols // 8, 8, depth), axis=0)
             source_ref[span, c * depth : (c + 1) * depth] = work.astype(BF16).reshape(cols, depth)
-        if s > 0:
-            faces_of(s - 1)
-    faces_of(steps - 1)
+        faces_of(at, span)
 
     total = jnp.concatenate([jnp.sum(jnp.sum(v, axis=0, keepdims=True), axis=1, keepdims=True) for v in sums], axis=0)
     turn = jnp.concatenate(turns, axis=0)
@@ -178,12 +182,17 @@
     send_ref[:, tail] = aux.astype(BF16)
 
 
+def row_cuts(nx):
+    rows = 16 if nx % 16 == 0 else nx
+    return [(start, rows) for start in range(0, nx, rows)]
+
+
 def faces_call(density, design_mask, energy, decay, case_index, case_weight):
     cases, nx, ny, depth = energy.shape
-    bx = 16
+    cuts = row_cuts(nx)
     width = nx * ny + LANES
     return pl.pallas_call(
-        functools.partial(faces_kernel, energy.shape, bx),
+        functools.partial(faces_kernel, energy.shape, cuts),
         in_specs=[HBM] * 6,
         out_specs=[VMEM] * 7,
         out_shape=[
@@ -201,7 +210,7 @@
             pltpu.VMEM(decay.shape, F32),
             pltpu.VMEM(energy.shape, BF16),
             pltpu.SemaphoreType.DMA((3,)),
-            pltpu.SemaphoreType.DMA((3, nx // bx)),
+            pltpu.SemaphoreType.DMA((3, len(cuts))),
         ],
         compiler_params=pltpu.CompilerParams(vmem_limit_bytes=20 * MIB),
         name="faces",
@@ -269,7 +278,7 @@
     mine = lax.axis_index("gz")
     low = lax.axis_index("gx") % 2 == 1
     stack[0] = own_ref[...].astype(F32)
-    for m, msg in enumerate(msgs):
+    for m, msg in enumerate(reversed(msgs) if swapped else msgs):
         stack[m + 1] = msg[...].astype(F32)
     total = jnp.zeros((cases, 1), F32)
     for m in range(nslabs):
@@ -598,7 +607,7 @@
         density, design_mask, energy, decay, case_index, case_weight)
     swapped = nz in (1, 2, 4)
     if swapped:
-        msgs = [lax.ppermute(send, "gz", xor_pairs(nz, m)) for m in range(1, nz)]
+        msgs = [lax.ppermute(send, "gz", xor_pairs(nz, m)) for m in range(nz - 1, 0, -1)]
     else:
         every = lax.all_gather(send, "gz")
         own, *msgs = [every[j] for j in range(nz)]

time: 29.1 us -> 27.6 us (0.948)
  starting transfers between devices: 10.2 us -> 8.82 us
  Pallas kernels: 14.4 us -> 13.9 us
  waiting for transfers between devices: 3.45 us -> 3.84 us
    ppermute x2, starting transfers between devices: 4.03 us -> 2.42 us  [shards(): lax.ppermute(y_sends[k], 'gy', swap_pairs(gy, k) + (ends if k else []))]
    pallas_call x1, Pallas kernels: 5.26 us -> 4.79 us  [faces_call(): pl.pallas_call(functools.partial(faces_kernel, energy.shape, cuts), in_sp...]
    ppermute x3, waiting for transfers between devices: 2.79 us -> 3.18 us  [shards(): lax.ppermute(send, 'gz', xor_pairs(nz, m))]
  transfers between devices with their start and end apart: 7 -> 7, of which waited for: 3 -> 2; matrix products, arithmetic and copies ran while one was open for 0% -> 0% of each run, Pallas kernels for 26% -> 28%
where the time goes in v6:
time: 27.6 us; the launch traced here: 27.3 us
  Pallas kernels  13.9 us (50%)
  starting transfers between devices  8.82 us (32%)
  waiting for transfers between devices  3.84 us (14%)
  between operations  0.71 us (3%)
    pallas_call x1, Pallas kernels, faces_call(): pl.pallas_call(functools.partial(faces_kernel, energy.shape, cuts), in_sp...  4.79 us
    ppermute x3, starting transfers between devices, shards(): lax.ppermute(send, 'gz', xor_pairs(nz, m))  4.57 us
    ppermute x3, waiting for transfers between devices, shards(): lax.ppermute(send, 'gz', xor_pairs(nz, m))  3.18 us
    pallas_call x1, Pallas kernels, body_call(): pl.pallas_call(functools.partial(body_kernel, part.shape, chunk), in_spec...  2.45 us
    ppermute x2, starting transfers between devices, shards(): lax.ppermute(y_sends[k], 'gy', swap_pairs(gy, k) + (ends if k else []))  2.42 us
    pallas_call x1, Pallas kernels, local_call(): pl.pallas_call(functools.partial(local_kernel, (cases, nx, ny, depth), 16...  2.23 us
    pallas_call x1, Pallas kernels, rest_call(): pl.pallas_call(functools.partial(rest_kernel, t.shape, chunk), in_specs=[...  1.87 us
    ppermute x1, starting transfers between devices, shards(): lax.ppermute(x_sends[k], 'gx', swap_pairs(gx, k))  1.43 us
  transfers between devices with their start and end apart: 7, of which 2 were waited for; matrix products, arithmetic and copies ran while one was open for 0% of the time, Pallas kernels for 28%

profile of v6, /device:TPU:1, one launch (start us, length us, event | category | flops | bytes accessed | tf_op | source)
XLA Modules:
  0.0 27.3 jit_solution(1382299007595496203)
XLA Ops:
  0.6 4.8 %faces.1 = (bf16[8,4224]{1,0:T(8,128)(2,1)S(1)}, f32[8,4224]{1,0:T(8,128)S(1)}, bf16[4096,512]{1,0:T(8,128)(2,1)S(1)}, f32[64,64,128]{2,1,0:T(8,128)S(1)}, s32[6...) custom-call(s32[4]{0:T(128)} %refs_0_.1, f32[16]{0:T(128)} %refs_1_.1, f32[4,128]{1,0:T(4,128)} %refs_2_.1, ...), custom_call_target="tpu_custom_call" | custom-call | tf_op jit(solution)/shard_map/faces/pallas_call | solution.py:194
  5.4 4.2 %collective-permute-start = (bf16[8,4224]{1,0:T(8,128)(2,1)S(1)}, bf16[8,4224]{1,0:T(8,128)(2,1)S(1)}, u32[]{:S(2)}, u32[]{:S(2)}) collective-permute-start(bf16[8,4224]{1,0:T(8,128)(2,1)S(1)} %get-tuple-element.31), channel_id=1, source_target_pairs={{0,24},{8,16},{16,8},{24,0},{1,25},{9,17},{17,9},{25,1},{2,26},{10... | collective-permute-start | bytes 202760 | tf_op jit(solution)/shard_map/ppermute | solution.py:610
  9.6 0.0 collective-permute-start.1
  9.6 0.4 %collective-permute-start.2 = (bf16[8,4224]{1,0:T(8,128)(2,1)S(1)}, bf16[8,4224]{1,0:T(8,128)(2,1)S(1)}, u32[]{:S(2)}, u32[]{:S(2)}) collective-permute-start(bf16[8,4224]{1,0:T(8,128)(2,1)S(1)} %get-tuple-element.31), channel_id=1, source_target_pairs={{0,8},{8,0},{16,24},{24,16},{1,9},{9,1},{17,25},{25,17},{2,10},{10... | collective-permute-start | bytes 202760 | tf_op jit(solution)/shard_map/ppermute | solution.py:610
  10.0 2.2 %local.1 = (f32[64,64,128]{2,1,0:T(8,128)S(1)}, f32[64,64,128]{2,1,0:T(8,128)S(1)}, bf16[32,128]{1,0:T(8,128)(2,1)S(1)}) custom-call(bf16[4096,512]{1,0:T(8,128)(2,1)S(1)} %get-tuple-element.32.source_ref, f32[64,64,128]{2,1,0:T(8,128)S(1)} %get-tuple-element.33.density_ref, s32[64,64,128]{2,1,0:T(8,128)S(1)} %get-tuple-element.34.mask_ref, ...), custom_call_target="tpu_custom_call" | custom-call | tf_op jit(solution)/shard_map/local/pallas_call | solution.py:255
  12.2 0.0 collective-permute-done.refs_1_
  12.2 3.2 %collective-permute-done.1.refs_2_ = bf16[8,4224]{1,0:T(8,128)(2,1)S(1)} collective-permute-done((bf16[8,4224]{1,0:T(8,128)(2,1)S(1)}, bf16[8,4224]{1,0:T(8,128)(2,1)S(1)}, u32[]{:S(2)}, u32[]{:S(2)}) %collective-permute-start.1) | collective-permute-done | bytes 67616 | tf_op jit(solution)/shard_map/ppermute | solution.py:610
  15.4 0.0 collective-permute-done.2.refs_3_
  15.4 0.5 %head.1 = (bf16[32,4096]{1,0:T(8,128)(2,1)S(1)}, bf16[208,128]{1,0:T(8,128)(2,1)S(1)}) custom-call(f32[8,4224]{1,0:T(8,128)S(1)} %get-tuple-element.30.refs_0_, bf16[8,4224]{1,0:T(8,128)(2,1)S(1)} %collective-permute-done.refs_1_, bf16[8,4224]{1,0:T(8,128)(2,1)S(1)} %collective-permute-done.1.refs_2_, bf16[8,4224]{1,0:T(8,128)(2,1)S(1)} %collective-permute-done.2.refs_3_, ...), custom_call_target="tpu_custom_call" | custom-call | tf_op jit(solution)/shard_map/head/pallas_call | solution.py:320
  16.0 1.4 %collective-permute-start.3 = (bf16[208,128]{1,0:T(8,128)(2,1)S(1)}, bf16[208,128]{1,0:T(8,128)(2,1)S(1)}, u32[]{:S(2)}, u32[]{:S(2)}) collective-permute-start(bf16[208,128]{1,0:T(8,128)(2,1)S(1)} %get-tuple-element.42.refs_2_), channel_id=1, source_target_pairs={{0,4},{4,0},{1,5},{5,1},{2,6},{6,2},{3,7},{7,3},{8,12},{12,8},{9,1... | collective-permute-start | bytes 159752 | tf_op jit(solution)/shard_map/ppermute | solution.py:616
  17.4 2.4 %body.1 = (f32[64,64,128]{2,1,0:T(8,128)S(1)}, f32[64,64,128]{2,1,0:T(8,128)}, f32[64,8,128]{2,1,0:T(8,128)S(1)}, f32[64,8,128]{2,1,0:T(8,128)S(1)}) custom-call(bf16[32,4096]{1,0:T(8,128)(2,1)S(1)} %get-tuple-element.39.lhs_ref, bf16[32,128]{1,0:T(8,128)(2,1)S(1)} %get-tuple-element.38.refs_5_.umap_ref, ...), custom_call_target="tpu_custom_call" | custom-call | tf_op jit(solution)/shard_map/body/pallas_call | solution.py:449
  19.9 0.0 collective-permute-done.3.refs_1_
  19.9 0.3 %edge.1 = (bf16[208,128]{1,0:T(8,128)(2,1)S(1)}, bf16[208,128]{1,0:T(8,128)(2,1)S(1)}, f32[192,128]{1,0:T(8,128)S(1)}, f32[192,128]{1,0:T(8,128)S(1)}, f32[8,128]{1,0:T(8,128)S(1)}) custom-call(f32[64,64,128]{2,1,0:T(8,128)S(1)} %get-tuple-element.41.refs_0_.t_ref, bf16[208,128]{1,0:T(8,128)(2,1)S(1)} %collective-permute-done.3.refs_1_, ...), custom_call_target="tpu_custom_call" | custom-call | tf_op jit(solution)/shard_map/edge/pallas_call | solution.py:379
  20.2 2.4 %collective-permute-start.5 = (bf16[208,128]{1,0:T(8,128)(2,1)S(1)}, bf16[208,128]{1,0:T(8,128)(2,1)S(1)}, u32[]{:S(2)}, u32[]{:S(2)}) collective-permute-start(bf16[208,128]{1,0:T(8,128)(2,1)S(1)} %get-tuple-element.44), channel_id=1, source_target_pairs={{1,2},{2,1},{0,3},{3,0},{5,6},{6,5},{4,7},{7,4},{9,10},{10,9},{8,1... | collective-permute-start | bytes 159752 | tf_op jit(solution)/shard_map/ppermute | solution.py:621
  22.6 0.0 collective-permute-start.4
  22.6 1.9 %rest.1 = (f32[64,64,128]{2,1,0:T(8,128)}, f32[64,8,128]{2,1,0:T(8,128)S(1)}, f32[64,8,128]{2,1,0:T(8,128)S(1)}) custom-call(f32[64,64,128]{2,1,0:T(8,128)S(1)} %get-tuple-element.41.refs_0_.t_ref, f32[192,128]{1,0:T(8,128)S(1)} %get-tuple-element.45.xb_ref, ...), custom_call_target="tpu_custom_call", output_to_operand_aliasing={{0}: (4, {}), {1}: (5, {}), {2}: (6, {})} | custom-call | tf_op jit(solution)/shard_map/rest/pallas_call | solution.py:498
  24.5 0.7 %collective-permute-done.5.refs_1_.refs_3_ = bf16[208,128]{1,0:T(8,128)(2,1)S(1)} collective-permute-done((bf16[208,128]{1,0:T(8,128)(2,1)S(1)}, bf16[208,128]{1,0:T(8,128)(2,1)S(1)}, u32[]{:S(2)}, u32[]{:S(2)}) %collective-permute-start.5) | collective-permute-done | bytes 53280 | tf_op jit(solution)/shard_map/ppermute | solution.py:621
  25.2 0.4 %collective-permute-start.6 = (bf16[208,128]{1,0:T(8,128)(2,1)S(1)}, bf16[208,128]{1,0:T(8,128)(2,1)S(1)}, u32[]{:S(2)}, u32[]{:S(2)}) collective-permute-start(bf16[208,128]{1,0:T(8,128)(2,1)S(1)} %collective-permute-done.5.refs_1_.refs_3_), channel_id=1, source_target_pairs={{0,1},{1,0},{2,3},{3,2},{4,5},{5,4},{6,7},{7,6},{8,9},{9,8},{10,11... | collective-permute-start | bytes 159752 | tf_op jit(solution)/shard_map/ppermute | solution.py:625
  25.6 0.0 collective-permute-done.4.refs_0_.refs_2_
  25.6 1.0 %finish.1 = (f32[64,64,128]{2,1,0:T(8,128)}, f32[8,128]{1,0:T(8,128)S(1)}) custom-call(bf16[208,128]{1,0:T(8,128)(2,1)S(1)} %collective-permute-done.4.refs_0_.refs_2_, bf16[208,128]{1,0:T(8,128)(2,1)S(1)} %collective-permute-done.5.refs_1_.refs_3_, f32[64,8,128]{2,1,0:T(8,128)S(1)} %get-tuple-element.52.refs_2_, ...), custom_call_target="tpu_custom_call", output_to_operand_aliasing={{0}: (5, {})} | custom-call | tf_op jit(solution)/shard_map/finish/pallas_call | solution.py:558
  26.6 0.0 collective-permute-done.6.refs_4_
  26.6 0.7 %mean.1 = f32[4]{0:T(128)} custom-call(f32[8,128]{1,0:T(8,128)S(1)} %get-tuple-element.56.refs_0_, f32[8,128]{1,0:T(8,128)S(1)} %get-tuple-element.57.refs_1_, bf16[208,128]{1,0:T(8,128)(2,1)S(1)} %collective-permute-done.4.refs_0_.refs_2_, bf16[208,128]{1,0:T(8,128)(2,1)S(1)} %collective-permute-done.5.refs_1_.refs_3_, ...), custom_call_target="tpu_custom_call" | custom-call | tf_op jit(solution)/shard_map/mean/pallas_call | solution.py:580
Async XLA Ops:
  5.4 6.8 %collective-permute-start = (bf16[8,4224]{1,0:T(8,128)(2,1)S(1)}, bf16[8,4224]{1,0:T(8,128)(2,1)S(1)}, u32[]{:S(2)}, u32[]{:S(2)}) collective-permute-start(bf16[8,4224]{1,0:T(8,128)(2,1)S(1)} %get-tuple-element.31), channel_id=1, source_target_pairs={{0,24},{8,16},{16,8},{24,0},{1,25},{9,17},{17,9},{25,1},{2,26},{10... | collective-permute-start | bytes 202760 | tf_op jit(solution)/shard_map/ppermute | solution.py:610
  9.6 5.8 %collective-permute-start.1 = (bf16[8,4224]{1,0:T(8,128)(2,1)S(1)}, bf16[8,4224]{1,0:T(8,128)(2,1)S(1)}, u32[]{:S(2)}, u32[]{:S(2)}) collective-permute-start(bf16[8,4224]{1,0:T(8,128)(2,1)S(1)} %get-tuple-element.31), channel_id=1, source_target_pairs={{0,16},{8,24},{16,0},{24,8},{1,17},{9,25},{17,1},{25,9},{2,18},{10... | collective-permute-start | bytes 202760 | tf_op jit(solution)/shard_map/ppermute | solution.py:610
  9.6 5.8 %collective-permute-start.2 = (bf16[8,4224]{1,0:T(8,128)(2,1)S(1)}, bf16[8,4224]{1,0:T(8,128)(2,1)S(1)}, u32[]{:S(2)}, u32[]{:S(2)}) collective-permute-start(bf16[8,4224]{1,0:T(8,128)(2,1)S(1)} %get-tuple-element.31), channel_id=1, source_target_pairs={{0,8},{8,0},{16,24},{24,16},{1,9},{9,1},{17,25},{25,17},{2,10},{10... | collective-permute-start | bytes 202760 | tf_op jit(solution)/shard_map/ppermute | solution.py:610
  16.0 3.9 %collective-permute-start.3 = (bf16[208,128]{1,0:T(8,128)(2,1)S(1)}, bf16[208,128]{1,0:T(8,128)(2,1)S(1)}, u32[]{:S(2)}, u32[]{:S(2)}) collective-permute-start(bf16[208,128]{1,0:T(8,128)(2,1)S(1)} %get-tuple-element.42.refs_2_), channel_id=1, source_target_pairs={{0,4},{4,0},{1,5},{5,1},{2,6},{6,2},{3,7},{7,3},{8,12},{12,8},{9,1... | collective-permute-start | bytes 159752 | tf_op jit(solution)/shard_map/ppermute | solution.py:616
  20.2 5.0 %collective-permute-start.5 = (bf16[208,128]{1,0:T(8,128)(2,1)S(1)}, bf16[208,128]{1,0:T(8,128)(2,1)S(1)}, u32[]{:S(2)}, u32[]{:S(2)}) collective-permute-start(bf16[208,128]{1,0:T(8,128)(2,1)S(1)} %get-tuple-element.44), channel_id=1, source_target_pairs={{1,2},{2,1},{0,3},{3,0},{5,6},{6,5},{4,7},{7,4},{9,10},{10,9},{8,1... | collective-permute-start | bytes 159752 | tf_op jit(solution)/shard_map/ppermute | solution.py:621
  22.6 2.9 %collective-permute-start.4 = (bf16[208,128]{1,0:T(8,128)(2,1)S(1)}, bf16[208,128]{1,0:T(8,128)(2,1)S(1)}, u32[]{:S(2)}, u32[]{:S(2)}) collective-permute-start(bf16[208,128]{1,0:T(8,128)(2,1)S(1)} %get-tuple-element.43), channel_id=1, source_target_pairs={{0,1},{1,0},{2,3},{3,2},{4,5},{5,4},{6,7},{7,6},{8,9},{9,8},{10,11... | collective-permute-start | bytes 159752 | tf_op jit(solution)/shard_map/ppermute | solution.py:621
  25.2 1.4 %collective-permute-start.6 = (bf16[208,128]{1,0:T(8,128)(2,1)S(1)}, bf16[208,128]{1,0:T(8,128)(2,1)S(1)}, u32[]{:S(2)}, u32[]{:S(2)}) collective-permute-start(bf16[208,128]{1,0:T(8,128)(2,1)S(1)} %collective-permute-done.5.refs_1_.refs_3_), channel_id=1, source_target_pairs={{0,1},{1,0},{2,3},{3,2},{4,5},{5,4},{6,7},{7,6},{8,9},{9,8},{10,11... | collective-permute-start | bytes 159752 | tf_op jit(solution)/shard_map/ppermute | solution.py:625

commit v7 on v6

--- a/solution.py
+++ b/solution.py
@@ -278,8 +278,8 @@
     mine = lax.axis_index("gz")
     low = lax.axis_index("gx") % 2 == 1
     stack[0] = own_ref[...].astype(F32)
-    for m, msg in enumerate(reversed(msgs) if swapped else msgs):
-        stack[m + 1] = msg[...].astype(F32)
+    for m, msg in zip(swap_order(nslabs) if swapped else range(1, nslabs), msgs):
+        stack[m] = msg[...].astype(F32)
     total = jnp.zeros((cases, 1), F32)
     for m in range(nslabs):
         total = total + sum3(stack[m, 0:cases, cols : cols + LANES], 6)
@@ -595,6 +595,10 @@
     return min(count - 1, 2)
 
 
+def swap_order(count):
+    return {1: (), 2: (1,), 4: (2, 3, 1)}[count]
+
+
 def xor_pairs(count, m):
     return [(i, i ^ m) for i in range(count)]
 
@@ -607,7 +611,7 @@
         density, design_mask, energy, decay, case_index, case_weight)
     swapped = nz in (1, 2, 4)
     if swapped:
-        msgs = [lax.ppermute(send, "gz", xor_pairs(nz, m)) for m in range(nz - 1, 0, -1)]
+        msgs = [lax.ppermute(send, "gz", xor_pairs(nz, m)) for m in swap_order(nz)]
     else:
         every = lax.all_gather(send, "gz")
         own, *msgs = [every[j] for j in range(nz)]

time: 27.6 us -> 27.1 us (0.982)
  waiting for transfers between devices: 3.84 us -> 2 us
  starting transfers between devices: 8.82 us -> 10.2 us
    ppermute x3, waiting for transfers between devices: 3.18 us -> 1.51 us  [shards(): msgs = [lax.ppermute(send, 'gz', xor_pairs(nz, m)) for m in swap_order(nz)]]
    ppermute x2, starting transfers between devices: 2.42 us -> 3.43 us  [shards(): lax.ppermute(y_sends[k], 'gy', swap_pairs(gy, k) + (ends if k else []))]
    ppermute x1, starting transfers between devices: 1.43 us -> 1.84 us  [shards(): lax.ppermute(x_sends[k], 'gx', swap_pairs(gx, k))]
where the time goes in v7:
time: 27.1 us; the launch traced here: 26.8 us
  Pallas kernels  13.9 us (51%)
  starting transfers between devices  10.2 us (38%)
  waiting for transfers between devices  2 us (7%)
  between operations  0.71 us (3%)
    pallas_call x1, Pallas kernels, faces_call(): pl.pallas_call(functools.partial(faces_kernel, energy.shape, cuts), in_sp...  4.79 us
    ppermute x3, starting transfers between devices, shards(): msgs = [lax.ppermute(send, 'gz', xor_pairs(nz, m)) for m in swap_order(nz)]  4.49 us
    ppermute x2, starting transfers between devices, shards(): lax.ppermute(y_sends[k], 'gy', swap_pairs(gy, k) + (ends if k else []))  3.43 us
    pallas_call x1, Pallas kernels, body_call(): pl.pallas_call(functools.partial(body_kernel, part.shape, chunk), in_spec...  2.45 us
    pallas_call x1, Pallas kernels, local_call(): pl.pallas_call(functools.partial(local_kernel, (cases, nx, ny, depth), 16...  2.23 us
    pallas_call x1, Pallas kernels, rest_call(): pl.pallas_call(functools.partial(rest_kernel, t.shape, chunk), in_specs=[...  1.87 us
    ppermute x1, starting transfers between devices, shards(): lax.ppermute(x_sends[k], 'gx', swap_pairs(gx, k))  1.84 us
    ppermute x3, waiting for transfers between devices, shards(): msgs = [lax.ppermute(send, 'gz', xor_pairs(nz, m)) for m in swap_order(nz)]  1.51 us
  transfers between devices with their start and end apart: 7, of which 2 were waited for; matrix products, arithmetic and copies ran while one was open for 0% of the time, Pallas kernels for 28%

profile of v7, /device:TPU:1, one launch (start us, length us, event | category | flops | bytes accessed | tf_op | source)
XLA Modules:
  0.0 26.8 jit_solution(13917098352345008396)
XLA Ops:
  0.6 4.8 %faces.1 = (bf16[8,4224]{1,0:T(8,128)(2,1)S(1)}, f32[8,4224]{1,0:T(8,128)S(1)}, bf16[4096,512]{1,0:T(8,128)(2,1)S(1)}, f32[64,64,128]{2,1,0:T(8,128)S(1)}, s32[6...) custom-call(s32[4]{0:T(128)} %refs_0_.1, f32[16]{0:T(128)} %refs_1_.1, f32[4,128]{1,0:T(4,128)} %refs_2_.1, ...), custom_call_target="tpu_custom_call" | custom-call | tf_op jit(solution)/shard_map/faces/pallas_call | solution.py:194
  5.4 3.2 %collective-permute-start = (bf16[8,4224]{1,0:T(8,128)(2,1)S(1)}, bf16[8,4224]{1,0:T(8,128)(2,1)S(1)}, u32[]{:S(2)}, u32[]{:S(2)}) collective-permute-start(bf16[8,4224]{1,0:T(8,128)(2,1)S(1)} %get-tuple-element.31), channel_id=1, source_target_pairs={{0,16},{8,24},{16,0},{24,8},{1,17},{9,25},{17,1},{25,9},{2,18},{10... | collective-permute-start | bytes 202760 | tf_op jit(solution)/shard_map/ppermute | solution.py:614
  8.6 1.1 %collective-permute-start.1 = (bf16[8,4224]{1,0:T(8,128)(2,1)S(1)}, bf16[8,4224]{1,0:T(8,128)(2,1)S(1)}, u32[]{:S(2)}, u32[]{:S(2)}) collective-permute-start(bf16[8,4224]{1,0:T(8,128)(2,1)S(1)} %get-tuple-element.31), channel_id=1, source_target_pairs={{0,24},{8,16},{16,8},{24,0},{1,25},{9,17},{17,9},{25,1},{2,26},{10... | collective-permute-start | bytes 202760 | tf_op jit(solution)/shard_map/ppermute | solution.py:614
  9.7 0.2 collective-permute-start.2
  9.9 2.2 %local.1 = (f32[64,64,128]{2,1,0:T(8,128)S(1)}, f32[64,64,128]{2,1,0:T(8,128)S(1)}, bf16[32,128]{1,0:T(8,128)(2,1)S(1)}) custom-call(bf16[4096,512]{1,0:T(8,128)(2,1)S(1)} %get-tuple-element.32.source_ref, f32[64,64,128]{2,1,0:T(8,128)S(1)} %get-tuple-element.33.density_ref, s32[64,64,128]{2,1,0:T(8,128)S(1)} %get-tuple-element.34.mask_ref, ...), custom_call_target="tpu_custom_call" | custom-call | tf_op jit(solution)/shard_map/local/pallas_call | solution.py:255
  12.2 0.0 collective-permute-done.refs_1_
  12.2 1.5 %collective-permute-done.1.refs_2_ = bf16[8,4224]{1,0:T(8,128)(2,1)S(1)} collective-permute-done((bf16[8,4224]{1,0:T(8,128)(2,1)S(1)}, bf16[8,4224]{1,0:T(8,128)(2,1)S(1)}, u32[]{:S(2)}, u32[]{:S(2)}) %collective-permute-start.1) | collective-permute-done | bytes 67616 | tf_op jit(solution)/shard_map/ppermute | solution.py:614
  13.7 0.0 collective-permute-done.2.refs_3_
  13.7 0.5 %head.1 = (bf16[32,4096]{1,0:T(8,128)(2,1)S(1)}, bf16[208,128]{1,0:T(8,128)(2,1)S(1)}) custom-call(f32[8,4224]{1,0:T(8,128)S(1)} %get-tuple-element.30.refs_0_, bf16[8,4224]{1,0:T(8,128)(2,1)S(1)} %collective-permute-done.refs_1_, bf16[8,4224]{1,0:T(8,128)(2,1)S(1)} %collective-permute-done.1.refs_2_, bf16[8,4224]{1,0:T(8,128)(2,1)S(1)} %collective-permute-done.2.refs_3_, ...), custom_call_target="tpu_custom_call" | custom-call | tf_op jit(solution)/shard_map/head/pallas_call | solution.py:320
  14.2 1.8 %collective-permute-start.3 = (bf16[208,128]{1,0:T(8,128)(2,1)S(1)}, bf16[208,128]{1,0:T(8,128)(2,1)S(1)}, u32[]{:S(2)}, u32[]{:S(2)}) collective-permute-start(bf16[208,128]{1,0:T(8,128)(2,1)S(1)} %get-tuple-element.42.refs_2_), channel_id=1, source_target_pairs={{0,4},{4,0},{1,5},{5,1},{2,6},{6,2},{3,7},{7,3},{8,12},{12,8},{9,1... | collective-permute-start | bytes 159752 | tf_op jit(solution)/shard_map/ppermute | solution.py:620
  16.1 2.4 %body.1 = (f32[64,64,128]{2,1,0:T(8,128)S(1)}, f32[64,64,128]{2,1,0:T(8,128)}, f32[64,8,128]{2,1,0:T(8,128)S(1)}, f32[64,8,128]{2,1,0:T(8,128)S(1)}) custom-call(bf16[32,4096]{1,0:T(8,128)(2,1)S(1)} %get-tuple-element.39.lhs_ref, bf16[32,128]{1,0:T(8,128)(2,1)S(1)} %get-tuple-element.38.refs_5_.umap_ref, ...), custom_call_target="tpu_custom_call" | custom-call | tf_op jit(solution)/shard_map/body/pallas_call | solution.py:449
  18.5 0.0 collective-permute-done.3.refs_1_
  18.5 0.3 %edge.1 = (bf16[208,128]{1,0:T(8,128)(2,1)S(1)}, bf16[208,128]{1,0:T(8,128)(2,1)S(1)}, f32[192,128]{1,0:T(8,128)S(1)}, f32[192,128]{1,0:T(8,128)S(1)}, f32[8,128]{1,0:T(8,128)S(1)}) custom-call(f32[64,64,128]{2,1,0:T(8,128)S(1)} %get-tuple-element.41.refs_0_.t_ref, bf16[208,128]{1,0:T(8,128)(2,1)S(1)} %collective-permute-done.3.refs_1_, ...), custom_call_target="tpu_custom_call" | custom-call | tf_op jit(solution)/shard_map/edge/pallas_call | solution.py:379
  18.9 3.4 %collective-permute-start.5 = (bf16[208,128]{1,0:T(8,128)(2,1)S(1)}, bf16[208,128]{1,0:T(8,128)(2,1)S(1)}, u32[]{:S(2)}, u32[]{:S(2)}) collective-permute-start(bf16[208,128]{1,0:T(8,128)(2,1)S(1)} %get-tuple-element.44), channel_id=1, source_target_pairs={{1,2},{2,1},{0,3},{3,0},{5,6},{6,5},{4,7},{7,4},{9,10},{10,9},{8,1... | collective-permute-start | bytes 159752 | tf_op jit(solution)/shard_map/ppermute | solution.py:625
  22.3 0.0 collective-permute-start.4
  22.3 1.9 %rest.1 = (f32[64,64,128]{2,1,0:T(8,128)}, f32[64,8,128]{2,1,0:T(8,128)S(1)}, f32[64,8,128]{2,1,0:T(8,128)S(1)}) custom-call(f32[64,64,128]{2,1,0:T(8,128)S(1)} %get-tuple-element.41.refs_0_.t_ref, f32[192,128]{1,0:T(8,128)S(1)} %get-tuple-element.45.xb_ref, ...), custom_call_target="tpu_custom_call", output_to_operand_aliasing={{0}: (4, {}), {1}: (5, {}), {2}: (6, {})} | custom-call | tf_op jit(solution)/shard_map/rest/pallas_call | solution.py:498
  24.2 0.5 %collective-permute-done.5.refs_1_.refs_3_ = bf16[208,128]{1,0:T(8,128)(2,1)S(1)} collective-permute-done((bf16[208,128]{1,0:T(8,128)(2,1)S(1)}, bf16[208,128]{1,0:T(8,128)(2,1)S(1)}, u32[]{:S(2)}, u32[]{:S(2)}) %collective-permute-start.5) | collective-permute-done | bytes 53280 | tf_op jit(solution)/shard_map/ppermute | solution.py:625
  24.7 0.4 %collective-permute-start.6 = (bf16[208,128]{1,0:T(8,128)(2,1)S(1)}, bf16[208,128]{1,0:T(8,128)(2,1)S(1)}, u32[]{:S(2)}, u32[]{:S(2)}) collective-permute-start(bf16[208,128]{1,0:T(8,128)(2,1)S(1)} %collective-permute-done.5.refs_1_.refs_3_), channel_id=1, source_target_pairs={{0,1},{1,0},{2,3},{3,2},{4,5},{5,4},{6,7},{7,6},{8,9},{9,8},{10,11... | collective-permute-start | bytes 159752 | tf_op jit(solution)/shard_map/ppermute | solution.py:629
  25.1 0.0 collective-permute-done.4.refs_0_.refs_2_
  25.1 1.0 %finish.1 = (f32[64,64,128]{2,1,0:T(8,128)}, f32[8,128]{1,0:T(8,128)S(1)}) custom-call(bf16[208,128]{1,0:T(8,128)(2,1)S(1)} %collective-permute-done.4.refs_0_.refs_2_, bf16[208,128]{1,0:T(8,128)(2,1)S(1)} %collective-permute-done.5.refs_1_.refs_3_, f32[64,8,128]{2,1,0:T(8,128)S(1)} %get-tuple-element.52.refs_2_, ...), custom_call_target="tpu_custom_call", output_to_operand_aliasing={{0}: (5, {})} | custom-call | tf_op jit(solution)/shard_map/finish/pallas_call | solution.py:558
  26.1 0.0 collective-permute-done.6.refs_4_
  26.1 0.7 %mean.1 = f32[4]{0:T(128)} custom-call(f32[8,128]{1,0:T(8,128)S(1)} %get-tuple-element.56.refs_0_, f32[8,128]{1,0:T(8,128)S(1)} %get-tuple-element.57.refs_1_, bf16[208,128]{1,0:T(8,128)(2,1)S(1)} %collective-permute-done.4.refs_0_.refs_2_, bf16[208,128]{1,0:T(8,128)(2,1)S(1)} %collective-permute-done.5.refs_1_.refs_3_, ...), custom_call_target="tpu_custom_call" | custom-call | tf_op jit(solution)/shard_map/mean/pallas_call | solution.py:580
Async XLA Ops:
  5.4 6.7 %collective-permute-start = (bf16[8,4224]{1,0:T(8,128)(2,1)S(1)}, bf16[8,4224]{1,0:T(8,128)(2,1)S(1)}, u32[]{:S(2)}, u32[]{:S(2)}) collective-permute-start(bf16[8,4224]{1,0:T(8,128)(2,1)S(1)} %get-tuple-element.31), channel_id=1, source_target_pairs={{0,16},{8,24},{16,0},{24,8},{1,17},{9,25},{17,1},{25,9},{2,18},{10... | collective-permute-start | bytes 202760 | tf_op jit(solution)/shard_map/ppermute | solution.py:614
  8.6 5.0 %collective-permute-start.1 = (bf16[8,4224]{1,0:T(8,128)(2,1)S(1)}, bf16[8,4224]{1,0:T(8,128)(2,1)S(1)}, u32[]{:S(2)}, u32[]{:S(2)}) collective-permute-start(bf16[8,4224]{1,0:T(8,128)(2,1)S(1)} %get-tuple-element.31), channel_id=1, source_target_pairs={{0,24},{8,16},{16,8},{24,0},{1,25},{9,17},{17,9},{25,1},{2,26},{10... | collective-permute-start | bytes 202760 | tf_op jit(solution)/shard_map/ppermute | solution.py:614
  9.7 4.0 %collective-permute-start.2 = (bf16[8,4224]{1,0:T(8,128)(2,1)S(1)}, bf16[8,4224]{1,0:T(8,128)(2,1)S(1)}, u32[]{:S(2)}, u32[]{:S(2)}) collective-permute-start(bf16[8,4224]{1,0:T(8,128)(2,1)S(1)} %get-tuple-element.31), channel_id=1, source_target_pairs={{0,8},{8,0},{16,24},{24,16},{1,9},{9,1},{17,25},{25,17},{2,10},{10... | collective-permute-start | bytes 202760 | tf_op jit(solution)/shard_map/ppermute | solution.py:614
  14.2 4.3 %collective-permute-start.3 = (bf16[208,128]{1,0:T(8,128)(2,1)S(1)}, bf16[208,128]{1,0:T(8,128)(2,1)S(1)}, u32[]{:S(2)}, u32[]{:S(2)}) collective-permute-start(bf16[208,128]{1,0:T(8,128)(2,1)S(1)} %get-tuple-element.42.refs_2_), channel_id=1, source_target_pairs={{0,4},{4,0},{1,5},{5,1},{2,6},{6,2},{3,7},{7,3},{8,12},{12,8},{9,1... | collective-permute-start | bytes 159752 | tf_op jit(solution)/shard_map/ppermute | solution.py:620
  18.9 5.8 %collective-permute-start.5 = (bf16[208,128]{1,0:T(8,128)(2,1)S(1)}, bf16[208,128]{1,0:T(8,128)(2,1)S(1)}, u32[]{:S(2)}, u32[]{:S(2)}) collective-permute-start(bf16[208,128]{1,0:T(8,128)(2,1)S(1)} %get-tuple-element.44), channel_id=1, source_target_pairs={{1,2},{2,1},{0,3},{3,0},{5,6},{6,5},{4,7},{7,4},{9,10},{10,9},{8,1... | collective-permute-start | bytes 159752 | tf_op jit(solution)/shard_map/ppermute | solution.py:625
  22.3 2.8 %collective-permute-start.4 = (bf16[208,128]{1,0:T(8,128)(2,1)S(1)}, bf16[208,128]{1,0:T(8,128)(2,1)S(1)}, u32[]{:S(2)}, u32[]{:S(2)}) collective-permute-start(bf16[208,128]{1,0:T(8,128)(2,1)S(1)} %get-tuple-element.43), channel_id=1, source_target_pairs={{0,1},{1,0},{2,3},{3,2},{4,5},{5,4},{6,7},{7,6},{8,9},{9,8},{10,11... | collective-permute-start | bytes 159752 | tf_op jit(solution)/shard_map/ppermute | solution.py:625
  24.7 1.4 %collective-permute-start.6 = (bf16[208,128]{1,0:T(8,128)(2,1)S(1)}, bf16[208,128]{1,0:T(8,128)(2,1)S(1)}, u32[]{:S(2)}, u32[]{:S(2)}) collective-permute-start(bf16[208,128]{1,0:T(8,128)(2,1)S(1)} %collective-permute-done.5.refs_1_.refs_3_), channel_id=1, source_target_pairs={{0,1},{1,0},{2,3},{3,2},{4,5},{5,4},{6,7},{7,6},{8,9},{9,8},{10,11... | collective-permute-start | bytes 159752 | tf_op jit(solution)/shard_map/ppermute | solution.py:629

commit v8 on v7

--- a/solution.py
+++ b/solution.py
@@ -217,8 +217,9 @@
     )(*in_hbm(case_index, case_weight, decay, density, design_mask, energy))
 
 
-def local_kernel(shape, bx, source_ref, density_ref, mask_ref, map_ref, rows_ref, t_ref, factor_ref, umap_ref, rmat):
+def local_kernel(shape, bx, source_ref, density_ref, mask_ref, map_ref, rows_ref, t_ref, factor_ref, umap_ref, *rest):
     cases, nx, ny, depth = shape
+    *sends, rmat = rest
     steps, cols = nx // bx, bx * ny
     row = lax.broadcasted_iota(jnp.int32, (depth, depth), 0)
     col = lax.broadcasted_iota(jnp.int32, (depth, depth), 1)
@@ -247,20 +248,26 @@
         at = slice(s * bx, (s + 1) * bx)
         t_ref[at] = (both[:, 0:depth] + both[:, depth : 2 * depth]).reshape(bx, ny, depth)
         factor_ref[at] = jnp.where(mask_ref[at] == 0, 1.0 / jnp.maximum(density_ref[at], 0.1), 0.0)
-
-
-def local_call(source, density, mask, maps, rows):
+    low = lax.axis_index("gx") % 2 == 1
+    for k, ref in enumerate(sends):
+        bottom = low if k == 0 else jnp.logical_not(low)
+        start = jnp.where(bottom, 0, nx - RADIUS)
+        ref[...] = t_ref[pl.ds(start, RADIUS)].reshape(RADIUS * ny, depth).astype(BF16)
+
+
+def local_call(source, density, mask, maps, rows, nsends):
     nx, ny, depth = density.shape
     cases = maps.shape[0]
     return pl.pallas_call(
         functools.partial(local_kernel, (cases, nx, ny, depth), 16),
         in_specs=[VMEM] * 5,
-        out_specs=[VMEM] * 3,
+        out_specs=[VMEM] * (3 + nsends),
         out_shape=[
             pltpu.VMEM(density.shape, F32),
             pltpu.VMEM(density.shape, F32),
             pltpu.VMEM((8 * cases, depth), BF16),
-        ],
+        ]
+        + [pltpu.VMEM((RADIUS * ny, depth), BF16)] * nsends,
         scratch_shapes=[pltpu.VMEM((cases * depth, 2 * depth), BF16)],
         compiler_params=pltpu.CompilerParams(vmem_limit_bytes=16 * MIB),
         name="local",
@@ -271,8 +278,8 @@
     cases, nx, ny, depth = shape
     own_ref = refs[0]
     msgs = refs[1:nslabs]
-    t_ref, umap_ref, lhs_ref = refs[nslabs : 3 + nslabs]
-    sends = refs[3 + nslabs : 3 + nslabs + nsends]
+    lhs_ref = refs[nslabs]
+    sends = refs[1 + nslabs : 1 + nslabs + nsends]
     stack = refs[-1]
     cols = nx * ny
     mine = lax.axis_index("gz")
@@ -302,31 +309,29 @@
     lhs_ref[...] = jnp.concatenate([hi, faces - hi, hi, jnp.zeros_like(hi)], axis=0).astype(BF16)
     aux = pad_rows(put_lanes(split3(total)), 16).astype(BF16)
     rows = RADIUS + 1
-    wide, edge = rows * ny, RADIUS * ny
+    wide = rows * ny
     for k, ref in enumerate(sends):
         bottom = low if k == 0 else jnp.logical_not(low)
-        start = jnp.where(bottom, 0, nx - rows)
-        part = lhs_ref[:, pl.ds(pl.multiple_of(start * ny, wide), wide)]
-        add = lax.dot_general(part, umap_ref[...], (((0,), (0,)), ((), ())), preferred_element_type=F32)
-        full = t_ref[pl.ds(start, rows)].reshape(wide, depth) + add
-        ref[0:edge, :] = jnp.where(bottom, full[0:edge], full[ny:wide]).astype(BF16)
-        ref[edge:, :] = aux
-
-
-def head_call(own, msgs, t_local, umap, nsends, swapped):
-    nx, ny, depth = t_local.shape
+        start = jnp.where(bottom, 0, nx - rows) * ny
+        ref[0:16, :] = lhs_ref[0:16, pl.ds(pl.multiple_of(start, wide), wide)]
+        ref[16:32, 0:LANES] = aux
+        ref[16:32, LANES:] = jnp.zeros((16, wide - LANES), BF16)
+
+
+def head_call(own, msgs, shape, nsends, swapped):
+    nx, ny, depth = shape
     cases = own.shape[0] // 2
     nslabs = len(msgs) + 1
     return pl.pallas_call(
         functools.partial(head_kernel, (cases, nx, ny, depth), nslabs, nsends, swapped),
-        in_specs=[VMEM] * (nslabs + 2),
+        in_specs=[VMEM] * nslabs,
         out_specs=[VMEM] * (1 + nsends),
         out_shape=[pltpu.VMEM((8 * cases, nx * ny), BF16)]
-        + [jax.ShapeDtypeStruct((RADIUS * ny + 16, depth), BF16)] * nsends,
+        + [pltpu.VMEM((32, (RADIUS + 1) * ny), BF16)] * nsends,
         scratch_shapes=[pltpu.VMEM((nslabs,) + own.shape, F32)],
         compiler_params=pltpu.CompilerParams(vmem_limit_bytes=20 * MIB),
         name="head",
-    )(own, *msgs, *in_vmem(t_local), umap)
+    )(own, *msgs)
 
 
 def sided(even, got):
@@ -337,22 +342,29 @@
 
 def edge_kernel(shape, nx_sends, ny_sends, *refs):
     cases, nx, ny, depth = shape
-    t_ref = refs[0]
-    got_refs = refs[1 : 1 + nx_sends]
-    own_send = refs[1 + nx_sends]
-    sends = refs[2 + nx_sends : 2 + nx_sends + ny_sends]
-    xb_ref, xa_ref, sums_ref, line = refs[2 + nx_sends + ny_sends :]
+    t_ref, umap_ref = refs[0:2]
+    part_refs = refs[2 : 2 + nx_sends]
+    got_refs = refs[2 + nx_sends : 2 + 2 * nx_sends]
+    own_send = refs[2 + 2 * nx_sends]
+    sends = refs[3 + 2 * nx_sends : 3 + 2 * nx_sends + ny_sends]
+    xb_ref, xa_ref, sums_ref, line = refs[3 + 2 * nx_sends + ny_sends :]
     taps = taps_1d()
     edge = RADIUS * ny
     even_x = lax.axis_index("gx") % 2 == 0
     flip_y = lax.axis_index("gy") % 2 == 1
-    blocks = [r[0:edge, :].astype(F32) for r in got_refs]
+    blocks = []
+    for k, (part, got) in enumerate(zip(part_refs, got_refs)):
+        lhs = got[0:16, :]
+        lhs = jnp.concatenate([lhs, pad_rows(lhs[0:8], 16)], axis=0)
+        add = lax.dot_general(lhs, umap_ref[...], (((0,), (0,)), ((), ())), preferred_element_type=F32)
+        first_rows = even_x if k == 0 else jnp.logical_not(even_x)
+        blocks.append(part[...].astype(F32) + jnp.where(first_rows, add[0:edge], add[ny:]))
     before, after = sided(even_x, blocks)
     xb_ref[...] = before
     xa_ref[...] = after
-    total = sum3(own_send[edge : edge + 16, :].astype(F32), 0)
+    total = sum3(own_send[16:32, 0:LANES].astype(F32), 0)
     for ref in got_refs:
-        total = total + sum3(ref[edge : edge + 16, :].astype(F32), 0)
+        total = total + sum3(ref[16:32, 0:LANES].astype(F32), 0)
     sums_ref[...] = jnp.broadcast_to(total[0:8], (8, LANES))
     aux = put_lanes(split3(total)).astype(BF16)
     flat = t_ref.reshape(nx * ny, depth)
@@ -374,11 +386,11 @@
         ref[RADIUS * nx :, :] = aux
 
 
-def edge_call(t, got, own_send, ny_sends, cases):
+def edge_call(t, umap, parts, got, own_send, ny_sends, cases):
     nx, ny, depth = t.shape
     return pl.pallas_call(
         functools.partial(edge_kernel, (cases, nx, ny, depth), len(got), ny_sends),
-        in_specs=[VMEM] * (2 + len(got)),
+        in_specs=[VMEM] * (3 + 2 * len(got)),
         out_specs=[VMEM] * (ny_sends + 3),
         out_shape=[jax.ShapeDtypeStruct((RADIUS * nx + 16, depth), BF16)] * ny_sends
         + [jax.ShapeDtypeStruct((RADIUS * ny, depth), F32)] * 2
@@ -386,7 +398,7 @@
         scratch_shapes=[pltpu.VMEM((nx + 16, depth), F32)],
         compiler_params=pltpu.CompilerParams(vmem_limit_bytes=16 * MIB),
         name="edge",
-    )(t, *got, own_send)
+    )(t, umap, *parts, *got, own_send)
 
 
 def filter_row(ny, read, line, factor):
@@ -429,7 +441,7 @@
 
 
 def split_row(nx):
-    return nx * 9 // 16
+    return nx * 11 // 32
 
 
 def body_kernel(shape, chunk, lhs_ref, umap_ref, part_ref, factor_ref, t_ref, out_hbm, first_ref, last_ref, line, out_ref, sem):
@@ -445,7 +457,7 @@
 
 def body_call(lhs, umap, part, factor):
     nx, ny, depth = part.shape
-    chunk = 11
+    chunk = 10
     return pl.pallas_call(
         functools.partial(body_kernel, part.shape, chunk),
         in_specs=[VMEM] * 4,
@@ -494,7 +506,7 @@
 
 def rest_call(t, xb, xa, factor, out, first, last):
     nx, ny, depth = t.shape
-    chunk = 9
+    chunk = 13
     return pl.pallas_call(
         functools.partial(rest_kernel, t.shape, chunk),
         in_specs=[VMEM] * 4 + [HBM, VMEM, VMEM],
@@ -615,11 +627,12 @@
     else:
         every = lax.all_gather(send, "gz")
         own, *msgs = [every[j] for j in range(nz)]
-    part, factor, umap = local_call(source, density_v, mask_v, maps, rows)
-    lhs, *x_sends = head_call(own, msgs, part, umap, max(swaps_of(gx), 1), swapped)
+    part, factor, umap, *x_parts = local_call(source, density_v, mask_v, maps, rows, swaps_of(gx))
+    x_parts = [lax.ppermute(v, "gx", swap_pairs(gx, k)) for k, v in enumerate(x_parts)]
+    lhs, *x_sends = head_call(own, msgs, part.shape, max(swaps_of(gx), 1), swapped)
     x_got = [lax.ppermute(x_sends[k], "gx", swap_pairs(gx, k)) for k in range(swaps_of(gx))]
     t, out, first, last = body_call(lhs, umap, part, factor)
-    *y_sends, xb, xa, sums = edge_call(t, x_got, x_sends[0], swaps_of(gy), cases)
+    *y_sends, xb, xa, sums = edge_call(t, umap, x_parts, x_got, x_sends[0], swaps_of(gy), cases)
     ring = gy == 4
     ends = [(0, gy - 1), (gy - 1, 0)] if ring else []
     y_got = [lax.ppermute(y_sends[k], "gy", swap_pairs(gy, k) + (ends if k else [])) for k in range(swaps_of(gy))]

time: 27.1 us -> 26.9 us (level)
  waiting for transfers between devices: 2 us -> 0.24 us
  starting transfers between devices: 10.2 us -> 11.7 us
    ppermute x3, waiting for transfers between devices: 1.51 us -> 0.23 us  [shards(): msgs = [lax.ppermute(send, 'gz', xor_pairs(nz, m)) for m in swap_order(nz)]]
    ppermute x0 -> x1, starting transfers between devices: none -> 1.27 us  [shards(): lax.ppermute(v, 'gx', swap_pairs(gx, k))]
    pallas_call x1, Pallas kernels: 1.87 us -> 2.42 us  [rest_call(): pl.pallas_call(functools.partial(rest_kernel, t.shape, chunk), in_specs=[...]
    pallas_call x1, Pallas kernels: 2.45 us -> 1.93 us  [body_call(): pl.pallas_call(functools.partial(body_kernel, part.shape, chunk), in_spec...]
    ppermute x2, waiting for transfers between devices: 0.48 us -> 0.01 us  [shards(): lax.ppermute(y_sends[k], 'gy', swap_pairs(gy, k) + (ends if k else []))]
  transfers between devices with their start and end apart: 7 -> 8, of which waited for: 2 -> 1; matrix products, arithmetic and copies ran while one was open for 0% -> 0% of each run, Pallas kernels for 28% -> 30%
where the time goes in v8:
time: 26.9 us; the launch traced here: 26.6 us
  Pallas kernels  13.9 us (52%)
  starting transfers between devices  11.7 us (43%)
  between operations  0.72 us (3%)
    pallas_call x1, Pallas kernels, faces_call(): pl.pallas_call(functools.partial(faces_kernel, energy.shape, cuts), in_sp...  4.79 us
    ppermute x3, starting transfers between devices, shards(): msgs = [lax.ppermute(send, 'gz', xor_pairs(nz, m)) for m in swap_order(nz)]  4.49 us
    ppermute x2, starting transfers between devices, shards(): lax.ppermute(y_sends[k], 'gy', swap_pairs(gy, k) + (ends if k else []))  3.54 us
    pallas_call x1, Pallas kernels, rest_call(): pl.pallas_call(functools.partial(rest_kernel, t.shape, chunk), in_specs=[...  2.42 us
    pallas_call x1, Pallas kernels, local_call(): pl.pallas_call(functools.partial(local_kernel, (cases, nx, ny, depth), 16...  2.25 us
    pallas_call x1, Pallas kernels, body_call(): pl.pallas_call(functools.partial(body_kernel, part.shape, chunk), in_spec...  1.93 us
    ppermute x1, starting transfers between devices, shards(): lax.ppermute(x_sends[k], 'gx', swap_pairs(gx, k))  1.84 us
    ppermute x1, starting transfers between devices, shards(): lax.ppermute(v, 'gx', swap_pairs(gx, k))  1.27 us
  transfers between devices with their start and end apart: 8, of which 1 were waited for; matrix products, arithmetic and copies ran while one was open for 0% of the time, Pallas kernels for 30%

profile of v8, /device:TPU:1, one launch (start us, length us, event | category | flops | bytes accessed | tf_op | source)
XLA Modules:
  0.0 26.6 jit_solution(6680742206376407404)
XLA Ops:
  0.6 4.8 %faces.1 = (bf16[8,4224]{1,0:T(8,128)(2,1)S(1)}, f32[8,4224]{1,0:T(8,128)S(1)}, bf16[4096,512]{1,0:T(8,128)(2,1)S(1)}, f32[64,64,128]{2,1,0:T(8,128)S(1)}, s32[6...) custom-call(s32[4]{0:T(128)} %refs_0_.1, f32[16]{0:T(128)} %refs_1_.1, f32[4,128]{1,0:T(4,128)} %refs_2_.1, ...), custom_call_target="tpu_custom_call" | custom-call | tf_op jit(solution)/shard_map/faces/pallas_call | solution.py:194
  5.4 3.2 %collective-permute-start = (bf16[8,4224]{1,0:T(8,128)(2,1)S(1)}, bf16[8,4224]{1,0:T(8,128)(2,1)S(1)}, u32[]{:S(2)}, u32[]{:S(2)}) collective-permute-start(bf16[8,4224]{1,0:T(8,128)(2,1)S(1)} %get-tuple-element.32), channel_id=1, source_target_pairs={{0,16},{8,24},{16,0},{24,8},{1,17},{9,25},{17,1},{25,9},{2,18},{10... | collective-permute-start | bytes 202760 | tf_op jit(solution)/shard_map/ppermute | solution.py:626
  8.6 1.1 %collective-permute-start.1 = (bf16[8,4224]{1,0:T(8,128)(2,1)S(1)}, bf16[8,4224]{1,0:T(8,128)(2,1)S(1)}, u32[]{:S(2)}, u32[]{:S(2)}) collective-permute-start(bf16[8,4224]{1,0:T(8,128)(2,1)S(1)} %get-tuple-element.32), channel_id=1, source_target_pairs={{0,24},{8,16},{16,8},{24,0},{1,25},{9,17},{17,9},{25,1},{2,26},{10... | collective-permute-start | bytes 202760 | tf_op jit(solution)/shard_map/ppermute | solution.py:626
  9.7 0.2 collective-permute-start.2
  9.9 2.2 %local.1 = (f32[64,64,128]{2,1,0:T(8,128)S(1)}, f32[64,64,128]{2,1,0:T(8,128)S(1)}, bf16[32,128]{1,0:T(8,128)(2,1)S(1)}, bf16[192,128]{1,0:T(8,128)(2,1)S(1)}) custom-call(bf16[4096,512]{1,0:T(8,128)(2,1)S(1)} %get-tuple-element.34.source_ref, f32[64,64,128]{2,1,0:T(8,128)S(1)} %get-tuple-element.35.density_ref, ...), custom_call_target="tpu_custom_call" | custom-call | tf_op jit(solution)/shard_map/local/pallas_call | solution.py:261
  12.2 1.3 %collective-permute-start.3 = (bf16[192,128]{1,0:T(8,128)(2,1)S(1)}, bf16[192,128]{1,0:T(8,128)(2,1)S(1)}, u32[]{:S(2)}, u32[]{:S(2)}) collective-permute-start(bf16[192,128]{1,0:T(8,128)(2,1)S(1)} %get-tuple-element.43), channel_id=1, source_target_pairs={{0,4},{4,0},{1,5},{5,1},{2,6},{6,2},{3,7},{7,3},{8,12},{12,8},{9,1... | collective-permute-start | bytes 147464 | tf_op jit(solution)/shard_map/ppermute | solution.py:631
  13.4 0.0 collective-permute-done.refs_1_
  13.4 0.2 collective-permute-done.1.refs_2_
  13.7 0.0 collective-permute-done.2.refs_3_
  13.7 0.3 %head.1 = (bf16[32,4096]{1,0:T(8,128)(2,1)S(1)}, bf16[32,256]{1,0:T(8,128)(2,1)S(1)}) custom-call(f32[8,4224]{1,0:T(8,128)S(1)} %get-tuple-element.31.refs_0_, bf16[8,4224]{1,0:T(8,128)(2,1)S(1)} %collective-permute-done.refs_1_, bf16[8,4224]{1,0:T(8,128)(2,1)S(1)} %collective-permute-done.1.refs_2_, bf16[8,4224]{1,0:T(8,128)(2,1)S(1)} %collective-permute-done.2.refs_3_), custom_call_target="tpu_custom_call" | custom-call | tf_op jit(solution)/shard_map/head/pallas_call | solution.py:325
  14.0 1.8 %collective-permute-start.4 = (bf16[32,256]{1,0:T(8,128)(2,1)S(1)}, bf16[32,256]{1,0:T(8,128)(2,1)S(1)}, u32[]{:S(2)}, u32[]{:S(2)}) collective-permute-start(bf16[32,256]{1,0:T(8,128)(2,1)S(1)} %get-tuple-element.44.refs_4_), channel_id=1, source_target_pairs={{0,4},{4,0},{1,5},{5,1},{2,6},{6,2},{3,7},{7,3},{8,12},{12,8},{9,1... | collective-permute-start | bytes 49160 | tf_op jit(solution)/shard_map/ppermute | solution.py:633
  15.9 1.9 %body.1 = (f32[64,64,128]{2,1,0:T(8,128)S(1)}, f32[64,64,128]{2,1,0:T(8,128)}, f32[64,8,128]{2,1,0:T(8,128)S(1)}, f32[64,8,128]{2,1,0:T(8,128)S(1)}) custom-call(bf16[32,4096]{1,0:T(8,128)(2,1)S(1)} %get-tuple-element.33.lhs_ref, bf16[32,128]{1,0:T(8,128)(2,1)S(1)} %get-tuple-element.39.umap_ref.refs_1_, f32[64,64,128]{2,1,0:T(8,128)S(1)} %get-tuple-element.40.part_ref, ...), custom_call_target="tpu_custom_call" | custom-call | tf_op jit(solution)/shard_map/body/pallas_call | solution.py:461
  17.8 0.0 collective-permute-done.3.refs_2_
  17.8 0.0 collective-permute-done.4.refs_3_
  17.8 0.4 %edge.1 = (bf16[208,128]{1,0:T(8,128)(2,1)S(1)}, bf16[208,128]{1,0:T(8,128)(2,1)S(1)}, f32[192,128]{1,0:T(8,128)S(1)}, f32[192,128]{1,0:T(8,128)S(1)}, f32[8,128]{1,0:T(8,128)S(1)}) custom-call(f32[64,64,128]{2,1,0:T(8,128)S(1)} %get-tuple-element.42.refs_0_.t_ref, bf16[32,128]{1,0:T(8,128)(2,1)S(1)} %get-tuple-element.39.umap_ref.refs_1_, ...), custom_call_target="tpu_custom_call" | custom-call | tf_op jit(solution)/shard_map/edge/pallas_call | solution.py:391
  18.3 3.5 %collective-permute-start.6 = (bf16[208,128]{1,0:T(8,128)(2,1)S(1)}, bf16[208,128]{1,0:T(8,128)(2,1)S(1)}, u32[]{:S(2)}, u32[]{:S(2)}) collective-permute-start(bf16[208,128]{1,0:T(8,128)(2,1)S(1)} %get-tuple-element.46), channel_id=1, source_target_pairs={{1,2},{2,1},{0,3},{3,0},{5,6},{6,5},{4,7},{7,4},{9,10},{10,9},{8,1... | collective-permute-start | bytes 159752 | tf_op jit(solution)/shard_map/ppermute | solution.py:638
  21.8 0.0 collective-permute-start.5
  21.8 2.4 %rest.1 = (f32[64,64,128]{2,1,0:T(8,128)}, f32[64,8,128]{2,1,0:T(8,128)S(1)}, f32[64,8,128]{2,1,0:T(8,128)S(1)}) custom-call(f32[64,64,128]{2,1,0:T(8,128)S(1)} %get-tuple-element.42.refs_0_.t_ref, f32[192,128]{1,0:T(8,128)S(1)} %get-tuple-element.47.xb_ref, ...), custom_call_target="tpu_custom_call", output_to_operand_aliasing={{0}: (4, {}), {1}: (5, {}), {2}: (6, {})} | custom-call | tf_op jit(solution)/shard_map/rest/pallas_call | solution.py:510
  24.2 0.0 collective-permute-done.6.refs_1_.refs_3_
  24.2 0.6 %collective-permute-start.7 = (bf16[208,128]{1,0:T(8,128)(2,1)S(1)}, bf16[208,128]{1,0:T(8,128)(2,1)S(1)}, u32[]{:S(2)}, u32[]{:S(2)}) collective-permute-start(bf16[208,128]{1,0:T(8,128)(2,1)S(1)} %collective-permute-done.6.refs_1_.refs_3_), channel_id=1, source_target_pairs={{0,1},{1,0},{2,3},{3,2},{4,5},{5,4},{6,7},{7,6},{8,9},{9,8},{10,11... | collective-permute-start | bytes 159752 | tf_op jit(solution)/shard_map/ppermute | solution.py:642
  24.8 0.0 collective-permute-done.5.refs_0_.refs_2_
  24.8 1.0 %finish.1 = (f32[64,64,128]{2,1,0:T(8,128)}, f32[8,128]{1,0:T(8,128)S(1)}) custom-call(bf16[208,128]{1,0:T(8,128)(2,1)S(1)} %collective-permute-done.5.refs_0_.refs_2_, bf16[208,128]{1,0:T(8,128)(2,1)S(1)} %collective-permute-done.6.refs_1_.refs_3_, f32[64,8,128]{2,1,0:T(8,128)S(1)} %get-tuple-element.54.refs_2_, ...), custom_call_target="tpu_custom_call", output_to_operand_aliasing={{0}: (5, {})} | custom-call | tf_op jit(solution)/shard_map/finish/pallas_call | solution.py:570
  25.9 0.0 collective-permute-done.7.refs_4_
  25.9 0.7 %mean.1 = f32[4]{0:T(128)} custom-call(f32[8,128]{1,0:T(8,128)S(1)} %get-tuple-element.58.refs_0_, f32[8,128]{1,0:T(8,128)S(1)} %get-tuple-element.59.refs_1_, bf16[208,128]{1,0:T(8,128)(2,1)S(1)} %collective-permute-done.5.refs_0_.refs_2_, bf16[208,128]{1,0:T(8,128)(2,1)S(1)} %collective-permute-done.6.refs_1_.refs_3_, ...), custom_call_target="tpu_custom_call" | custom-call | tf_op jit(solution)/shard_map/mean/pallas_call | solution.py:592
Async XLA Ops:
  5.4 8.0 %collective-permute-start = (bf16[8,4224]{1,0:T(8,128)(2,1)S(1)}, bf16[8,4224]{1,0:T(8,128)(2,1)S(1)}, u32[]{:S(2)}, u32[]{:S(2)}) collective-permute-start(bf16[8,4224]{1,0:T(8,128)(2,1)S(1)} %get-tuple-element.32), channel_id=1, source_target_pairs={{0,16},{8,24},{16,0},{24,8},{1,17},{9,25},{17,1},{25,9},{2,18},{10... | collective-permute-start | bytes 202760 | tf_op jit(solution)/shard_map/ppermute | solution.py:626
  8.6 5.0 %collective-permute-start.1 = (bf16[8,4224]{1,0:T(8,128)(2,1)S(1)}, bf16[8,4224]{1,0:T(8,128)(2,1)S(1)}, u32[]{:S(2)}, u32[]{:S(2)}) collective-permute-start(bf16[8,4224]{1,0:T(8,128)(2,1)S(1)} %get-tuple-element.32), channel_id=1, source_target_pairs={{0,24},{8,16},{16,8},{24,0},{1,25},{9,17},{17,9},{25,1},{2,26},{10... | collective-permute-start | bytes 202760 | tf_op jit(solution)/shard_map/ppermute | solution.py:626
  9.7 4.0 %collective-permute-start.2 = (bf16[8,4224]{1,0:T(8,128)(2,1)S(1)}, bf16[8,4224]{1,0:T(8,128)(2,1)S(1)}, u32[]{:S(2)}, u32[]{:S(2)}) collective-permute-start(bf16[8,4224]{1,0:T(8,128)(2,1)S(1)} %get-tuple-element.32), channel_id=1, source_target_pairs={{0,8},{8,0},{16,24},{24,16},{1,9},{9,1},{17,25},{25,17},{2,10},{10... | collective-permute-start | bytes 202760 | tf_op jit(solution)/shard_map/ppermute | solution.py:626
  12.2 5.6 %collective-permute-start.3 = (bf16[192,128]{1,0:T(8,128)(2,1)S(1)}, bf16[192,128]{1,0:T(8,128)(2,1)S(1)}, u32[]{:S(2)}, u32[]{:S(2)}) collective-permute-start(bf16[192,128]{1,0:T(8,128)(2,1)S(1)} %get-tuple-element.43), channel_id=1, source_target_pairs={{0,4},{4,0},{1,5},{5,1},{2,6},{6,2},{3,7},{7,3},{8,12},{12,8},{9,1... | collective-permute-start | bytes 147464 | tf_op jit(solution)/shard_map/ppermute | solution.py:631
  14.0 3.8 %collective-permute-start.4 = (bf16[32,256]{1,0:T(8,128)(2,1)S(1)}, bf16[32,256]{1,0:T(8,128)(2,1)S(1)}, u32[]{:S(2)}, u32[]{:S(2)}) collective-permute-start(bf16[32,256]{1,0:T(8,128)(2,1)S(1)} %get-tuple-element.44.refs_4_), channel_id=1, source_target_pairs={{0,4},{4,0},{1,5},{5,1},{2,6},{6,2},{3,7},{7,3},{8,12},{12,8},{9,1... | collective-permute-start | bytes 49160 | tf_op jit(solution)/shard_map/ppermute | solution.py:633
  18.3 6.0 %collective-permute-start.6 = (bf16[208,128]{1,0:T(8,128)(2,1)S(1)}, bf16[208,128]{1,0:T(8,128)(2,1)S(1)}, u32[]{:S(2)}, u32[]{:S(2)}) collective-permute-start(bf16[208,128]{1,0:T(8,128)(2,1)S(1)} %get-tuple-element.46), channel_id=1, source_target_pairs={{1,2},{2,1},{0,3},{3,0},{5,6},{6,5},{4,7},{7,4},{9,10},{10,9},{8,1... | collective-permute-start | bytes 159752 | tf_op jit(solution)/shard_map/ppermute | solution.py:638
  21.8 3.0 %collective-permute-start.5 = (bf16[208,128]{1,0:T(8,128)(2,1)S(1)}, bf16[208,128]{1,0:T(8,128)(2,1)S(1)}, u32[]{:S(2)}, u32[]{:S(2)}) collective-permute-start(bf16[208,128]{1,0:T(8,128)(2,1)S(1)} %get-tuple-element.45), channel_id=1, source_target_pairs={{0,1},{1,0},{2,3},{3,2},{4,5},{5,4},{6,7},{7,6},{8,9},{9,8},{10,11... | collective-permute-start | bytes 159752 | tf_op jit(solution)/shard_map/ppermute | solution.py:638
  24.2 1.6 %collective-permute-start.7 = (bf16[208,128]{1,0:T(8,128)(2,1)S(1)}, bf16[208,128]{1,0:T(8,128)(2,1)S(1)}, u32[]{:S(2)}, u32[]{:S(2)}) collective-permute-start(bf16[208,128]{1,0:T(8,128)(2,1)S(1)} %collective-permute-done.6.refs_1_.refs_3_), channel_id=1, source_target_pairs={{0,1},{1,0},{2,3},{3,2},{4,5},{5,4},{6,7},{7,6},{8,9},{9,8},{10,11... | collective-permute-start | bytes 159752 | tf_op jit(solution)/shard_map/ppermute | solution.py:642

commit v9 on v8

--- a/solution.py
+++ b/solution.py
@@ -68,7 +68,6 @@
 class Slab:
     def __init__(self, decay):
         cases, depth = decay.shape
-        self.decay = decay
         self.row = lax.broadcasted_iota(jnp.int32, (depth, depth), 0)
         self.col = lax.broadcasted_iota(jnp.int32, (depth, depth), 1)
         logs = jnp.log(decay)
@@ -148,7 +147,7 @@
 
     sums = [jnp.zeros((8, depth), F32) for _ in range(cases)]
 
-    def faces_of(at, span):
+    def faces_of(span):
         faces = lax.dot_general(
             wmat, source_ref[span, :], (((1,), (1,)), ((), ())), preferred_element_type=F32)
         faces = faces[0 : 2 * cases] + faces[2 * cases : 4 * cases]
@@ -171,7 +170,7 @@
             work = cube * energy_ref[c, at].astype(F32)
             sums[c] = sums[c] + jnp.sum(work.reshape(cols // 8, 8, depth), axis=0)
             source_ref[span, c * depth : (c + 1) * depth] = work.astype(BF16).reshape(cols, depth)
-        faces_of(at, span)
+        faces_of(span)
 
     total = jnp.concatenate([jnp.sum(jnp.sum(v, axis=0, keepdims=True), axis=1, keepdims=True) for v in sums], axis=0)
     turn = jnp.concatenate(turns, axis=0)
@@ -275,7 +274,7 @@
 
 
 def head_kernel(shape, nslabs, nsends, swapped, *refs):
-    cases, nx, ny, depth = shape
+    cases, nx, ny, _ = shape
     own_ref = refs[0]
     msgs = refs[1:nslabs]
     lhs_ref = refs[nslabs]
@@ -341,7 +340,7 @@
 
 
 def edge_kernel(shape, nx_sends, ny_sends, *refs):
-    cases, nx, ny, depth = shape
+    _, nx, ny, depth = shape
     t_ref, umap_ref = refs[0:2]
     part_refs = refs[2 : 2 + nx_sends]
     got_refs = refs[2 + nx_sends : 2 + 2 * nx_sends]
@@ -441,7 +440,7 @@
 
 
 def split_row(nx):
-    return nx * 11 // 32
+    return nx * 28 // 64
 
 
 def body_kernel(shape, chunk, lhs_ref, umap_ref, part_ref, factor_ref, t_ref, out_hbm, first_ref, last_ref, line, out_ref, sem):
@@ -565,7 +564,7 @@
 
 
 def finish_call(got, first, last, factor, out):
-    nx, ny, depth = out.shape
+    nx, _, depth = out.shape
     nin = len(got)
     return pl.pallas_call(
         functools.partial(finish_kernel, out.shape, len(got)),
@@ -635,7 +634,9 @@
     *y_sends, xb, xa, sums = edge_call(t, umap, x_parts, x_got, x_sends[0], swaps_of(gy), cases)
     ring = gy == 4
     ends = [(0, gy - 1), (gy - 1, 0)] if ring else []
-    y_got = [lax.ppermute(y_sends[k], "gy", swap_pairs(gy, k) + (ends if k else [])) for k in range(swaps_of(gy))]
+    y_got = []
+    for k in range(swaps_of(gy)):
+        y_got.append(lax.ppermute(y_sends[k], "gy", swap_pairs(gy, k) + (ends if k else [])))
     out, first, last = rest_call(t, xb, xa, factor, out, first, last)
     if ring:
         y_got[1], first = lax.optimization_barrier((y_got[1], first))

time: 26.9 us -> 26.6 us (0.989)
  starting transfers between devices: 11.7 us -> 11.4 us
    pallas_call x1, Pallas kernels: 2.42 us -> 2.13 us  [rest_call(): pl.pallas_call(functools.partial(rest_kernel, t.shape, chunk), in_specs=[...]
  transfers between devices with their start and end apart: 8 -> 8, of which waited for: 1 -> 2; matrix products, arithmetic and copies ran while one was open for 0% -> 0% of each run, Pallas kernels for 30% -> 30%
where the time goes in v9:
time: 26.6 us; the launch traced here: 26.3 us
  Pallas kernels  13.8 us (52%)
  starting transfers between devices  11.4 us (43%)
  between operations  0.71 us (3%)
  waiting for transfers between devices  0.45 us (2%)
    pallas_call x1, Pallas kernels, faces_call(): pl.pallas_call(functools.partial(faces_kernel, energy.shape, cuts), in_sp...  4.79 us
    ppermute x3, starting transfers between devices, shards(): msgs = [lax.ppermute(send, 'gz', xor_pairs(nz, m)) for m in swap_order(nz)]  4.49 us
    ppermute x2, starting transfers between devices, shards(): lax.ppermute(y_sends[k], 'gy', swap_pairs(gy, k) + (ends if k else []))  3.37 us
    pallas_call x1, Pallas kernels, local_call(): pl.pallas_call(functools.partial(local_kernel, (cases, nx, ny, depth), 16...  2.25 us
    pallas_call x1, Pallas kernels, rest_call(): pl.pallas_call(functools.partial(rest_kernel, t.shape, chunk), in_specs=[...  2.13 us
    pallas_call x1, Pallas kernels, body_call(): pl.pallas_call(functools.partial(body_kernel, part.shape, chunk), in_spec...  2.1 us
    ppermute x1, starting transfers between devices, shards(): lax.ppermute(x_sends[k], 'gx', swap_pairs(gx, k))  1.84 us
    ppermute x1, starting transfers between devices, shards(): lax.ppermute(v, 'gx', swap_pairs(gx, k))  1.27 us
  transfers between devices with their start and end apart: 8, of which 2 were waited for; matrix products, arithmetic and copies ran while one was open for 0% of the time, Pallas kernels for 30%

profile of v9, /device:TPU:1, one launch (start us, length us, event | category | flops | bytes accessed | tf_op | source)
XLA Modules:
  0.0 26.3 jit_solution(6894797851383282594)
XLA Ops:
  0.6 4.8 %faces.1 = (bf16[8,4224]{1,0:T(8,128)(2,1)S(1)}, f32[8,4224]{1,0:T(8,128)S(1)}, bf16[4096,512]{1,0:T(8,128)(2,1)S(1)}, f32[64,64,128]{2,1,0:T(8,128)S(1)}, s32[6...) custom-call(s32[4]{0:T(128)} %refs_0_.1, f32[16]{0:T(128)} %refs_1_.1, f32[4,128]{1,0:T(4,128)} %refs_2_.1, ...), custom_call_target="tpu_custom_call" | custom-call | tf_op jit(solution)/shard_map/faces/pallas_call | solution.py:193
  5.4 3.2 %collective-permute-start = (bf16[8,4224]{1,0:T(8,128)(2,1)S(1)}, bf16[8,4224]{1,0:T(8,128)(2,1)S(1)}, u32[]{:S(2)}, u32[]{:S(2)}) collective-permute-start(bf16[8,4224]{1,0:T(8,128)(2,1)S(1)} %get-tuple-element.32), channel_id=1, source_target_pairs={{0,16},{8,24},{16,0},{24,8},{1,17},{9,25},{17,1},{25,9},{2,18},{10... | collective-permute-start | bytes 202760 | tf_op jit(solution)/shard_map/ppermute | solution.py:625
  8.6 1.1 %collective-permute-start.1 = (bf16[8,4224]{1,0:T(8,128)(2,1)S(1)}, bf16[8,4224]{1,0:T(8,128)(2,1)S(1)}, u32[]{:S(2)}, u32[]{:S(2)}) collective-permute-start(bf16[8,4224]{1,0:T(8,128)(2,1)S(1)} %get-tuple-element.32), channel_id=1, source_target_pairs={{0,24},{8,16},{16,8},{24,0},{1,25},{9,17},{17,9},{25,1},{2,26},{10... | collective-permute-start | bytes 202760 | tf_op jit(solution)/shard_map/ppermute | solution.py:625
  9.7 0.2 collective-permute-start.2
  9.9 2.2 %local.1 = (f32[64,64,128]{2,1,0:T(8,128)S(1)}, f32[64,64,128]{2,1,0:T(8,128)S(1)}, bf16[32,128]{1,0:T(8,128)(2,1)S(1)}, bf16[192,128]{1,0:T(8,128)(2,1)S(1)}) custom-call(bf16[4096,512]{1,0:T(8,128)(2,1)S(1)} %get-tuple-element.34.source_ref, f32[64,64,128]{2,1,0:T(8,128)S(1)} %get-tuple-element.35.density_ref, ...), custom_call_target="tpu_custom_call" | custom-call | tf_op jit(solution)/shard_map/local/pallas_call | solution.py:260
  12.2 1.3 %collective-permute-start.3 = (bf16[192,128]{1,0:T(8,128)(2,1)S(1)}, bf16[192,128]{1,0:T(8,128)(2,1)S(1)}, u32[]{:S(2)}, u32[]{:S(2)}) collective-permute-start(bf16[192,128]{1,0:T(8,128)(2,1)S(1)} %get-tuple-element.43), channel_id=1, source_target_pairs={{0,4},{4,0},{1,5},{5,1},{2,6},{6,2},{3,7},{7,3},{8,12},{12,8},{9,1... | collective-permute-start | bytes 147464 | tf_op jit(solution)/shard_map/ppermute | solution.py:630
  13.4 0.0 collective-permute-done.refs_1_
  13.4 0.2 collective-permute-done.1.refs_2_
  13.7 0.0 collective-permute-done.2.refs_3_
  13.7 0.3 %head.1 = (bf16[32,4096]{1,0:T(8,128)(2,1)S(1)}, bf16[32,256]{1,0:T(8,128)(2,1)S(1)}) custom-call(f32[8,4224]{1,0:T(8,128)S(1)} %get-tuple-element.31.refs_0_, bf16[8,4224]{1,0:T(8,128)(2,1)S(1)} %collective-permute-done.refs_1_, bf16[8,4224]{1,0:T(8,128)(2,1)S(1)} %collective-permute-done.1.refs_2_, bf16[8,4224]{1,0:T(8,128)(2,1)S(1)} %collective-permute-done.2.refs_3_), custom_call_target="tpu_custom_call" | custom-call | tf_op jit(solution)/shard_map/head/pallas_call | solution.py:324
  14.0 1.8 %collective-permute-start.4 = (bf16[32,256]{1,0:T(8,128)(2,1)S(1)}, bf16[32,256]{1,0:T(8,128)(2,1)S(1)}, u32[]{:S(2)}, u32[]{:S(2)}) collective-permute-start(bf16[32,256]{1,0:T(8,128)(2,1)S(1)} %get-tuple-element.44.refs_4_), channel_id=1, source_target_pairs={{0,4},{4,0},{1,5},{5,1},{2,6},{6,2},{3,7},{7,3},{8,12},{12,8},{9,1... | collective-permute-start | bytes 49160 | tf_op jit(solution)/shard_map/ppermute | solution.py:632
  15.9 2.1 %body.1 = (f32[64,64,128]{2,1,0:T(8,128)S(1)}, f32[64,64,128]{2,1,0:T(8,128)}, f32[64,8,128]{2,1,0:T(8,128)S(1)}, f32[64,8,128]{2,1,0:T(8,128)S(1)}) custom-call(bf16[32,4096]{1,0:T(8,128)(2,1)S(1)} %get-tuple-element.33.lhs_ref, bf16[32,128]{1,0:T(8,128)(2,1)S(1)} %get-tuple-element.39.umap_ref.refs_1_, f32[64,64,128]{2,1,0:T(8,128)S(1)} %get-tuple-element.40.part_ref, ...), custom_call_target="tpu_custom_call" | custom-call | tf_op jit(solution)/shard_map/body/pallas_call | solution.py:460
  18.0 0.0 collective-permute-done.3.refs_2_
  18.0 0.0 collective-permute-done.4.refs_3_
  18.0 0.4 %edge.1 = (bf16[208,128]{1,0:T(8,128)(2,1)S(1)}, bf16[208,128]{1,0:T(8,128)(2,1)S(1)}, f32[192,128]{1,0:T(8,128)S(1)}, f32[192,128]{1,0:T(8,128)S(1)}, f32[8,128]{1,0:T(8,128)S(1)}) custom-call(f32[64,64,128]{2,1,0:T(8,128)S(1)} %get-tuple-element.42.refs_0_.t_ref, bf16[32,128]{1,0:T(8,128)(2,1)S(1)} %get-tuple-element.39.umap_ref.refs_1_, ...), custom_call_target="tpu_custom_call" | custom-call | tf_op jit(solution)/shard_map/edge/pallas_call | solution.py:390
  18.4 3.4 %collective-permute-start.6 = (bf16[208,128]{1,0:T(8,128)(2,1)S(1)}, bf16[208,128]{1,0:T(8,128)(2,1)S(1)}, u32[]{:S(2)}, u32[]{:S(2)}) collective-permute-start(bf16[208,128]{1,0:T(8,128)(2,1)S(1)} %get-tuple-element.46), channel_id=1, source_target_pairs={{1,2},{2,1},{0,3},{3,0},{5,6},{6,5},{4,7},{7,4},{9,10},{10,9},{8,1... | collective-permute-start | bytes 159752 | tf_op jit(solution)/shard_map/ppermute | solution.py:639
  21.8 0.0 collective-permute-start.5
  21.8 2.1 %rest.1 = (f32[64,64,128]{2,1,0:T(8,128)}, f32[64,8,128]{2,1,0:T(8,128)S(1)}, f32[64,8,128]{2,1,0:T(8,128)S(1)}) custom-call(f32[64,64,128]{2,1,0:T(8,128)S(1)} %get-tuple-element.42.refs_0_.t_ref, f32[192,128]{1,0:T(8,128)S(1)} %get-tuple-element.47.xb_ref, ...), custom_call_target="tpu_custom_call", output_to_operand_aliasing={{0}: (4, {}), {1}: (5, {}), {2}: (6, {})} | custom-call | tf_op jit(solution)/shard_map/rest/pallas_call | solution.py:509
  24.0 0.2 collective-permute-done.6.refs_1_.refs_3_
  24.2 0.4 %collective-permute-start.7 = (bf16[208,128]{1,0:T(8,128)(2,1)S(1)}, bf16[208,128]{1,0:T(8,128)(2,1)S(1)}, u32[]{:S(2)}, u32[]{:S(2)}) collective-permute-start(bf16[208,128]{1,0:T(8,128)(2,1)S(1)} %collective-permute-done.6.refs_1_.refs_3_), channel_id=1, source_target_pairs={{0,1},{1,0},{2,3},{3,2},{4,5},{5,4},{6,7},{7,6},{8,9},{9,8},{10,11... | collective-permute-start | bytes 159752 | tf_op jit(solution)/shard_map/ppermute | solution.py:643
  24.6 0.0 collective-permute-done.5.refs_0_.refs_2_
  24.6 1.0 %finish.1 = (f32[64,64,128]{2,1,0:T(8,128)}, f32[8,128]{1,0:T(8,128)S(1)}) custom-call(bf16[208,128]{1,0:T(8,128)(2,1)S(1)} %collective-permute-done.5.refs_0_.refs_2_, bf16[208,128]{1,0:T(8,128)(2,1)S(1)} %collective-permute-done.6.refs_1_.refs_3_, f32[64,8,128]{2,1,0:T(8,128)S(1)} %get-tuple-element.54.refs_2_, ...), custom_call_target="tpu_custom_call", output_to_operand_aliasing={{0}: (5, {})} | custom-call | tf_op jit(solution)/shard_map/finish/pallas_call | solution.py:569
  25.6 0.0 collective-permute-done.7.refs_4_
  25.6 0.7 %mean.1 = f32[4]{0:T(128)} custom-call(f32[8,128]{1,0:T(8,128)S(1)} %get-tuple-element.58.refs_0_, f32[8,128]{1,0:T(8,128)S(1)} %get-tuple-element.59.refs_1_, bf16[208,128]{1,0:T(8,128)(2,1)S(1)} %collective-permute-done.5.refs_0_.refs_2_, bf16[208,128]{1,0:T(8,128)(2,1)S(1)} %collective-permute-done.6.refs_1_.refs_3_, ...), custom_call_target="tpu_custom_call" | custom-call | tf_op jit(solution)/shard_map/mean/pallas_call | solution.py:591
Async XLA Ops:
  5.4 8.0 %collective-permute-start = (bf16[8,4224]{1,0:T(8,128)(2,1)S(1)}, bf16[8,4224]{1,0:T(8,128)(2,1)S(1)}, u32[]{:S(2)}, u32[]{:S(2)}) collective-permute-start(bf16[8,4224]{1,0:T(8,128)(2,1)S(1)} %get-tuple-element.32), channel_id=1, source_target_pairs={{0,16},{8,24},{16,0},{24,8},{1,17},{9,25},{17,1},{25,9},{2,18},{10... | collective-permute-start | bytes 202760 | tf_op jit(solution)/shard_map/ppermute | solution.py:625
  8.6 5.0 %collective-permute-start.1 = (bf16[8,4224]{1,0:T(8,128)(2,1)S(1)}, bf16[8,4224]{1,0:T(8,128)(2,1)S(1)}, u32[]{:S(2)}, u32[]{:S(2)}) collective-permute-start(bf16[8,4224]{1,0:T(8,128)(2,1)S(1)} %get-tuple-element.32), channel_id=1, source_target_pairs={{0,24},{8,16},{16,8},{24,0},{1,25},{9,17},{17,9},{25,1},{2,26},{10... | collective-permute-start | bytes 202760 | tf_op jit(solution)/shard_map/ppermute | solution.py:625
  9.7 4.0 %collective-permute-start.2 = (bf16[8,4224]{1,0:T(8,128)(2,1)S(1)}, bf16[8,4224]{1,0:T(8,128)(2,1)S(1)}, u32[]{:S(2)}, u32[]{:S(2)}) collective-permute-start(bf16[8,4224]{1,0:T(8,128)(2,1)S(1)} %get-tuple-element.32), channel_id=1, source_target_pairs={{0,8},{8,0},{16,24},{24,16},{1,9},{9,1},{17,25},{25,17},{2,10},{10... | collective-permute-start | bytes 202760 | tf_op jit(solution)/shard_map/ppermute | solution.py:625
  12.2 5.8 %collective-permute-start.3 = (bf16[192,128]{1,0:T(8,128)(2,1)S(1)}, bf16[192,128]{1,0:T(8,128)(2,1)S(1)}, u32[]{:S(2)}, u32[]{:S(2)}) collective-permute-start(bf16[192,128]{1,0:T(8,128)(2,1)S(1)} %get-tuple-element.43), channel_id=1, source_target_pairs={{0,4},{4,0},{1,5},{5,1},{2,6},{6,2},{3,7},{7,3},{8,12},{12,8},{9,1... | collective-permute-start | bytes 147464 | tf_op jit(solution)/shard_map/ppermute | solution.py:630
  14.0 4.0 %collective-permute-start.4 = (bf16[32,256]{1,0:T(8,128)(2,1)S(1)}, bf16[32,256]{1,0:T(8,128)(2,1)S(1)}, u32[]{:S(2)}, u32[]{:S(2)}) collective-permute-start(bf16[32,256]{1,0:T(8,128)(2,1)S(1)} %get-tuple-element.44.refs_4_), channel_id=1, source_target_pairs={{0,4},{4,0},{1,5},{5,1},{2,6},{6,2},{3,7},{7,3},{8,12},{12,8},{9,1... | collective-permute-start | bytes 49160 | tf_op jit(solution)/shard_map/ppermute | solution.py:632
  18.4 5.7 %collective-permute-start.6 = (bf16[208,128]{1,0:T(8,128)(2,1)S(1)}, bf16[208,128]{1,0:T(8,128)(2,1)S(1)}, u32[]{:S(2)}, u32[]{:S(2)}) collective-permute-start(bf16[208,128]{1,0:T(8,128)(2,1)S(1)} %get-tuple-element.46), channel_id=1, source_target_pairs={{1,2},{2,1},{0,3},{3,0},{5,6},{6,5},{4,7},{7,4},{9,10},{10,9},{8,1... | collective-permute-start | bytes 159752 | tf_op jit(solution)/shard_map/ppermute | solution.py:639
  21.8 2.8 %collective-permute-start.5 = (bf16[208,128]{1,0:T(8,128)(2,1)S(1)}, bf16[208,128]{1,0:T(8,128)(2,1)S(1)}, u32[]{:S(2)}, u32[]{:S(2)}) collective-permute-start(bf16[208,128]{1,0:T(8,128)(2,1)S(1)} %get-tuple-element.45), channel_id=1, source_target_pairs={{0,1},{1,0},{2,3},{3,2},{4,5},{5,4},{6,7},{7,6},{8,9},{9,8},{10,11... | collective-permute-start | bytes 159752 | tf_op jit(solution)/shard_map/ppermute | solution.py:639
  24.2 1.4 %collective-permute-start.7 = (bf16[208,128]{1,0:T(8,128)(2,1)S(1)}, bf16[208,128]{1,0:T(8,128)(2,1)S(1)}, u32[]{:S(2)}, u32[]{:S(2)}) collective-permute-start(bf16[208,128]{1,0:T(8,128)(2,1)S(1)} %collective-permute-done.6.refs_1_.refs_3_), channel_id=1, source_target_pairs={{0,1},{1,0},{2,3},{3,2},{4,5},{5,4},{6,7},{7,6},{8,9},{9,8},{10,11... | collective-permute-start | bytes 159752 | tf_op jit(solution)/shard_map/ppermute | solution.py:643
